TPU v7x, 256 devices: a whole 4x4x8 slice. The times are simulated.
256 devices in a mesh: row: 8 (over x, core), col: 32 (over y, z).
Axes of the slice: x: 4, y: 4, z: 8, core: 2. Of those that a mesh axis runs over, the one named last changes fastest.
Arguments:
- connectivity: int32 [4, 2097152], P(None, ('row', 'col')), may hold values from 0 to 3071
- gradients: float32 [9, 2097152], P(None, ('row', 'col')), may hold values from -4 to 4
- volumes: float32 [2097152], P(('row', 'col')), may hold values from 0.2 to 1
- live_blocks: int32 [256], P(('row', 'col')), may hold values from 1 to 8, as said below
- send_lists: int32 [4, 65536], P(None, ('row', 'col')), may hold values from 0 to 2047
- divergence: float32 [524288], P(('row', 'col')), may hold values from -6 to 6
- mass_shift: float32 [524288], P(('row', 'col')), may hold values from 0.5 to 4
- boundary_nodes: int32 [81920], P(('row', 'col')), may hold values from 0 to 2047
- surface_points: float32 [3, 81920], P(None, ('row', 'col')), may hold values from 0 to 1
- normal_cos: float32 [81920], P(('row', 'col')), may hold values from -1 to 1
- normal_angle: float32 [81920], P(('row', 'col')), may hold values from -3.140625 to 3.140625
- node_areas: float32 [81920], P(('row', 'col')), may hold values from 0.00036621094 to 0.0014648438
Outputs:
- potential: float32 [524288], P(('row', 'col'))
- dirichlet: float32 [8192], P(('row', 'col'))
Inputs may be any that keep to these rules, and one draw needn't show every extreme that they name: The first live_blocks[p] element blocks of partition p are live, the rest are padding; some partition has all 8 blocks live. `connectivity`: indices into the partition's extended node list. `send_lists`: indices of the partition's own nodes. `boundary_nodes`: indices of the partition's own nodes.
All inputs are finite; a program needn't handle non-finite values.
Results may differ from a plain program's by a relative error of at most 0.0024.
Values sent between devices are 32-bit elements; how exact they have to be, the bound alone decides.
No kernel may reach another device: no remote copies, remote signals or barrier semaphores. Data moves between devices by JAX's collectives and lax.ppermute only.
A program may use at most 64 MiB of HBM per device.

v0:
```python
import math

import jax
import jax.numpy as jnp
from jax import lax
from jax.sharding import PartitionSpec as P

TGT_DEV = 32
NBLK = 8
ITERS = 3


smoothing = 0.0001
inverse_four_pi = 1.0 / (4.0 * math.pi)


def with_halo(block, sides, width):
    for axis, dim in sides:
        count = lax.axis_size(axis)
        forward = [(i, i + 1) for i in range(count - 1)]
        backward = [(target, source) for source, target in forward]
        low = lax.ppermute(
            lax.slice_in_dim(block, block.shape[dim] - width, None, axis=dim), axis, forward
        )
        high = lax.ppermute(lax.slice_in_dim(block, 0, width, axis=dim), axis, backward)
        block = jnp.concatenate([low, block, high], axis=dim)
    return block


def pick_block(total, largest):
    for candidate in range(min(total, largest), 0, -1):
        if total % candidate == 0:
            return candidate
    return 1


def element_terms(extended, corners, gradients, volumes):
    corner_values = extended[corners]
    grad_zero = gradients[0:3]
    grad_one = gradients[3:6]
    grad_two = gradients[6:9]
    grad_three = -(grad_zero + grad_one + grad_two)
    field_grad = (
        grad_zero * corner_values[0]
        + grad_one * corner_values[1]
        + grad_two * corner_values[2]
        + grad_three * corner_values[3]
    )
    return (
        jnp.stack(
            [
                jnp.sum(gradient * field_grad, axis=0)
                for gradient in (grad_zero, grad_one, grad_two, grad_three)
            ]
        )
        * volumes
    )


def kernel_rows(targets, sources):
    delta_x = targets[0][:, None] - sources[0][None, :]
    delta_y = targets[1][:, None] - sources[1][None, :]
    delta_z = targets[2][:, None] - sources[2][None, :]
    radius_sq = delta_x * delta_x + delta_y * delta_y + delta_z * delta_z + smoothing
    inverse = lax.rsqrt(radius_sq)
    numerator = (
        delta_x * sources[3][None, :]
        + delta_y * sources[4][None, :]
        + delta_z * sources[5][None, :]
    )
    entries = (numerator * (inverse * inverse * inverse) * inverse_four_pi).astype(jnp.bfloat16)
    return jnp.dot(entries, sources[6].astype(jnp.bfloat16), preferred_element_type=jnp.float32)


def fetch_ghosts(values, send_lists):
    picked = values[send_lists]
    empty = jnp.zeros_like(picked[0])
    layout = jnp.stack(
        [
            jnp.stack([empty, picked[1], empty]),
            jnp.stack([picked[3], empty, picked[2]]),
            jnp.stack([empty, picked[0], empty]),
        ]
    )
    extended = with_halo(layout, (("row", 0), ("col", 1)), 1)
    return jnp.concatenate([extended[0, 2], extended[4, 2], extended[2, 0], extended[2, 4]])


def return_ghosts(ghost_terms):
    empty = jnp.zeros_like(ghost_terms[0])
    layout = jnp.stack(
        [
            jnp.stack([empty, ghost_terms[0], empty]),
            jnp.stack([ghost_terms[2], empty, ghost_terms[3]]),
            jnp.stack([empty, ghost_terms[1], empty]),
        ]
    )
    extended = with_halo(layout, (("row", 0), ("col", 1)), 1)
    return jnp.stack([extended[4, 2], extended[0, 2], extended[2, 4], extended[2, 0]])


def apply_operator(values, connectivity, gradients, volumes, live_blocks, send_lists, mass_shift):
    nodes = values.shape[0]
    extended = jnp.concatenate([values, fetch_ghosts(values, send_lists)])
    block_size = connectivity.shape[1] // NBLK

    def add_block(block_index, total):
        start = block_index * block_size
        corners = lax.dynamic_slice_in_dim(connectivity, start, block_size, 1)
        block_grads = lax.dynamic_slice_in_dim(gradients, start, block_size, 1)
        block_volumes = lax.dynamic_slice_in_dim(volumes, start, block_size, 0)
        return total.at[corners].add(element_terms(extended, corners, block_grads, block_volumes))

    assembled = lax.fori_loop(0, live_blocks[0], add_block, jnp.zeros(extended.shape, jnp.float32))
    owned = assembled[:nodes]
    ghost_terms = assembled[nodes:].reshape(4, -1)
    owned = owned.at[send_lists].add(return_ghosts(ghost_terms))
    return mass_shift * values + owned


def squares(residual):
    return lax.psum(jnp.sum(residual * residual), ("row", "col"))


def per_device(
    connectivity,
    gradients,
    volumes,
    live_blocks,
    send_lists,
    divergence,
    mass_shift,
    boundary_nodes,
    surface_points,
    normal_cos,
    normal_angle,
    node_areas,
):
    potential = jnp.zeros_like(divergence)
    residual = divergence
    direction = divergence
    norm_now = squares(residual)
    for iteration in range(ITERS):
        image = apply_operator(
            direction, connectivity, gradients, volumes, live_blocks, send_lists, mass_shift
        )
        alpha = norm_now / lax.psum(jnp.sum(direction * image), ("row", "col"))
        potential = potential + alpha * direction
        residual = residual - alpha * image
        norm_next = squares(residual)
        direction = residual + norm_next / norm_now * direction
        norm_now = norm_next
    traces = potential[boundary_nodes]
    trace_bf = traces.astype(jnp.bfloat16)
    sine = jnp.sqrt(1.0 - normal_cos * normal_cos)
    normals = jnp.stack([sine * jnp.cos(normal_angle), sine * jnp.sin(normal_angle), normal_cos])
    weighted = node_areas[None, :] * normals
    sources = jnp.concatenate(
        [surface_points, weighted, trace_bf.astype(jnp.float32)[None, :]], axis=0
    )
    target_points = surface_points[:, :TGT_DEV]
    target_traces = traces[:TGT_DEV]
    piece = lax.all_gather(sources, ("row", "col"), axis=1, tiled=True)
    width = piece.shape[1]
    step = pick_block(width, 4096)

    def add_part(part_index, running):
        columns = lax.dynamic_slice_in_dim(piece, part_index * step, step, 1)
        return running + kernel_rows(target_points, columns)

    far_field = lax.fori_loop(0, width // step, add_part, jnp.zeros((TGT_DEV,), jnp.float32))
    dirichlet = far_field - 0.5 * target_traces
    return (potential, dirichlet)


def solution(mesh):
    return jax.shard_map(
        per_device,
        mesh=mesh,
        in_specs=(
            P(None, ("row", "col")),
            P(None, ("row", "col")),
            P(("row", "col")),
            P(("row", "col")),
            P(None, ("row", "col")),
            P(("row", "col")),
            P(("row", "col")),
            P(("row", "col")),
            P(None, ("row", "col")),
            P(("row", "col")),
            P(("row", "col")),
            P(("row", "col")),
        ),
        out_specs=(P(("row", "col")), P(("row", "col"))),
        check_vma=False,
    )
```

profile of v0, /device:TPU:1, one launch (start us, length us, event | category | flops | bytes accessed | tf_op | source)
XLA Modules:
  0.0 1839.5 jit_solution(16345966479136023931)
XLA Ops:
  31.8 336.5 %while.44 = (s32[]{:T(128)}, f32[3072]{0:T(1024)S(1)}, s32[]{:T(128)}, s32[4,8192]{1,0:T(4,128)S(1)}, f32[9,8192]{1,0:T(8,128)}, /*index=5*/f32[3072]{0:T(1024)S...) while((s32[]{:T(128)}, f32[3072]{0:T(1024)S(1)}, s32[]{:T(128)}, ...), condition=%wide.region_8.0_spmd, body=%wide.region_2.0_spmd.sunk | while | flops 88072 | bytes 393431 | solution.py:114
  32.5 23.0 %gather_fusion = f32[4096]{0:T(1024)S(1)} fusion(f32[3072]{0:T(1024)S(1)} %get-tuple-element.611, s32[4096]{0:T(1024)S(1)} %broadcast_clamp_fusion.7), kind=kCustom, calls=%fused_computation.clone.1 | custom fusion | bytes 49152 | tf_op jit(solution)/shard_map/while/body/gather | solution.py:38
  80.5 23.0 %gather_fusion = f32[4096]{0:T(1024)S(1)} fusion(f32[3072]{0:T(1024)S(1)} %get-tuple-element.611, s32[4096]{0:T(1024)S(1)} %broadcast_clamp_fusion.7), kind=kCustom, calls=%fused_computation.clone.1 | custom fusion | bytes 49152 | tf_op jit(solution)/shard_map/while/body/gather | solution.py:38
  128.4 23.0 %gather_fusion = f32[4096]{0:T(1024)S(1)} fusion(f32[3072]{0:T(1024)S(1)} %get-tuple-element.611, s32[4096]{0:T(1024)S(1)} %broadcast_clamp_fusion.7), kind=kCustom, calls=%fused_computation.clone.1 | custom fusion | bytes 49152 | tf_op jit(solution)/shard_map/while/body/gather | solution.py:38
  176.4 23.0 %gather_fusion = f32[4096]{0:T(1024)S(1)} fusion(f32[3072]{0:T(1024)S(1)} %get-tuple-element.611, s32[4096]{0:T(1024)S(1)} %broadcast_clamp_fusion.7), kind=kCustom, calls=%fused_computation.clone.1 | custom fusion | bytes 49152 | tf_op jit(solution)/shard_map/while/body/gather | solution.py:38
  224.4 23.0 %gather_fusion = f32[4096]{0:T(1024)S(1)} fusion(f32[3072]{0:T(1024)S(1)} %get-tuple-element.611, s32[4096]{0:T(1024)S(1)} %broadcast_clamp_fusion.7), kind=kCustom, calls=%fused_computation.clone.1 | custom fusion | bytes 49152 | tf_op jit(solution)/shard_map/while/body/gather | solution.py:38
  320.4 23.0 %gather_fusion = f32[4096]{0:T(1024)S(1)} fusion(f32[3072]{0:T(1024)S(1)} %get-tuple-element.611, s32[4096]{0:T(1024)S(1)} %broadcast_clamp_fusion.7), kind=kCustom, calls=%fused_computation.clone.1 | custom fusion | bytes 49152 | tf_op jit(solution)/shard_map/while/body/gather | solution.py:38
  387.6 125.2 %all-reduce = (f32[]{:T(128)}, f32[]{:T(128)}) all-reduce(f32[]{:T(128)} %get-tuple-element.227, f32[]{:T(128)} %get-tuple-element.226), channel_id=1, replica_groups=mesh['row'=8,'col'=32] {'row','col'}, use_global_device_ids=true, to_apply=%region_1.0 | all-reduce | flops 2 | bytes 16 | tf_op jit(solution)/shard_map/psum | solution.py:122
  514.8 73.0 %psum.44 = f32[]{:T(128)} all-reduce(f32[]{:T(128)} %get-tuple-element.284), channel_id=1, replica_groups=mesh['row'=8,'col'=32] {'row','col'}, use_global_device_ids=true, to_apply=%region_13.0 | all-reduce | flops 1 | bytes 8 | tf_op jit(solution)/shard_map/psum | solution.py:122
  610.5 336.5 %while.45 = (s32[]{:T(128)}, f32[3072]{0:T(1024)S(1)}, s32[]{:T(128)}, s32[4,8192]{1,0:T(4,128)S(1)}, f32[9,8192]{1,0:T(8,128)}, /*index=5*/f32[3072]{0:T(1024)S...) while((s32[]{:T(128)}, f32[3072]{0:T(1024)S(1)}, s32[]{:T(128)}, ...), condition=%wide.region_20.0_spmd, body=%wide.region_14.0_spmd.sunk | while | flops 88072 | bytes 393431 | solution.py:114
  611.2 23.0 %gather_fusion.1 = f32[4096]{0:T(1024)S(1)} fusion(f32[3072]{0:T(1024)S(1)} %get-tuple-element.650, s32[4096]{0:T(1024)S(1)} %broadcast_clamp_fusion.8), kind=kCustom, calls=%fused_computation.1.clone.1 | custom fusion | bytes 49152 | tf_op jit(solution)/shard_map/while/body/gather | solution.py:38
  659.2 23.0 %gather_fusion.1 = f32[4096]{0:T(1024)S(1)} fusion(f32[3072]{0:T(1024)S(1)} %get-tuple-element.650, s32[4096]{0:T(1024)S(1)} %broadcast_clamp_fusion.8), kind=kCustom, calls=%fused_computation.1.clone.1 | custom fusion | bytes 49152 | tf_op jit(solution)/shard_map/while/body/gather | solution.py:38
  803.1 23.0 %gather_fusion.1 = f32[4096]{0:T(1024)S(1)} fusion(f32[3072]{0:T(1024)S(1)} %get-tuple-element.650, s32[4096]{0:T(1024)S(1)} %broadcast_clamp_fusion.8), kind=kCustom, calls=%fused_computation.1.clone.1 | custom fusion | bytes 49152 | tf_op jit(solution)/shard_map/while/body/gather | solution.py:38
  851.1 23.0 %gather_fusion.1 = f32[4096]{0:T(1024)S(1)} fusion(f32[3072]{0:T(1024)S(1)} %get-tuple-element.650, s32[4096]{0:T(1024)S(1)} %broadcast_clamp_fusion.8), kind=kCustom, calls=%fused_computation.1.clone.1 | custom fusion | bytes 49152 | tf_op jit(solution)/shard_map/while/body/gather | solution.py:38
  966.3 119.9 %psum.45 = f32[]{:T(128)} all-reduce(f32[]{:T(128)} %multiply_reduce_fusion.14), channel_id=1, replica_groups=mesh['row'=8,'col'=32] {'row','col'}, use_global_device_ids=true, to_apply=%region_23.0 | all-reduce | flops 1 | bytes 8 | tf_op jit(solution)/shard_map/psum | solution.py:147
  1088.2 73.2 %psum.46 = f32[]{:T(128)} all-reduce(f32[]{:T(128)} %multiply_reduce_fusion.13), channel_id=1, replica_groups=mesh['row'=8,'col'=32] {'row','col'}, use_global_device_ids=true, to_apply=%region_25.0 | all-reduce | flops 1 | bytes 8 | tf_op jit(solution)/shard_map/psum | solution.py:122
  1184.1 336.5 %while.46 = (s32[]{:T(128)}, f32[3072]{0:T(1024)S(1)}, s32[]{:T(128)}, s32[4,8192]{1,0:T(4,128)S(1)}, f32[9,8192]{1,0:T(8,128)}, /*index=5*/f32[3072]{0:T(1024)S...) while((s32[]{:T(128)}, f32[3072]{0:T(1024)S(1)}, s32[]{:T(128)}, ...), condition=%wide.region_32.0_spmd, body=%wide.region_26.0_spmd.sunk | while | flops 88072 | bytes 393431 | solution.py:114
  1184.8 23.0 %gather_fusion.2 = f32[4096]{0:T(1024)S(1)} fusion(f32[3072]{0:T(1024)S(1)} %get-tuple-element.689, s32[4096]{0:T(1024)S(1)} %broadcast_clamp_fusion.9), kind=kCustom, calls=%fused_computation.2.clone.1 | custom fusion | bytes 49152 | tf_op jit(solution)/shard_map/while/body/gather | solution.py:38
  1232.8 23.0 %gather_fusion.2 = f32[4096]{0:T(1024)S(1)} fusion(f32[3072]{0:T(1024)S(1)} %get-tuple-element.689, s32[4096]{0:T(1024)S(1)} %broadcast_clamp_fusion.9), kind=kCustom, calls=%fused_computation.2.clone.1 | custom fusion | bytes 49152 | tf_op jit(solution)/shard_map/while/body/gather | solution.py:38
  1280.8 23.0 %gather_fusion.2 = f32[4096]{0:T(1024)S(1)} fusion(f32[3072]{0:T(1024)S(1)} %get-tuple-element.689, s32[4096]{0:T(1024)S(1)} %broadcast_clamp_fusion.9), kind=kCustom, calls=%fused_computation.2.clone.1 | custom fusion | bytes 49152 | tf_op jit(solution)/shard_map/while/body/gather | solution.py:38
  1328.7 23.0 %gather_fusion.2 = f32[4096]{0:T(1024)S(1)} fusion(f32[3072]{0:T(1024)S(1)} %get-tuple-element.689, s32[4096]{0:T(1024)S(1)} %broadcast_clamp_fusion.9), kind=kCustom, calls=%fused_computation.2.clone.1 | custom fusion | bytes 49152 | tf_op jit(solution)/shard_map/while/body/gather | solution.py:38
  1539.9 119.9 %psum.47 = f32[]{:T(128)} all-reduce(f32[]{:T(128)} %multiply_reduce_fusion.12), channel_id=1, replica_groups=mesh['row'=8,'col'=32] {'row','col'}, use_global_device_ids=true, to_apply=%region_35.0 | all-reduce | flops 1 | bytes 8 | tf_op jit(solution)/shard_map/psum | solution.py:147
  1664.1 101.4 %all-gather.3.cloned.1.call-done = f32[256,320,7]{1,2,0:T(8,128)} async-done(((f32[1,320,7]{1,2,0:T(8,128)}), f32[256,320,7]{1,2,0:T(8,128)}) %all-gather.3.cloned.1.call-update) | async-done | bytes 2293776 | tf_op jit(solution)/shard_map/all_gather | solution.py:163
  1770.8 61.3 %while.47 = (s32[]{:T(128)}, f32[32]{0:T(128)S(1)}, f32[3,32]{1,0:T(4,128)S(1)}, f32[7,81920]{1,0:T(8,128)}, s32[]{:T(128)}, /*index=5*/s32[]{:T(128)}, s32[]{:T...) while((s32[]{:T(128)}, f32[32]{0:T(128)S(1)}, f32[3,32]{1,0:T(4,128)S(1)}, ...), condition=%wide.region_37.0_spmd.clone, body=%wide.region_36.0_spmd.clone.sunk | while | flops 2752589 | bytes 312997 | solution.py:171
  (456 shorter events, 865.0 us)
Async XLA Ops:
  7.2 1758.3 %all-gather.3.cloned.1.call-start = ((), (), s32[]{:S(2)}) async-start(), calls=%async_computation | async-start | bytes 3158016 | tf_op jit(solution)/shard_map/all_gather | solution.py:163
  14.2 6.4 collective-permute-start
  18.7 4.9 collective-permute-start.1
  23.6 4.9 collective-permute-start.2
  27.2 4.6 collective-permute-start.3
  368.3 4.4 collective-permute-start.5
  370.3 4.9 collective-permute-start.4
  375.2 2.6 collective-permute-start.7
  376.5 4.4 collective-permute-start.6
  595.3 4.5 collective-permute-start.8
  597.9 4.9 collective-permute-start.9
  602.9 4.6 collective-permute-start.10
  606.1 4.4 collective-permute-start.11
  947.1 4.4 collective-permute-start.13
  949.0 4.9 collective-permute-start.12
  954.0 2.6 collective-permute-start.15
  955.3 4.4 collective-permute-start.14
  1169.0 4.5 collective-permute-start.16
  1171.5 4.9 collective-permute-start.17
  1176.4 4.6 collective-permute-start.18
  1179.7 4.4 collective-permute-start.19
  1520.7 4.4 collective-permute-start.21
  1522.6 4.9 collective-permute-start.20
  1528.8 4.4 collective-permute-start.22
  (11 other events, 1364.8 us)
Sparse Core Ops, SparseCore 0:
  1664.2 101.2 all-gather.2
where the time goes:
time: 1840 us
  local copies, waits for them, and re-layouts  557 us (30%)
  other arithmetic  517 us (28%)
  blocking collectives  511 us (28%)
  waiting for transfers between devices  136 us (7%)
  starting transfers between devices  49.9 us (3%)
  matrix products  28.8 us (2%)
  between operations  21.8 us (1%)
    gather x21, local copies, waits for them, and re-layouts, element_terms(): corner_values = extended[corners]  484 us
    scatter-add x21, other arithmetic, add_block(): total.at[corners]  470 us
    psum x3, blocking collectives, squares(): return lax.psum(jnp.sum(residual * residual), ('row', 'col'))  271 us
    psum x2, blocking collectives, per_device(): alpha = norm_now / lax.psum(jnp.sum(direction * image), ('row', 'col'))  240 us
    all_gather x1, waiting for transfers between devices, per_device(): piece = lax.all_gather(sources, ('row', 'col'), axis=1, tiled=True)  101 us
  transfers between devices with their start and end apart: 25, of which 13 were waited for; matrix products, arithmetic and copies ran while one was open for 0% of the time, Pallas kernels for 0%

commit v1 on v0

v1 whole, which is shorter than its diff:
```python
import functools
import math

import jax
import jax.numpy as jnp
from jax import lax
from jax.experimental import pallas as pl
from jax.experimental.pallas import tpu as pltpu
from jax.sharding import PartitionSpec as P

F32 = jnp.float32
BF16 = jnp.bfloat16
LANES = 128
NN_DEV = 2048
NE_DEV = 8192
EBLK = 1024
GH = 256
TGT_DEV = 32
OWN_ROWS = NN_DEV // LANES
GHOST_ROWS = 4 * GH // LANES
EXT_ROWS = OWN_ROWS + GHOST_ROWS
ELEM_ROWS = NE_DEV // LANES
SLOTS = 320
PAD_SLOTS = 384
N_DEV = 256
SPLITS = 3
SCALE = 1.0 / 64.0
smoothing = 0.0001
inverse_four_pi = 1.0 / (4.0 * math.pi)


def gather_rows(table, index):
    rows = table.shape[0]
    high = index >> 7
    low = index & 127
    out = jnp.zeros(index.shape, F32)
    for r in range(rows):
        row = jnp.broadcast_to(table[r:r + 1, :], index.shape)
        out = jnp.where(high == r, jnp.take_along_axis(row, low, axis=1), out)
    return out


def split_terms(terms):
    parts = []
    rest = terms
    for _ in range(SPLITS):
        part = rest.astype(BF16)
        parts.append(part.astype(F32))
        rest = rest - parts[-1]
    return parts


def scatter_block(index_rows, term_rows, rows):
    sub = lax.broadcasted_iota(jnp.int32, (LANES, LANES), 0)
    sub_rows = lax.broadcasted_iota(jnp.int32, (rows, LANES), 0)
    hot_blocks = []
    weight_blocks = []
    for index, terms in zip(index_rows, term_rows):
        low = jnp.broadcast_to(index & 127, (LANES, LANES))
        hot_blocks.append(jnp.where(sub == low, 1.0, 0.0).astype(BF16))
        mine = sub_rows == jnp.broadcast_to(index >> 7, (rows, LANES))
        pieces = [
            jnp.where(mine, jnp.broadcast_to(part, (rows, LANES)), 0.0)
            for part in split_terms(terms)
        ]
        weight_blocks.append(jnp.concatenate(pieces, axis=0).astype(BF16))
    hot = jnp.concatenate(hot_blocks, axis=1)
    weights = jnp.concatenate(weight_blocks, axis=1)
    total = lax.dot_general(
        weights, hot, (((1,), (1,)), ((), ())), preferred_element_type=F32
    )
    out = total[0:rows]
    for k in range(1, SPLITS):
        out = out + total[k * rows:(k + 1) * rows]
    return out


def element_gradient(ext, conn_ref, grad_ref, t):
    block = pl.ds(pl.multiple_of(t * 8, 8), 8)
    corner = [gather_rows(ext, conn_ref[a, block, :]) for a in range(4)]
    grads = [grad_ref[c, block, :] for c in range(9)]
    base = corner[3]
    diff = [corner[a] - base for a in range(3)]
    field = [
        grads[k] * diff[0] + grads[3 + k] * diff[1] + grads[6 + k] * diff[2]
        for k in range(3)
    ]
    return grads, field


def live_volume(live_ref, vol_ref, t):
    block = pl.ds(pl.multiple_of(t * 8, 8), 8)
    return jnp.where(t < live_ref[0], vol_ref[block, :], 0.0)


def extend(parity_ref, v, ghosts):
    first = parity_ref[0] == 0
    second = parity_ref[1] == 0
    row_a, row_b, col_a, col_b = ghosts
    return jnp.concatenate(
        [
            v,
            jnp.where(first, row_b, row_a),
            jnp.where(first, row_a, row_b),
            jnp.where(second, col_b, col_a),
            jnp.where(second, col_a, col_b),
        ],
        axis=0,
    )


def put_outgoing(parity_ref, blocks, out_refs):
    first = parity_ref[0] == 0
    second = parity_ref[1] == 0
    out_refs[0][...] = jnp.where(first, blocks[0], blocks[1])
    out_refs[1][...] = jnp.where(first, blocks[1], blocks[0])
    out_refs[2][...] = jnp.where(second, blocks[2], blocks[3])
    out_refs[3][...] = jnp.where(second, blocks[3], blocks[2])


def blocks_of(rows):
    return [rows[2 * d:2 * d + 2] for d in range(4)]


def pick_kernel(parity_ref, v_ref, list_ref, *out_refs):
    put_outgoing(parity_ref, blocks_of(gather_rows(v_ref[...], list_ref[...])), out_refs)


def apply_kernel(parity_ref, live_ref, v_ref, ga, gb, gc, gd, conn_ref, grad_ref, vol_ref,
                 own_ref, oa, ob, oc, od, ext_ref, term_ref, acc_ref):
    ext_ref[...] = extend(parity_ref, v_ref[...], [ga[...], gb[...], gc[...], gd[...]])

    def element_block(t, carry):
        ext = ext_ref[...]
        grads, field = element_gradient(ext, conn_ref, grad_ref, t)
        vol = live_volume(live_ref, vol_ref, t)
        block = pl.ds(pl.multiple_of(t * 8, 8), 8)
        field = [vol * f for f in field]
        last = jnp.zeros_like(vol)
        for a in range(3):
            term = grads[3 * a] * field[0] + grads[3 * a + 1] * field[1] + grads[3 * a + 2] * field[2]
            term_ref[a, block, :] = term
            last = last - term
        term_ref[3, block, :] = last
        return carry

    lax.fori_loop(0, NE_DEV // EBLK, element_block, 0)
    acc_ref[...] = jnp.zeros_like(acc_ref)

    def scatter_step(t, carry):
        block = pl.ds(pl.multiple_of(t * 8, 8), 8)
        total = acc_ref[...]
        for a in range(4):
            index = conn_ref[a, block, :]
            terms = term_ref[a, block, :]
            total = total + scatter_block(
                [index[s:s + 1] for s in range(8)], [terms[s:s + 1] for s in range(8)], EXT_ROWS
            )
        acc_ref[...] = total
        return carry

    lax.fori_loop(0, NE_DEV // EBLK, scatter_step, 0)
    own_ref[...] = acc_ref[0:OWN_ROWS, :]
    put_outgoing(parity_ref, swap_pairs(blocks_of(acc_ref[OWN_ROWS:EXT_ROWS, :])), (oa, ob, oc, od))


def swap_pairs(blocks):
    return [blocks[1], blocks[0], blocks[3], blocks[2]]


def combine_kernel(parity_ref, own_ref, ra, rb, rc, rd, list_ref, v_ref, mass_ref,
                   next_ref, oa, ob, oc, od):
    first = parity_ref[0] == 0
    second = parity_ref[1] == 0
    lists = list_ref[...]
    returned = jnp.concatenate(
        [
            jnp.where(first, ra[...], rb[...]),
            jnp.where(first, rb[...], ra[...]),
            jnp.where(second, rc[...], rd[...]),
            jnp.where(second, rd[...], rc[...]),
        ],
        axis=0,
    )
    added = scatter_block(
        [lists[s:s + 1] for s in range(8)], [returned[s:s + 1] for s in range(8)], OWN_ROWS
    )
    value = (mass_ref[...] * v_ref[...] + own_ref[...] + added) * SCALE
    next_ref[...] = value
    put_outgoing(parity_ref, blocks_of(gather_rows(value, lists)), (oa, ob, oc, od))


def far_kernel(parity_ref, live_ref, b_ref, v1_ref, v2_ref, ga, gb, gc, gd, conn_ref, grad_ref, vol_ref,
               mass_ref, node_ref, src_ref, tgt_ref,
               out_ref, trace_ref, ext_ref, tx, ty, tz, d0, d1, d2, lhs_ref):
    b = b_ref[...]
    v1 = v1_ref[...]
    v2 = v2_ref[...]
    ext_ref[...] = extend(parity_ref, v2, [ga[...], gb[...], gc[...], gd[...]])

    def energy_block(t, total):
        ext = ext_ref[...]
        _, field = element_gradient(ext, conn_ref, grad_ref, t)
        vol = live_volume(live_ref, vol_ref, t)
        return total + vol * (field[0] * field[0] + field[1] * field[1] + field[2] * field[2])

    energy = lax.fori_loop(0, NE_DEV // EBLK, energy_block, jnp.zeros((8, LANES), F32))
    pairs = [b * b, b * v1, v1 * v1, v1 * v2, v2 * v2, mass_ref[...] * v2 * v2]
    sums = [p[0:8] + p[8:16] for p in pairs]
    sums[5] = (sums[5] + energy) * SCALE
    sub = lax.broadcasted_iota(jnp.int32, (8, LANES), 0)
    lane_row = lax.broadcasted_iota(jnp.int32, (1, LANES), 1)
    moments = jnp.zeros((1, LANES), F32)
    for k in range(6):
        moments = jnp.where(lane_row == 96 + k, jnp.sum(sums[k]), moments)

    nodes = node_ref[...]
    traces = [gather_rows(table, nodes) for table in (b, v1, v2)]
    for k in range(3):
        trace_ref[k] = traces[k]
    slot = lax.broadcasted_iota(jnp.int32, (8, LANES), 0) * LANES + lax.broadcasted_iota(jnp.int32, (8, LANES), 1)
    for r in range(PAD_SLOTS // LANES):
        block = jnp.zeros((8, LANES), F32)
        for k in range(3):
            t = jnp.where(slot < SLOTS, traces[k], 0.0)[r:r + 1, :]
            high = t.astype(BF16).astype(F32)
            block = jnp.where(sub == 2 * k, high, block)
            block = jnp.where(sub == 2 * k + 1, t - high, block)
        lhs_ref[:, r * LANES:(r + 1) * LANES] = block.astype(BF16)

    lane = lax.broadcasted_iota(jnp.int32, (N_DEV // 4, LANES), 1)
    for c, ref in enumerate((tx, ty, tz)):
        out = jnp.zeros((N_DEV // 4, LANES), F32)
        for j in range(4):
            part = tgt_ref[pl.ds(j, N_DEV // 4, stride=4), :]
            shift = (32 * j - 32 * c) % LANES
            if shift:
                part = pltpu.roll(part, shift, 1)
            out = jnp.where((lane >= 32 * j) & (lane < 32 * j + 32), part, out)
        ref[...] = out

    cols = jnp.transpose(src_ref[...])

    def target_row(g, carry):
        at = pl.ds(g, 1)
        px = tx[at, :]
        py = ty[at, :]
        pz = tz[at, :]
        dx = px - cols[:, 0:1]
        dy = py - cols[:, 1:2]
        dz = pz - cols[:, 2:3]
        radius_sq = dx * dx + dy * dy + dz * dz + smoothing
        inverse = lax.rsqrt(radius_sq)
        numerator = dx * cols[:, 3:4] + dy * cols[:, 4:5] + dz * cols[:, 5:6]
        entries = (numerator * (inverse * inverse * inverse)).astype(BF16)
        res = jnp.dot(lhs_ref[...], entries, preferred_element_type=F32)
        d0[at, :] = res[0:1] + res[1:2]
        d1[at, :] = res[2:3] + res[3:4]
        d2[at, :] = res[4:5] + res[5:6]
        return carry

    lax.fori_loop(0, N_DEV // 4, target_row, 0)
    spread = jnp.broadcast_to(moments, (N_DEV // 4, LANES))
    for j in range(4):
        out = spread
        for k, ref in enumerate((d0, d1, d2)):
            part = ref[...]
            shift = (32 * k - 32 * j) % LANES
            if shift:
                part = pltpu.roll(part, shift, 1)
            out = jnp.where((lane >= 32 * k) & (lane < 32 * k + 32), part, out)
        out_ref[pl.ds(j, N_DEV // 4, stride=4), :] = out


def final_kernel(got_ref, b_ref, v1_ref, v2_ref, trace_ref, pot_ref, dir_ref):
    total = jnp.sum(got_ref[...], axis=0, keepdims=True)
    lane = lax.broadcasted_iota(jnp.int32, (1, LANES), 1)
    m = [jnp.sum(jnp.where(lane == 96 + k, total, 0.0), axis=1, keepdims=True) for k in range(6)]
    l1 = m[2] / m[1]
    l2 = m[3] / m[1]
    s11 = m[3] - l1 * m[2]
    s12 = m[4] - l1 * m[3]
    s22 = m[5] - l2 * m[3]
    y1 = m[1] - l1 * m[0]
    y2 = m[2] - l2 * m[0]
    keep1 = s11 > 4e-7 * m[3]
    safe11 = jnp.where(keep1, s11, 1.0)
    ratio = jnp.where(keep1, s12 / safe11, 0.0)
    d2 = s22 - ratio * s12
    keep2 = keep1 & (d2 > 4e-7 * m[5])
    c2 = jnp.where(keep2, (y2 - ratio * y1) / jnp.where(keep2, d2, 1.0), 0.0)
    c1 = jnp.where(keep1, (y1 - s12 * c2) / safe11, 0.0)
    c0 = (m[0] - m[2] * c1 - m[3] * c2) / m[1]
    c0 = c0 * SCALE
    c1 = c1 * SCALE
    c2 = c2 * SCALE
    pot_ref[...] = c0 * b_ref[...] + c1 * v1_ref[...] + c2 * v2_ref[...]
    out = jnp.zeros((1, LANES), F32)
    for k, c in enumerate((c0, c1, c2)):
        part = total
        if k:
            part = pltpu.roll(total, LANES - 32 * k, 1)
        out = out + c * (part - 0.5 * trace_ref[k, 0:1, :])
    dir_ref[...] = out


def call(body, out_shapes, smem, args, scratch=(), flops=1000000):
    specs = [pl.BlockSpec(memory_space=pltpu.SMEM)] * smem
    specs += [pl.BlockSpec(memory_space=pltpu.VMEM)] * (len(args) - smem)
    return pl.pallas_call(
        body,
        out_shape=[jax.ShapeDtypeStruct(s, F32) for s in out_shapes],
        in_specs=specs,
        out_specs=[pl.BlockSpec(memory_space=pltpu.VMEM)] * len(out_shapes),
        scratch_shapes=list(scratch),
    )(*args)


PIECE = (2, LANES)


def pairs(count, start):
    out = []
    for i in range(start, count - 1, 2):
        out += [(i, i + 1), (i + 1, i)]
    return out


def exchange(pieces):
    rows = lax.axis_size("row")
    cols = lax.axis_size("col")
    return [
        lax.ppermute(pieces[0], "row", pairs(rows, 0)),
        lax.ppermute(pieces[1], "row", pairs(rows, 1)),
        lax.ppermute(pieces[2], "col", pairs(cols, 0)),
        lax.ppermute(pieces[3], "col", pairs(cols, 1)),
    ]


def per_device(connectivity, gradients, volumes, live_blocks, send_lists, divergence, mass_shift,
               boundary_nodes, surface_points, normal_cos, normal_angle, node_areas):
    parity = jnp.stack([lax.axis_index("row") % 2, lax.axis_index("col") % 2]).astype(jnp.int32)
    conn = connectivity.reshape(4, ELEM_ROWS, LANES)
    grads = gradients.reshape(9, ELEM_ROWS, LANES)
    vol = volumes.reshape(ELEM_ROWS, LANES)
    lists = send_lists.reshape(4 * GH // LANES, LANES)
    b = divergence.reshape(OWN_ROWS, LANES)
    mass = mass_shift.reshape(OWN_ROWS, LANES)
    nodes = jnp.pad(boundary_nodes, (0, 8 * LANES - SLOTS)).reshape(8, LANES)

    own_targets = jnp.pad(surface_points[:, :TGT_DEV].reshape(1, 3 * TGT_DEV), ((0, 0), (0, TGT_DEV)))
    targets = lax.all_to_all(
        jnp.broadcast_to(own_targets, (N_DEV, LANES)), ("row", "col"), 0, 0, tiled=True
    )
    sine = jnp.sqrt(1.0 - normal_cos * normal_cos)
    normals = jnp.stack([sine * jnp.cos(normal_angle), sine * jnp.sin(normal_angle), normal_cos])
    weighted = (node_areas * inverse_four_pi)[None, :] * normals
    sources = jnp.pad(
        jnp.concatenate([surface_points, weighted], axis=0), ((0, 2), (0, PAD_SLOTS - SLOTS))
    )

    def apply(v, pieces):
        ghosts = exchange(pieces)
        own, *back = call(
            apply_kernel, [(OWN_ROWS, LANES)] + [PIECE] * 4, 2,
            (parity, live_blocks, v, *ghosts, conn, grads, vol),
            scratch=[
                pltpu.VMEM((EXT_ROWS, LANES), F32),
                pltpu.VMEM((4, ELEM_ROWS, LANES), F32),
                pltpu.VMEM((EXT_ROWS, LANES), F32),
            ],
        )
        returned = exchange(back)
        new, *out = call(
            combine_kernel, [(OWN_ROWS, LANES)] + [PIECE] * 4, 1,
            (parity, own, *returned, lists, v, mass),
        )
        return new, out

    first = call(pick_kernel, [PIECE] * 4, 1, (parity, b, lists))
    v1, second = apply(b, first)
    v2, third = apply(v1, second)
    ghosts = exchange(third)
    sub = (N_DEV // 4, LANES)
    partial, trace = call(
        far_kernel, [(N_DEV, LANES), (3, 8, LANES)], 2,
        (parity, live_blocks, b, v1, v2, *ghosts, conn, grads, vol, mass, nodes, sources, targets),
        scratch=[pltpu.VMEM((EXT_ROWS, LANES), F32)]
        + [pltpu.VMEM(sub, F32)] * 6
        + [pltpu.VMEM((8, PAD_SLOTS), BF16)],
    )
    got = lax.all_to_all(partial, ("row", "col"), 0, 0, tiled=True)
    potential, dirichlet = call(
        final_kernel, [(OWN_ROWS, LANES), (1, LANES)], 0, (got, b, v1, v2, trace)
    )
    return potential.reshape(NN_DEV), dirichlet[0, :TGT_DEV]


def solution(mesh):
    both = ("row", "col")
    return jax.shard_map(
        per_device,
        mesh=mesh,
        in_specs=(
            P(None, both), P(None, both), P(both), P(both), P(None, both), P(both),
            P(both), P(both), P(None, both), P(both), P(both), P(both),
        ),
        out_specs=(P(both), P(both)),
        check_vma=False,
    )
```

time: 1840 us -> 165 us (0.09)
  local copies, waits for them, and re-layouts: 557 us -> 13.5 us
  other arithmetic: 517 us -> 1.26 us
  blocking collectives: 511 us -> 30.6 us
  waiting for transfers between devices: 136 us -> 1.87 us
  Pallas kernels: 0 us -> 59.2 us
  matrix products: 28.8 us -> 0 us
  between operations: 21.8 us -> 1.87 us
    psum x5 -> x0, blocking collectives: 511 us -> none  [the longest x3 271 us: squares(): return lax.psum(jnp.sum(residual * residual), ('row', 'col'))]
    gather x25 -> x0, local copies, waits for them, and re-layouts: 504 us -> none  [the longest x21 484 us: element_terms(): corner_values = extended[corners]]
    scatter-add x24 -> x0, other arithmetic: 488 us -> none  [the longest x21 470 us: add_block(): total.at[corners]]
    all_gather x1 -> x0, waiting for transfers between devices: 101 us -> none  [per_device(): piece = lax.all_gather(sources, ('row', 'col'), axis=1, tiled=True)]
    pallas_call x0 -> x7, Pallas kernels: none -> 59.2 us  [call(): pl.pallas_call(body, out_shape=[jax.ShapeDtypeStruct(s, F32) for s in out...]
    ppermute x24 -> x20, waiting for transfers between devices: 34.3 us -> 1.87 us  [the longest x5 1.83 us: exchange(): lax.ppermute(pieces[1], 'row', pairs(rows, 1))]
    slice x67 -> x2, local copies, waits for them, and re-layouts: 32.4 us -> 0.01 us  [per_device(): surface_points[:, :TGT_DEV].reshape(1, 3 * TGT_DEV)]
    all_to_all x0 -> x1, blocking collectives: none -> 30.6 us  [per_device(): got = lax.all_to_all(partial, ('row', 'col'), 0, 0, tiled=True)]
  transfers between devices with their start and end apart: 25 -> 21, of which waited for: 13 -> 2; matrix products, arithmetic and copies ran while one was open for 0% -> 3% of each run, Pallas kernels for 0% -> 11%
where the time goes in v1:
time: 165 us; the launch traced here: 164 us
  Pallas kernels  59.2 us (36%)
  starting transfers between devices  55.7 us (34%)
  blocking collectives  30.6 us (19%)
  local copies, waits for them, and re-layouts  13.5 us (8%)
  waiting for transfers between devices  1.87 us (1%)
  between operations  1.87 us (1%)
    pallas_call x7, Pallas kernels, call(): pl.pallas_call(body, out_shape=[jax.ShapeDtypeStruct(s, F32) for s in out...  59.2 us
    all_to_all x1, blocking collectives, per_device(): got = lax.all_to_all(partial, ('row', 'col'), 0, 0, tiled=True)  30.6 us
    ppermute x5, starting transfers between devices, exchange(): lax.ppermute(pieces[2], 'col', pairs(cols, 0))  17.2 us
    ppermute x5, starting transfers between devices, exchange(): lax.ppermute(pieces[1], 'row', pairs(rows, 1))  14.8 us
    all_to_all x1, starting transfers between devices, per_device(): lax.all_to_all(jnp.broadcast_to(own_targets, (N_DEV, LANES)), ('row', 'co...  14.6 us
    unnamed x94, local copies, waits for them, and re-layouts  10.2 us
    ppermute x5, starting transfers between devices, exchange(): lax.ppermute(pieces[0], 'row', pairs(rows, 0))  5.53 us
    ppermute x5, starting transfers between devices, exchange(): lax.ppermute(pieces[3], 'col', pairs(cols, 1))  3.51 us
  transfers between devices with their start and end apart: 21, of which 2 were waited for; matrix products, arithmetic and copies ran while one was open for 3% of the time, Pallas kernels for 11%

profile of v1, /device:TPU:1, one launch (start us, length us, event | category | flops | bytes accessed | tf_op | source)
XLA Modules:
  0.0 163.9 jit_solution(5112766193669327410)
XLA Ops:
  2.5 1.4 shard_map.131
  4.6 3.2 %collective-permute-start = (f32[2,128]{1,0:T(2,128)S(1)}, f32[2,128]{1,0:T(2,128)S(1)}, u32[]{:S(2)}, u32[]{:S(2)}) collective-permute-start(f32[2,128]{1,0:T(2,128)S(1)} %copy-done.32), channel_id=1, source_target_pairs={{0,32},{32,0},{64,96},{96,64},{128,160},{160,128},{192,224},{224,1... | collective-permute-start | bytes 3080 | tf_op jit(solution)/shard_map/ppermute | solution.py:333
  7.8 2.1 %collective-permute-start.1 = (f32[2,128]{1,0:T(2,128)S(1)}, f32[2,128]{1,0:T(2,128)S(1)}, u32[]{:S(2)}, u32[]{:S(2)}) collective-permute-start(f32[2,128]{1,0:T(2,128)S(1)} %copy-done.30), channel_id=1, source_target_pairs={{32,64},{64,32},{96,128},{128,96},{160,192},{192,160},{33,65},{65,... | collective-permute-start | bytes 3080 | tf_op jit(solution)/shard_map/ppermute | solution.py:334
  9.9 1.7 %collective-permute-start.2 = (f32[2,128]{1,0:T(2,128)S(1)}, f32[2,128]{1,0:T(2,128)S(1)}, u32[]{:S(2)}, u32[]{:S(2)}) collective-permute-start(f32[2,128]{1,0:T(2,128)S(1)} %copy-done.29), channel_id=1, source_target_pairs={{0,1},{1,0},{2,3},{3,2},{4,5},{5,4},{6,7},{7,6},{8,9},{9,8},{10,11... | collective-permute-start | bytes 3080 | tf_op jit(solution)/shard_map/ppermute | solution.py:335
  13.3 14.6 %all-to-all-start = ((f32[256,1,128]{2,1,0:T(1,128)}), f32[256,1,128]{2,1,0:T(1,128)S(1)}, u32[]{:S(2)}, u32[]{:S(2)}) async-start(f32[256,1,128]{2,1,0:T(1,128)} %broadcast_in_dim.2), calls=%async_computation | async-start | bytes 262144 | tf_op jit(solution)/shard_map/all_to_all | solution.py:352
  27.9 1.1 copy.16
  32.0 7.2 %shard_map.132 = (f32[16,128]{1,0:T(8,128)}, f32[2,128]{1,0:T(2,128)}, f32[2,128]{1,0:T(2,128)}, f32[2,128]{1,0:T(2,128)}, f32[2,128]{1,0:T(2,128)}) custom-call(s32[2]{0:T(128)} %pad_add_fusion.parity_ref, s32[1]{0:T(128)S(6)} %copy.19.live_ref, f32[16,128]{1,0:T(8,128)} %bitcast.35, f32[2,128]{1,0:T(2,128)} %copy-done.8, f32[2,128]{1,0:T(2,128)} %copy-done.9, ...), custom_call_target="tpu_custom_call" | custom-call | tf_op jit(solution)/shard_map/pallas_call | solution.py:310
  39.9 2.1 %collective-permute-start.4 = (f32[2,128]{1,0:T(2,128)S(1)}, f32[2,128]{1,0:T(2,128)S(1)}, u32[]{:S(2)}, u32[]{:S(2)}) collective-permute-start(f32[2,128]{1,0:T(2,128)S(1)} %copy-done.41), channel_id=1, source_target_pairs={{0,32},{32,0},{64,96},{96,64},{128,160},{160,128},{192,224},{224,1... | collective-permute-start | bytes 3080 | tf_op jit(solution)/shard_map/ppermute | solution.py:333
  42.0 2.2 %collective-permute-start.5 = (f32[2,128]{1,0:T(2,128)S(1)}, f32[2,128]{1,0:T(2,128)S(1)}, u32[]{:S(2)}, u32[]{:S(2)}) collective-permute-start(f32[2,128]{1,0:T(2,128)S(1)} %copy-done.38), channel_id=1, source_target_pairs={{32,64},{64,32},{96,128},{128,96},{160,192},{192,160},{33,65},{65,... | collective-permute-start | bytes 3080 | tf_op jit(solution)/shard_map/ppermute | solution.py:334
  44.2 1.4 collective-permute-start.6
  47.6 1.7 %shard_map.133 = (f32[16,128]{1,0:T(8,128)}, f32[2,128]{1,0:T(2,128)}, f32[2,128]{1,0:T(2,128)}, f32[2,128]{1,0:T(2,128)}, f32[2,128]{1,0:T(2,128)}) custom-call(s32[2]{0:T(128)} %pad_add_fusion.parity_ref, f32[16,128]{1,0:T(8,128)} %get-tuple-element.34.own_ref, f32[2,128]{1,0:T(2,128)} %copy-done.20, f32[2,128]{1,0:T(2,128)} %copy-done.21, ...), custom_call_target="tpu_custom_call" | custom-call | tf_op jit(solution)/shard_map/pallas_call | solution.py:310
  50.0 4.3 %collective-permute-start.10 = (f32[2,128]{1,0:T(2,128)S(1)}, f32[2,128]{1,0:T(2,128)S(1)}, u32[]{:S(2)}, u32[]{:S(2)}) collective-permute-start(f32[2,128]{1,0:T(2,128)S(1)} %copy-done.42), channel_id=1, source_target_pairs={{0,1},{1,0},{2,3},{3,2},{4,5},{5,4},{6,7},{7,6},{8,9},{9,8},{10,11... | collective-permute-start | bytes 3080 | tf_op jit(solution)/shard_map/ppermute | solution.py:335
  54.4 0.8 collective-permute-start.11
  55.9 3.9 %collective-permute-start.9 = (f32[2,128]{1,0:T(2,128)S(1)}, f32[2,128]{1,0:T(2,128)S(1)}, u32[]{:S(2)}, u32[]{:S(2)}) collective-permute-start(f32[2,128]{1,0:T(2,128)S(1)} %copy-done.33), channel_id=1, source_target_pairs={{32,64},{64,32},{96,128},{128,96},{160,192},{192,160},{33,65},{65,... | collective-permute-start | bytes 3080 | tf_op jit(solution)/shard_map/ppermute | solution.py:334
  59.8 1.2 collective-permute-done.9.gb
  61.6 7.2 %shard_map.134 = (f32[16,128]{1,0:T(8,128)}, f32[2,128]{1,0:T(2,128)}, f32[2,128]{1,0:T(2,128)}, f32[2,128]{1,0:T(2,128)}, f32[2,128]{1,0:T(2,128)}) custom-call(s32[2]{0:T(128)} %pad_add_fusion.parity_ref, s32[1]{0:T(128)S(6)} %copy.19.live_ref, f32[16,128]{1,0:T(8,128)} %get-tuple-element.39.v_ref.v1_ref, f32[2,128]{1,0:T(2,128)} %copy-done.18, ...), custom_call_target="tpu_custom_call" | custom-call | tf_op jit(solution)/shard_map/pallas_call | solution.py:310
  68.9 3.7 %collective-permute-start.13 = (f32[2,128]{1,0:T(2,128)}, f32[2,128]{1,0:T(2,128)S(1)}, u32[]{:S(2)}, u32[]{:S(2)}) collective-permute-start(f32[2,128]{1,0:T(2,128)} %get-tuple-element.46), channel_id=1, source_target_pairs={{32,64},{64,32},{96,128},{128,96},{160,192},{192,160},{33,65},{65,... | collective-permute-start | bytes 3080 | tf_op jit(solution)/shard_map/ppermute | solution.py:334
  72.7 4.6 %collective-permute-start.14 = (f32[2,128]{1,0:T(2,128)}, f32[2,128]{1,0:T(2,128)S(1)}, u32[]{:S(2)}, u32[]{:S(2)}) collective-permute-start(f32[2,128]{1,0:T(2,128)} %get-tuple-element.47), channel_id=1, source_target_pairs={{0,1},{1,0},{2,3},{3,2},{4,5},{5,4},{6,7},{7,6},{8,9},{9,8},{10,11... | collective-permute-start | bytes 3080 | tf_op jit(solution)/shard_map/ppermute | solution.py:335
  79.1 1.7 %shard_map.135 = (f32[16,128]{1,0:T(8,128)}, f32[2,128]{1,0:T(2,128)}, f32[2,128]{1,0:T(2,128)}, f32[2,128]{1,0:T(2,128)}, f32[2,128]{1,0:T(2,128)}) custom-call(s32[2]{0:T(128)} %pad_add_fusion.parity_ref, f32[16,128]{1,0:T(8,128)} %get-tuple-element.44.own_ref, f32[2,128]{1,0:T(2,128)} %copy-done.22, f32[2,128]{1,0:T(2,128)} %copy-done.24, ...), custom_call_target="tpu_custom_call" | custom-call | tf_op jit(solution)/shard_map/pallas_call | solution.py:310
  82.2 3.0 %collective-permute-start.17 = (f32[2,128]{1,0:T(2,128)S(1)}, f32[2,128]{1,0:T(2,128)S(1)}, u32[]{:S(2)}, u32[]{:S(2)}) collective-permute-start(f32[2,128]{1,0:T(2,128)S(1)} %copy-done.43), channel_id=1, source_target_pairs={{32,64},{64,32},{96,128},{128,96},{160,192},{192,160},{33,65},{65,... | collective-permute-start | bytes 3080 | tf_op jit(solution)/shard_map/ppermute | solution.py:334
  85.2 5.2 %collective-permute-start.18 = (f32[2,128]{1,0:T(2,128)S(1)}, f32[2,128]{1,0:T(2,128)S(1)}, u32[]{:S(2)}, u32[]{:S(2)}) collective-permute-start(f32[2,128]{1,0:T(2,128)S(1)} %copy-done.40), channel_id=1, source_target_pairs={{0,1},{1,0},{2,3},{3,2},{4,5},{5,4},{6,7},{7,6},{8,9},{9,8},{10,11... | collective-permute-start | bytes 3080 | tf_op jit(solution)/shard_map/ppermute | solution.py:335
  92.3 38.2 %shard_map.136 = (f32[256,128]{1,0:T(8,128)}, f32[3,8,128]{2,1,0:T(8,128)}) custom-call(s32[2]{0:T(128)} %pad_add_fusion.parity_ref, s32[1]{0:T(128)S(6)} %copy.19.live_ref, f32[16,128]{1,0:T(8,128)} %bitcast.37, f32[16,128]{1,0:T(8,128)} %get-tuple-element.39.v_ref.v1_ref, f32[16,128]{1,0:T(8,128)} %get-tuple-element.49.v2_ref, f32[2,128]{1,0:T(2,128)} %copy-done.12, ...), custom_call_target="tpu_custom_call" | custom-call | tf_op jit(solution)/shard_map/pallas_call | solution.py:310
  130.5 30.6 %all_to_all.19 = f32[256,1,128]{2,1,0:T(1,128)} all-to-all(f32[256,1,128]{2,1,0:T(1,128)} %bitcast.40), channel_id=1, replica_groups=mesh['row'=8,'col'=32] {'row','col'}, dimensions={0} | all-to-all | bytes 262144 | tf_op jit(solution)/shard_map/all_to_all | solution.py:392
  161.1 1.7 %shard_map.137 = (f32[16,128]{1,0:T(8,128)}, f32[1,128]{1,0:T(1,128)}) custom-call(f32[256,128]{1,0:T(8,128)} %bitcast.30, f32[16,128]{1,0:T(8,128)} %bitcast.38, f32[16,128]{1,0:T(8,128)} %get-tuple-element.39.v_ref.v1_ref, f32[16,128]{1,0:T(8,128)} %get-tuple-element.49.v2_ref, f32[3,8,128]{2,1,0:T(8,128)} %get-tuple-element.55.trace_ref), custom_call_target="tpu_custom_call" | custom-call | tf_op jit(solution)/shard_map/pallas_call | solution.py:310
  (137 shorter events, 17.2 us)
Async XLA Ops:
  4.6 26.7 %collective-permute-start = (f32[2,128]{1,0:T(2,128)S(1)}, f32[2,128]{1,0:T(2,128)S(1)}, u32[]{:S(2)}, u32[]{:S(2)}) collective-permute-start(f32[2,128]{1,0:T(2,128)S(1)} %copy-done.32), channel_id=1, source_target_pairs={{0,32},{32,0},{64,96},{96,64},{128,160},{160,128},{192,224},{224,1... | collective-permute-start | bytes 3080 | tf_op jit(solution)/shard_map/ppermute | solution.py:333
  7.8 23.6 %collective-permute-start.1 = (f32[2,128]{1,0:T(2,128)S(1)}, f32[2,128]{1,0:T(2,128)S(1)}, u32[]{:S(2)}, u32[]{:S(2)}) collective-permute-start(f32[2,128]{1,0:T(2,128)S(1)} %copy-done.30), channel_id=1, source_target_pairs={{32,64},{64,32},{96,128},{128,96},{160,192},{192,160},{33,65},{65,... | collective-permute-start | bytes 3080 | tf_op jit(solution)/shard_map/ppermute | solution.py:334
  9.9 21.5 %collective-permute-start.2 = (f32[2,128]{1,0:T(2,128)S(1)}, f32[2,128]{1,0:T(2,128)S(1)}, u32[]{:S(2)}, u32[]{:S(2)}) collective-permute-start(f32[2,128]{1,0:T(2,128)S(1)} %copy-done.29), channel_id=1, source_target_pairs={{0,1},{1,0},{2,3},{3,2},{4,5},{5,4},{6,7},{7,6},{8,9},{9,8},{10,11... | collective-permute-start | bytes 3080 | tf_op jit(solution)/shard_map/ppermute | solution.py:335
  11.6 19.8 %collective-permute-start.3 = (f32[2,128]{1,0:T(2,128)S(1)}, f32[2,128]{1,0:T(2,128)S(1)}, u32[]{:S(2)}, u32[]{:S(2)}) collective-permute-start(f32[2,128]{1,0:T(2,128)S(1)} %copy-done.28), channel_id=1, source_target_pairs={{1,2},{2,1},{3,4},{4,3},{5,6},{6,5},{7,8},{8,7},{9,10},{10,9},{11,... | collective-permute-start | bytes 3080 | tf_op jit(solution)/shard_map/ppermute | solution.py:336
  13.3 14.6 %copy-start.3 = (f32[320]{0:T(512)S(1)}, f32[320]{0:T(512)}, u32[]{:S(2)}) copy-start(f32[320]{0:T(512)} %param.21) | copy-start | bytes 3844
  13.3 14.6 %copy-start.7 = (f32[320]{0:T(512)S(1)}, f32[320]{0:T(512)}, u32[]{:S(2)}) copy-start(f32[320]{0:T(512)} %param.22) | copy-start | bytes 3844
  13.3 78.4 %all-to-all-start = ((f32[256,1,128]{2,1,0:T(1,128)}), f32[256,1,128]{2,1,0:T(1,128)S(1)}, u32[]{:S(2)}, u32[]{:S(2)}) async-start(f32[256,1,128]{2,1,0:T(1,128)} %broadcast_in_dim.2), calls=%async_computation | async-start | bytes 262144 | tf_op jit(solution)/shard_map/all_to_all | solution.py:352
  39.9 6.5 %collective-permute-start.4 = (f32[2,128]{1,0:T(2,128)S(1)}, f32[2,128]{1,0:T(2,128)S(1)}, u32[]{:S(2)}, u32[]{:S(2)}) collective-permute-start(f32[2,128]{1,0:T(2,128)S(1)} %copy-done.41), channel_id=1, source_target_pairs={{0,32},{32,0},{64,96},{96,64},{128,160},{160,128},{192,224},{224,1... | collective-permute-start | bytes 3080 | tf_op jit(solution)/shard_map/ppermute | solution.py:333
  42.0 5.0 %collective-permute-start.5 = (f32[2,128]{1,0:T(2,128)S(1)}, f32[2,128]{1,0:T(2,128)S(1)}, u32[]{:S(2)}, u32[]{:S(2)}) collective-permute-start(f32[2,128]{1,0:T(2,128)S(1)} %copy-done.38), channel_id=1, source_target_pairs={{32,64},{64,32},{96,128},{128,96},{160,192},{192,160},{33,65},{65,... | collective-permute-start | bytes 3080 | tf_op jit(solution)/shard_map/ppermute | solution.py:334
  44.2 2.8 %collective-permute-start.6 = (f32[2,128]{1,0:T(2,128)S(1)}, f32[2,128]{1,0:T(2,128)S(1)}, u32[]{:S(2)}, u32[]{:S(2)}) collective-permute-start(f32[2,128]{1,0:T(2,128)S(1)} %copy-done.34), channel_id=1, source_target_pairs={{0,1},{1,0},{2,3},{3,2},{4,5},{5,4},{6,7},{7,6},{8,9},{9,8},{10,11... | collective-permute-start | bytes 3080 | tf_op jit(solution)/shard_map/ppermute | solution.py:335
  45.7 1.4 collective-permute-start.7
  50.0 9.7 %collective-permute-start.10 = (f32[2,128]{1,0:T(2,128)S(1)}, f32[2,128]{1,0:T(2,128)S(1)}, u32[]{:S(2)}, u32[]{:S(2)}) collective-permute-start(f32[2,128]{1,0:T(2,128)S(1)} %copy-done.42), channel_id=1, source_target_pairs={{0,1},{1,0},{2,3},{3,2},{4,5},{5,4},{6,7},{7,6},{8,9},{9,8},{10,11... | collective-permute-start | bytes 3080 | tf_op jit(solution)/shard_map/ppermute | solution.py:335
  54.4 5.4 %collective-permute-start.11 = (f32[2,128]{1,0:T(2,128)S(1)}, f32[2,128]{1,0:T(2,128)S(1)}, u32[]{:S(2)}, u32[]{:S(2)}) collective-permute-start(f32[2,128]{1,0:T(2,128)S(1)} %copy-done.39), channel_id=1, source_target_pairs={{1,2},{2,1},{3,4},{4,3},{5,6},{6,5},{7,8},{8,7},{9,10},{10,9},{11,... | collective-permute-start | bytes 3080 | tf_op jit(solution)/shard_map/ppermute | solution.py:336
  55.2 4.6 %collective-permute-start.8 = (f32[2,128]{1,0:T(2,128)S(1)}, f32[2,128]{1,0:T(2,128)S(1)}, u32[]{:S(2)}, u32[]{:S(2)}) collective-permute-start(f32[2,128]{1,0:T(2,128)S(1)} %copy-done.35), channel_id=1, source_target_pairs={{0,32},{32,0},{64,96},{96,64},{128,160},{160,128},{192,224},{224,1... | collective-permute-start | bytes 3080 | tf_op jit(solution)/shard_map/ppermute | solution.py:333
  55.9 5.1 %collective-permute-start.9 = (f32[2,128]{1,0:T(2,128)S(1)}, f32[2,128]{1,0:T(2,128)S(1)}, u32[]{:S(2)}, u32[]{:S(2)}) collective-permute-start(f32[2,128]{1,0:T(2,128)S(1)} %copy-done.33), channel_id=1, source_target_pairs={{32,64},{64,32},{96,128},{128,96},{160,192},{192,160},{33,65},{65,... | collective-permute-start | bytes 3080 | tf_op jit(solution)/shard_map/ppermute | solution.py:334
  68.8 9.1 %copy-start.2 = (f32[3,320]{1,0:T(4,128)S(1)}, f32[3,320]{1,0:T(4,128)}, u32[]{:S(2)}) copy-start(f32[3,320]{1,0:T(4,128)} %param.20) | copy-start | bytes 11524
  68.8 9.7 %collective-permute-start.12 = (f32[2,128]{1,0:T(2,128)}, f32[2,128]{1,0:T(2,128)S(1)}, u32[]{:S(2)}, u32[]{:S(2)}) collective-permute-start(f32[2,128]{1,0:T(2,128)} %get-tuple-element.45), channel_id=1, source_target_pairs={{0,32},{32,0},{64,96},{96,64},{128,160},{160,128},{192,224},{224,1... | collective-permute-start | bytes 3080 | tf_op jit(solution)/shard_map/ppermute | solution.py:333
  68.9 9.6 %collective-permute-start.13 = (f32[2,128]{1,0:T(2,128)}, f32[2,128]{1,0:T(2,128)S(1)}, u32[]{:S(2)}, u32[]{:S(2)}) collective-permute-start(f32[2,128]{1,0:T(2,128)} %get-tuple-element.46), channel_id=1, source_target_pairs={{32,64},{64,32},{96,128},{128,96},{160,192},{192,160},{33,65},{65,... | collective-permute-start | bytes 3080 | tf_op jit(solution)/shard_map/ppermute | solution.py:334
  72.7 5.9 %collective-permute-start.14 = (f32[2,128]{1,0:T(2,128)}, f32[2,128]{1,0:T(2,128)S(1)}, u32[]{:S(2)}, u32[]{:S(2)}) collective-permute-start(f32[2,128]{1,0:T(2,128)} %get-tuple-element.47), channel_id=1, source_target_pairs={{0,1},{1,0},{2,3},{3,2},{4,5},{5,4},{6,7},{7,6},{8,9},{9,8},{10,11... | collective-permute-start | bytes 3080 | tf_op jit(solution)/shard_map/ppermute | solution.py:335
  77.2 1.3 collective-permute-start.15
  81.5 10.1 %collective-permute-start.16 = (f32[2,128]{1,0:T(2,128)S(1)}, f32[2,128]{1,0:T(2,128)S(1)}, u32[]{:S(2)}, u32[]{:S(2)}) collective-permute-start(f32[2,128]{1,0:T(2,128)S(1)} %copy-done.44), channel_id=1, source_target_pairs={{0,32},{32,0},{64,96},{96,64},{128,160},{160,128},{192,224},{224,1... | collective-permute-start | bytes 3080 | tf_op jit(solution)/shard_map/ppermute | solution.py:333
  82.2 9.4 %collective-permute-start.17 = (f32[2,128]{1,0:T(2,128)S(1)}, f32[2,128]{1,0:T(2,128)S(1)}, u32[]{:S(2)}, u32[]{:S(2)}) collective-permute-start(f32[2,128]{1,0:T(2,128)S(1)} %copy-done.43), channel_id=1, source_target_pairs={{32,64},{64,32},{96,128},{128,96},{160,192},{192,160},{33,65},{65,... | collective-permute-start | bytes 3080 | tf_op jit(solution)/shard_map/ppermute | solution.py:334
  85.2 6.4 %collective-permute-start.18 = (f32[2,128]{1,0:T(2,128)S(1)}, f32[2,128]{1,0:T(2,128)S(1)}, u32[]{:S(2)}, u32[]{:S(2)}) collective-permute-start(f32[2,128]{1,0:T(2,128)S(1)} %copy-done.40), channel_id=1, source_target_pairs={{0,1},{1,0},{2,3},{3,2},{4,5},{5,4},{6,7},{7,6},{8,9},{9,8},{10,11... | collective-permute-start | bytes 3080 | tf_op jit(solution)/shard_map/ppermute | solution.py:335
  90.3 1.3 collective-permute-start.19
  (44 other events, 65.8 us)

commit v2 on v1

--- a/solution.py
+++ b/solution.py
@@ -25,6 +25,8 @@
 N_DEV = 256
 SPLITS = 3
 SCALE = 1.0 / 64.0
+VMEM_GRANT = 16 << 20
+GROUP = 4
 smoothing = 0.0001
 inverse_four_pi = 1.0 / (4.0 * math.pi)
 
@@ -88,9 +90,8 @@
     return grads, field
 
 
-def live_volume(live_ref, vol_ref, t):
-    block = pl.ds(pl.multiple_of(t * 8, 8), 8)
-    return jnp.where(t < live_ref[0], vol_ref[block, :], 0.0)
+def block_volume(vol_ref, t):
+    return vol_ref[pl.ds(pl.multiple_of(t * 8, 8), 8), :]
 
 
 def extend(parity_ref, v, ghosts):
@@ -122,8 +123,16 @@
     return [rows[2 * d:2 * d + 2] for d in range(4)]
 
 
-def pick_kernel(parity_ref, v_ref, list_ref, *out_refs):
+def pick_kernel(parity_ref, v_ref, list_ref, point_ref, target_ref, *out_refs):
     put_outgoing(parity_ref, blocks_of(gather_rows(v_ref[...], list_ref[...])), out_refs)
+    lane = lax.broadcasted_iota(jnp.int32, (1, LANES), 1)
+    own = jnp.zeros((1, LANES), F32)
+    for c in range(3):
+        part = point_ref[c:c + 1, 0:LANES]
+        if c:
+            part = pltpu.roll(part, TGT_DEV * c, 1)
+        own = jnp.where((lane >= TGT_DEV * c) & (lane < TGT_DEV * (c + 1)), part, own)
+    target_ref[...] = jnp.broadcast_to(own, (N_DEV, LANES))
 
 
 def apply_kernel(parity_ref, live_ref, v_ref, ga, gb, gc, gd, conn_ref, grad_ref, vol_ref,
@@ -133,7 +142,7 @@
     def element_block(t, carry):
         ext = ext_ref[...]
         grads, field = element_gradient(ext, conn_ref, grad_ref, t)
-        vol = live_volume(live_ref, vol_ref, t)
+        vol = block_volume(vol_ref, t)
         block = pl.ds(pl.multiple_of(t * 8, 8), 8)
         field = [vol * f for f in field]
         last = jnp.zeros_like(vol)
@@ -144,7 +153,7 @@
         term_ref[3, block, :] = last
         return carry
 
-    lax.fori_loop(0, NE_DEV // EBLK, element_block, 0)
+    lax.fori_loop(0, live_ref[0], element_block, 0)
     acc_ref[...] = jnp.zeros_like(acc_ref)
 
     def scatter_step(t, carry):
@@ -159,7 +168,7 @@
         acc_ref[...] = total
         return carry
 
-    lax.fori_loop(0, NE_DEV // EBLK, scatter_step, 0)
+    lax.fori_loop(0, live_ref[0], scatter_step, 0)
     own_ref[...] = acc_ref[0:OWN_ROWS, :]
     put_outgoing(parity_ref, swap_pairs(blocks_of(acc_ref[OWN_ROWS:EXT_ROWS, :])), (oa, ob, oc, od))
 
@@ -192,7 +201,7 @@
 
 def far_kernel(parity_ref, live_ref, b_ref, v1_ref, v2_ref, ga, gb, gc, gd, conn_ref, grad_ref, vol_ref,
                mass_ref, node_ref, src_ref, tgt_ref,
-               out_ref, trace_ref, ext_ref, tx, ty, tz, d0, d1, d2, lhs_ref):
+               out_ref, trace_ref, ext_ref, tx, ty, tz, d0, d1, d2, lhs_ref, wide_ref, entry_ref):
     b = b_ref[...]
     v1 = v1_ref[...]
     v2 = v2_ref[...]
@@ -201,10 +210,10 @@
     def energy_block(t, total):
         ext = ext_ref[...]
         _, field = element_gradient(ext, conn_ref, grad_ref, t)
-        vol = live_volume(live_ref, vol_ref, t)
+        vol = block_volume(vol_ref, t)
         return total + vol * (field[0] * field[0] + field[1] * field[1] + field[2] * field[2])
 
-    energy = lax.fori_loop(0, NE_DEV // EBLK, energy_block, jnp.zeros((8, LANES), F32))
+    energy = lax.fori_loop(0, live_ref[0], energy_block, jnp.zeros((8, LANES), F32))
     pairs = [b * b, b * v1, v1 * v1, v1 * v2, v2 * v2, mass_ref[...] * v2 * v2]
     sums = [p[0:8] + p[8:16] for p in pairs]
     sums[5] = (sums[5] + energy) * SCALE
@@ -240,26 +249,36 @@
         ref[...] = out
 
     cols = jnp.transpose(src_ref[...])
-
-    def target_row(g, carry):
-        at = pl.ds(g, 1)
-        px = tx[at, :]
-        py = ty[at, :]
-        pz = tz[at, :]
-        dx = px - cols[:, 0:1]
-        dy = py - cols[:, 1:2]
-        dz = pz - cols[:, 2:3]
-        radius_sq = dx * dx + dy * dy + dz * dz + smoothing
-        inverse = lax.rsqrt(radius_sq)
-        numerator = dx * cols[:, 3:4] + dy * cols[:, 4:5] + dz * cols[:, 5:6]
-        entries = (numerator * (inverse * inverse * inverse)).astype(BF16)
-        res = jnp.dot(lhs_ref[...], entries, preferred_element_type=F32)
-        d0[at, :] = res[0:1] + res[1:2]
-        d1[at, :] = res[2:3] + res[3:4]
-        d2[at, :] = res[4:5] + res[5:6]
+    for c in range(6):
+        wide_ref[c] = jnp.broadcast_to(cols[:, c:c + 1], (PAD_SLOTS, LANES))
+    entry_ref[SLOTS:PAD_SLOTS, :] = jnp.zeros((PAD_SLOTS - SLOTS, GROUP * LANES), BF16)
+
+    def target_group(g, carry):
+        first = g * GROUP
+        for s in range(SLOTS // 16):
+            rows = slice(16 * s, 16 * s + 16)
+            sx, sy, sz, wx, wy, wz = [wide_ref[c, rows, :] for c in range(6)]
+            for q in range(GROUP):
+                at = pl.ds(first + q, 1)
+                dx = tx[at, :] - sx
+                dy = ty[at, :] - sy
+                dz = tz[at, :] - sz
+                radius_sq = dx * dx + dy * dy + dz * dz + smoothing
+                inverse = lax.rsqrt(radius_sq)
+                numerator = dx * wx + dy * wy + dz * wz
+                entry_ref[rows, q * LANES:(q + 1) * LANES] = (
+                    numerator * (inverse * inverse * inverse)
+                ).astype(BF16)
+        res = jnp.dot(lhs_ref[...], entry_ref[...], preferred_element_type=F32)
+        for q in range(GROUP):
+            at = pl.ds(first + q, 1)
+            part = res[:, q * LANES:(q + 1) * LANES]
+            d0[at, :] = part[0:1] + part[1:2]
+            d1[at, :] = part[2:3] + part[3:4]
+            d2[at, :] = part[4:5] + part[5:6]
         return carry
 
-    lax.fori_loop(0, N_DEV // 4, target_row, 0)
+    lax.fori_loop(0, N_DEV // 4 // GROUP, target_group, 0)
     spread = jnp.broadcast_to(moments, (N_DEV // 4, LANES))
     for j in range(4):
         out = spread
@@ -301,7 +320,7 @@
         if k:
             part = pltpu.roll(total, LANES - 32 * k, 1)
         out = out + c * (part - 0.5 * trace_ref[k, 0:1, :])
-    dir_ref[...] = out
+    dir_ref[...] = out[:, 0:TGT_DEV]
 
 
 def call(body, out_shapes, smem, args, scratch=(), flops=1000000):
@@ -313,6 +332,7 @@
         in_specs=specs,
         out_specs=[pl.BlockSpec(memory_space=pltpu.VMEM)] * len(out_shapes),
         scratch_shapes=list(scratch),
+        compiler_params=pltpu.CompilerParams(vmem_limit_bytes=VMEM_GRANT),
     )(*args)
 
 
@@ -329,12 +349,11 @@
 def exchange(pieces):
     rows = lax.axis_size("row")
     cols = lax.axis_size("col")
-    return [
-        lax.ppermute(pieces[0], "row", pairs(rows, 0)),
-        lax.ppermute(pieces[1], "row", pairs(rows, 1)),
-        lax.ppermute(pieces[2], "col", pairs(cols, 0)),
-        lax.ppermute(pieces[3], "col", pairs(cols, 1)),
-    ]
+    row_a = lax.ppermute(pieces[0], "row", pairs(rows, 0))
+    col_a = lax.ppermute(pieces[2], "col", pairs(cols, 0))
+    row_b = lax.ppermute(pieces[1], "row", pairs(rows, 1))
+    col_b = lax.ppermute(pieces[3], "col", pairs(cols, 1))
+    return [row_a, row_b, col_a, col_b]
 
 
 def per_device(connectivity, gradients, volumes, live_blocks, send_lists, divergence, mass_shift,
@@ -348,10 +367,6 @@
     mass = mass_shift.reshape(OWN_ROWS, LANES)
     nodes = jnp.pad(boundary_nodes, (0, 8 * LANES - SLOTS)).reshape(8, LANES)
 
-    own_targets = jnp.pad(surface_points[:, :TGT_DEV].reshape(1, 3 * TGT_DEV), ((0, 0), (0, TGT_DEV)))
-    targets = lax.all_to_all(
-        jnp.broadcast_to(own_targets, (N_DEV, LANES)), ("row", "col"), 0, 0, tiled=True
-    )
     sine = jnp.sqrt(1.0 - normal_cos * normal_cos)
     normals = jnp.stack([sine * jnp.cos(normal_angle), sine * jnp.sin(normal_angle), normal_cos])
     weighted = (node_areas * inverse_four_pi)[None, :] * normals
@@ -377,7 +392,10 @@
         )
         return new, out
 
-    first = call(pick_kernel, [PIECE] * 4, 1, (parity, b, lists))
+    mine, *first = call(
+        pick_kernel, [(N_DEV, LANES)] + [PIECE] * 4, 1, (parity, b, lists, surface_points)
+    )
+    targets = lax.all_to_all(mine, ("row", "col"), 0, 0, tiled=True)
     v1, second = apply(b, first)
     v2, third = apply(v1, second)
     ghosts = exchange(third)
@@ -387,13 +405,17 @@
         (parity, live_blocks, b, v1, v2, *ghosts, conn, grads, vol, mass, nodes, sources, targets),
         scratch=[pltpu.VMEM((EXT_ROWS, LANES), F32)]
         + [pltpu.VMEM(sub, F32)] * 6
-        + [pltpu.VMEM((8, PAD_SLOTS), BF16)],
+        + [
+            pltpu.VMEM((8, PAD_SLOTS), BF16),
+            pltpu.VMEM((6, PAD_SLOTS, LANES), F32),
+            pltpu.VMEM((PAD_SLOTS, GROUP * LANES), BF16),
+        ],
     )
     got = lax.all_to_all(partial, ("row", "col"), 0, 0, tiled=True)
     potential, dirichlet = call(
-        final_kernel, [(OWN_ROWS, LANES), (1, LANES)], 0, (got, b, v1, v2, trace)
-    )
-    return potential.reshape(NN_DEV), dirichlet[0, :TGT_DEV]
+        final_kernel, [(OWN_ROWS, LANES), (1, TGT_DEV)], 0, (got, b, v1, v2, trace)
+    )
+    return potential.reshape(NN_DEV), dirichlet.reshape(TGT_DEV)
 
 
 def solution(mesh):

time: 165 us -> 118 us (0.72)
  Pallas kernels: 59.2 us -> 19.4 us
  local copies, waits for them, and re-layouts: 13.5 us -> 3.46 us
  waiting for transfers between devices: 1.87 us -> 3.98 us
  starting transfers between devices: 55.7 us -> 57.4 us
    pallas_call x7, Pallas kernels: 59.2 us -> 19.4 us  [call(): pl.pallas_call(body, out_shape=[jax.ShapeDtypeStruct(s, F32) for s in out...]
    unnamed x94 -> x22, local copies, waits for them, and re-layouts: 10.2 us -> 3.41 us
    ppermute x20, waiting for transfers between devices: 1.87 us -> 3.98 us  [the longest x5 2.35 us: exchange(): col_a = lax.ppermute(pieces[2], 'col', pairs(cols, 0))]
  transfers between devices with their start and end apart: 21 -> 21, of which waited for: 2 -> 5; matrix products, arithmetic and copies ran while one was open for 3% -> 1% of each run, Pallas kernels for 11% -> 5%
where the time goes in v2:
time: 118 us; the launch traced here: 117 us
  starting transfers between devices  57.4 us (49%)
  blocking collectives  30.9 us (26%)
  Pallas kernels  19.4 us (16%)
  waiting for transfers between devices  3.98 us (3%)
  local copies, waits for them, and re-layouts  3.46 us (3%)
  between operations  1.69 us (1%)
    all_to_all x1, blocking collectives, per_device(): got = lax.all_to_all(partial, ('row', 'col'), 0, 0, tiled=True)  30.9 us
    ppermute x5, starting transfers between devices, exchange(): row_b = lax.ppermute(pieces[1], 'row', pairs(rows, 1))  23.8 us
    pallas_call x7, Pallas kernels, call(): pl.pallas_call(body, out_shape=[jax.ShapeDtypeStruct(s, F32) for s in out...  19.4 us
    all_to_all x1, starting transfers between devices, per_device(): targets = lax.all_to_all(mine, ('row', 'col'), 0, 0, tiled=True)  14.9 us
    ppermute x5, starting transfers between devices, exchange(): col_a = lax.ppermute(pieces[2], 'col', pairs(cols, 0))  9.08 us
    ppermute x5, starting transfers between devices, exchange(): row_a = lax.ppermute(pieces[0], 'row', pairs(rows, 0))  6.4 us
    unnamed x22, local copies, waits for them, and re-layouts  3.41 us
    ppermute x5, starting transfers between devices, exchange(): col_b = lax.ppermute(pieces[3], 'col', pairs(cols, 1))  3.26 us
  transfers between devices with their start and end apart: 21, of which 5 were waited for; matrix products, arithmetic and copies ran while one was open for 1% of the time, Pallas kernels for 5%

profile of v2, /device:TPU:1, one launch (start us, length us, event | category | flops | bytes accessed | tf_op | source)
XLA Modules:
  0.0 117.0 jit_solution(2411254298132904241)
XLA Ops:
  2.0 1.3 %shard_map.131 = (f32[256,128]{1,0:T(8,128)}, f32[2,128]{1,0:T(2,128)S(1)}, f32[2,128]{1,0:T(2,128)S(1)}, f32[2,128]{1,0:T(2,128)S(1)}, f32[2,128]{1,0:T(2,128)S(1)}) custom-call(s32[2]{0:T(128)S(1)} %pad_add_fusion.parity_ref, f32[16,128]{1,0:T(8,128)S(1)} %bitcast.32, s32[8,128]{1,0:T(8,128)S(1)} %reshape.37.list_ref, f32[3,320]{1,0:T(4,128)S(1)} %copy-done.3), custom_call_target="tpu_custom_call" | custom-call | tf_op jit(solution)/shard_map/pallas_call | solution.py:329
  3.3 3.2 %collective-permute-start = (f32[2,128]{1,0:T(2,128)S(1)}, f32[2,128]{1,0:T(2,128)S(1)}, u32[]{:S(2)}, u32[]{:S(2)}) collective-permute-start(f32[2,128]{1,0:T(2,128)S(1)} %get-tuple-element.31), channel_id=1, source_target_pairs={{0,32},{32,0},{64,96},{96,64},{128,160},{160,128},{192,224},{224,1... | collective-permute-start | bytes 3080 | tf_op jit(solution)/shard_map/ppermute | solution.py:352
  6.5 1.9 %collective-permute-start.1 = (f32[2,128]{1,0:T(2,128)S(1)}, f32[2,128]{1,0:T(2,128)S(1)}, u32[]{:S(2)}, u32[]{:S(2)}) collective-permute-start(f32[2,128]{1,0:T(2,128)S(1)} %get-tuple-element.32), channel_id=1, source_target_pairs={{32,64},{64,32},{96,128},{128,96},{160,192},{192,160},{33,65},{65,... | collective-permute-start | bytes 3080 | tf_op jit(solution)/shard_map/ppermute | solution.py:354
  8.4 1.1 collective-permute-start.2
  10.2 14.9 %all-to-all-start = ((f32[256,1,128]{2,1,0:T(1,128)}), f32[256,1,128]{2,1,0:T(1,128)S(1)}, u32[]{:S(2)}, u32[]{:S(2)}) async-start(f32[256,1,128]{2,1,0:T(1,128)} %bitcast.7), calls=%async_computation | async-start | bytes 262144 | tf_op jit(solution)/shard_map/all_to_all | solution.py:398
  25.2 1.1 copy.17
  26.4 0.9 copy-done.4
  28.1 1.9 %shard_map.132 = (f32[16,128]{1,0:T(8,128)S(1)}, f32[2,128]{1,0:T(2,128)S(1)}, f32[2,128]{1,0:T(2,128)S(1)}, f32[2,128]{1,0:T(2,128)S(1)}, f32[2,128]{1,0:T(2,128)S(1)}) custom-call(s32[2]{0:T(128)S(1)} %pad_add_fusion.parity_ref, s32[1]{0:T(128)S(6)} %copy.20.live_ref, f32[16,128]{1,0:T(8,128)S(1)} %bitcast.33, f32[2,128]{1,0:T(2,128)S(1)} %collective-permute-done.ga, ...), custom_call_target="tpu_custom_call" | custom-call | tf_op jit(solution)/shard_map/pallas_call | solution.py:329
  30.0 2.9 %collective-permute-start.4 = (f32[2,128]{1,0:T(2,128)S(1)}, f32[2,128]{1,0:T(2,128)S(1)}, u32[]{:S(2)}, u32[]{:S(2)}) collective-permute-start(f32[2,128]{1,0:T(2,128)S(1)} %get-tuple-element.36), channel_id=1, source_target_pairs={{0,32},{32,0},{64,96},{96,64},{128,160},{160,128},{192,224},{224,1... | collective-permute-start | bytes 3080 | tf_op jit(solution)/shard_map/ppermute | solution.py:352
  32.9 4.9 %collective-permute-start.5 = (f32[2,128]{1,0:T(2,128)S(1)}, f32[2,128]{1,0:T(2,128)S(1)}, u32[]{:S(2)}, u32[]{:S(2)}) collective-permute-start(f32[2,128]{1,0:T(2,128)S(1)} %get-tuple-element.37), channel_id=1, source_target_pairs={{32,64},{64,32},{96,128},{128,96},{160,192},{192,160},{33,65},{65,... | collective-permute-start | bytes 3080 | tf_op jit(solution)/shard_map/ppermute | solution.py:354
  39.1 1.3 %collective-permute-done.6.rc = f32[2,128]{1,0:T(2,128)S(1)} collective-permute-done((f32[2,128]{1,0:T(2,128)S(1)}, f32[2,128]{1,0:T(2,128)S(1)}, u32[]{:S(2)}, u32[]{:S(2)}) %collective-permute-start.6) | collective-permute-done | bytes 1056 | tf_op jit(solution)/shard_map/ppermute | solution.py:353
  40.3 0.9 shard_map.133
  41.2 3.4 %collective-permute-start.10 = (f32[2,128]{1,0:T(2,128)S(1)}, f32[2,128]{1,0:T(2,128)S(1)}, u32[]{:S(2)}, u32[]{:S(2)}) collective-permute-start(f32[2,128]{1,0:T(2,128)S(1)} %get-tuple-element.43), channel_id=1, source_target_pairs={{0,1},{1,0},{2,3},{3,2},{4,5},{5,4},{6,7},{7,6},{8,9},{9,8},{10,11... | collective-permute-start | bytes 3080 | tf_op jit(solution)/shard_map/ppermute | solution.py:353
  45.4 3.6 %collective-permute-start.9 = (f32[2,128]{1,0:T(2,128)S(1)}, f32[2,128]{1,0:T(2,128)S(1)}, u32[]{:S(2)}, u32[]{:S(2)}) collective-permute-start(f32[2,128]{1,0:T(2,128)S(1)} %get-tuple-element.42), channel_id=1, source_target_pairs={{32,64},{64,32},{96,128},{128,96},{160,192},{192,160},{33,65},{65,... | collective-permute-start | bytes 3080 | tf_op jit(solution)/shard_map/ppermute | solution.py:354
  49.1 1.2 %collective-permute-done.9.gb = f32[2,128]{1,0:T(2,128)S(1)} collective-permute-done((f32[2,128]{1,0:T(2,128)S(1)}, f32[2,128]{1,0:T(2,128)S(1)}, u32[]{:S(2)}, u32[]{:S(2)}) %collective-permute-start.9) | collective-permute-done | bytes 1056 | tf_op jit(solution)/shard_map/ppermute | solution.py:354
  50.3 1.9 %shard_map.134 = (f32[16,128]{1,0:T(8,128)S(1)}, f32[2,128]{1,0:T(2,128)S(1)}, f32[2,128]{1,0:T(2,128)S(1)}, f32[2,128]{1,0:T(2,128)S(1)}, f32[2,128]{1,0:T(2,128)S(1)}) custom-call(s32[2]{0:T(128)S(1)} %pad_add_fusion.parity_ref, s32[1]{0:T(128)S(6)} %copy.20.live_ref, f32[16,128]{1,0:T(8,128)S(1)} %get-tuple-element.40.v_ref.v1_ref, ...), custom_call_target="tpu_custom_call" | custom-call | tf_op jit(solution)/shard_map/pallas_call | solution.py:329
  52.3 7.8 %collective-permute-start.13 = (f32[2,128]{1,0:T(2,128)S(1)}, f32[2,128]{1,0:T(2,128)S(1)}, u32[]{:S(2)}, u32[]{:S(2)}) collective-permute-start(f32[2,128]{1,0:T(2,128)S(1)} %get-tuple-element.47), channel_id=1, source_target_pairs={{32,64},{64,32},{96,128},{128,96},{160,192},{192,160},{33,65},{65,... | collective-permute-start | bytes 3080 | tf_op jit(solution)/shard_map/ppermute | solution.py:354
  60.1 1.0 collective-permute-start.14
  61.8 0.8 collective-permute-done.14.rc
  62.6 0.8 shard_map.135
  63.6 5.6 %collective-permute-start.17 = (f32[2,128]{1,0:T(2,128)S(1)}, f32[2,128]{1,0:T(2,128)S(1)}, u32[]{:S(2)}, u32[]{:S(2)}) collective-permute-start(f32[2,128]{1,0:T(2,128)S(1)} %get-tuple-element.52), channel_id=1, source_target_pairs={{32,64},{64,32},{96,128},{128,96},{160,192},{192,160},{33,65},{65,... | collective-permute-start | bytes 3080 | tf_op jit(solution)/shard_map/ppermute | solution.py:354
  69.2 3.5 %collective-permute-start.18 = (f32[2,128]{1,0:T(2,128)S(1)}, f32[2,128]{1,0:T(2,128)S(1)}, u32[]{:S(2)}, u32[]{:S(2)}) collective-permute-start(f32[2,128]{1,0:T(2,128)S(1)} %get-tuple-element.53), channel_id=1, source_target_pairs={{0,1},{1,0},{2,3},{3,2},{4,5},{5,4},{6,7},{7,6},{8,9},{9,8},{10,11... | collective-permute-start | bytes 3080 | tf_op jit(solution)/shard_map/ppermute | solution.py:353
  73.6 11.8 %shard_map.136 = (f32[256,128]{1,0:T(8,128)S(1)}, f32[3,8,128]{2,1,0:T(8,128)S(1)}) custom-call(s32[2]{0:T(128)S(1)} %pad_add_fusion.parity_ref, s32[1]{0:T(128)S(6)} %copy.20.live_ref, f32[16,128]{1,0:T(8,128)S(1)} %bitcast.35, f32[16,128]{1,0:T(8,128)S(1)} %get-tuple-element.40.v_ref.v1_ref, f32[16,128]{1,0:T(8,128)S(1)} %get-tuple-element.50.v2_ref, ...), custom_call_target="tpu_custom_call" | custom-call | tf_op jit(solution)/shard_map/pallas_call | solution.py:329
  85.3 30.9 %all_to_all.22 = f32[256,1,128]{2,1,0:T(1,128)S(1)} all-to-all(f32[256,1,128]{2,1,0:T(1,128)S(1)} %bitcast.37), channel_id=1, replica_groups=mesh['row'=8,'col'=32] {'row','col'}, dimensions={0} | all-to-all | bytes 262144 | tf_op jit(solution)/shard_map/all_to_all | solution.py:414
  (59 shorter events, 6.7 us)
Async XLA Ops:
  3.3 24.6 %collective-permute-start = (f32[2,128]{1,0:T(2,128)S(1)}, f32[2,128]{1,0:T(2,128)S(1)}, u32[]{:S(2)}, u32[]{:S(2)}) collective-permute-start(f32[2,128]{1,0:T(2,128)S(1)} %get-tuple-element.31), channel_id=1, source_target_pairs={{0,32},{32,0},{64,96},{96,64},{128,160},{160,128},{192,224},{224,1... | collective-permute-start | bytes 3080 | tf_op jit(solution)/shard_map/ppermute | solution.py:352
  6.5 21.5 %collective-permute-start.1 = (f32[2,128]{1,0:T(2,128)S(1)}, f32[2,128]{1,0:T(2,128)S(1)}, u32[]{:S(2)}, u32[]{:S(2)}) collective-permute-start(f32[2,128]{1,0:T(2,128)S(1)} %get-tuple-element.32), channel_id=1, source_target_pairs={{32,64},{64,32},{96,128},{128,96},{160,192},{192,160},{33,65},{65,... | collective-permute-start | bytes 3080 | tf_op jit(solution)/shard_map/ppermute | solution.py:354
  8.4 19.5 %collective-permute-start.2 = (f32[2,128]{1,0:T(2,128)S(1)}, f32[2,128]{1,0:T(2,128)S(1)}, u32[]{:S(2)}, u32[]{:S(2)}) collective-permute-start(f32[2,128]{1,0:T(2,128)S(1)} %get-tuple-element.33), channel_id=1, source_target_pairs={{0,1},{1,0},{2,3},{3,2},{4,5},{5,4},{6,7},{7,6},{8,9},{9,8},{10,11... | collective-permute-start | bytes 3080 | tf_op jit(solution)/shard_map/ppermute | solution.py:353
  9.5 18.5 %collective-permute-start.3 = (f32[2,128]{1,0:T(2,128)S(1)}, f32[2,128]{1,0:T(2,128)S(1)}, u32[]{:S(2)}, u32[]{:S(2)}) collective-permute-start(f32[2,128]{1,0:T(2,128)S(1)} %get-tuple-element.34), channel_id=1, source_target_pairs={{1,2},{2,1},{3,4},{4,3},{5,6},{6,5},{7,8},{8,7},{9,10},{10,9},{11,... | collective-permute-start | bytes 3080 | tf_op jit(solution)/shard_map/ppermute | solution.py:355
  10.2 15.0 %copy-start.5 = (f32[320]{0:T(512)S(1)}, f32[320]{0:T(512)}, u32[]{:S(2)}) copy-start(f32[320]{0:T(512)} %param.21) | copy-start | bytes 3844
  10.2 15.0 %copy-start.9 = (f32[320]{0:T(512)S(1)}, f32[320]{0:T(512)}, u32[]{:S(2)}) copy-start(f32[320]{0:T(512)} %param.22) | copy-start | bytes 3844
  10.2 63.4 %all-to-all-start = ((f32[256,1,128]{2,1,0:T(1,128)}), f32[256,1,128]{2,1,0:T(1,128)S(1)}, u32[]{:S(2)}, u32[]{:S(2)}) async-start(f32[256,1,128]{2,1,0:T(1,128)} %bitcast.7), calls=%async_computation | async-start | bytes 262144 | tf_op jit(solution)/shard_map/all_to_all | solution.py:398
  30.0 8.7 %collective-permute-start.4 = (f32[2,128]{1,0:T(2,128)S(1)}, f32[2,128]{1,0:T(2,128)S(1)}, u32[]{:S(2)}, u32[]{:S(2)}) collective-permute-start(f32[2,128]{1,0:T(2,128)S(1)} %get-tuple-element.36), channel_id=1, source_target_pairs={{0,32},{32,0},{64,96},{96,64},{128,160},{160,128},{192,224},{224,1... | collective-permute-start | bytes 3080 | tf_op jit(solution)/shard_map/ppermute | solution.py:352
  32.9 6.1 %collective-permute-start.5 = (f32[2,128]{1,0:T(2,128)S(1)}, f32[2,128]{1,0:T(2,128)S(1)}, u32[]{:S(2)}, u32[]{:S(2)}) collective-permute-start(f32[2,128]{1,0:T(2,128)S(1)} %get-tuple-element.37), channel_id=1, source_target_pairs={{32,64},{64,32},{96,128},{128,96},{160,192},{192,160},{33,65},{65,... | collective-permute-start | bytes 3080 | tf_op jit(solution)/shard_map/ppermute | solution.py:354
  37.8 2.5 %collective-permute-start.6 = (f32[2,128]{1,0:T(2,128)S(1)}, f32[2,128]{1,0:T(2,128)S(1)}, u32[]{:S(2)}, u32[]{:S(2)}) collective-permute-start(f32[2,128]{1,0:T(2,128)S(1)} %get-tuple-element.38), channel_id=1, source_target_pairs={{0,1},{1,0},{2,3},{3,2},{4,5},{5,4},{6,7},{7,6},{8,9},{9,8},{10,11... | collective-permute-start | bytes 3080 | tf_op jit(solution)/shard_map/ppermute | solution.py:353
  37.9 2.4 %collective-permute-start.7 = (f32[2,128]{1,0:T(2,128)S(1)}, f32[2,128]{1,0:T(2,128)S(1)}, u32[]{:S(2)}, u32[]{:S(2)}) collective-permute-start(f32[2,128]{1,0:T(2,128)S(1)} %get-tuple-element.39), channel_id=1, source_target_pairs={{1,2},{2,1},{3,4},{4,3},{5,6},{6,5},{7,8},{8,7},{9,10},{10,9},{11,... | collective-permute-start | bytes 3080 | tf_op jit(solution)/shard_map/ppermute | solution.py:355
  41.2 7.8 %collective-permute-start.10 = (f32[2,128]{1,0:T(2,128)S(1)}, f32[2,128]{1,0:T(2,128)S(1)}, u32[]{:S(2)}, u32[]{:S(2)}) collective-permute-start(f32[2,128]{1,0:T(2,128)S(1)} %get-tuple-element.43), channel_id=1, source_target_pairs={{0,1},{1,0},{2,3},{3,2},{4,5},{5,4},{6,7},{7,6},{8,9},{9,8},{10,11... | collective-permute-start | bytes 3080 | tf_op jit(solution)/shard_map/ppermute | solution.py:353
  44.6 4.4 %collective-permute-start.11 = (f32[2,128]{1,0:T(2,128)S(1)}, f32[2,128]{1,0:T(2,128)S(1)}, u32[]{:S(2)}, u32[]{:S(2)}) collective-permute-start(f32[2,128]{1,0:T(2,128)S(1)} %get-tuple-element.44), channel_id=1, source_target_pairs={{1,2},{2,1},{3,4},{4,3},{5,6},{6,5},{7,8},{8,7},{9,10},{10,9},{11,... | collective-permute-start | bytes 3080 | tf_op jit(solution)/shard_map/ppermute | solution.py:355
  45.3 3.8 %collective-permute-start.8 = (f32[2,128]{1,0:T(2,128)S(1)}, f32[2,128]{1,0:T(2,128)S(1)}, u32[]{:S(2)}, u32[]{:S(2)}) collective-permute-start(f32[2,128]{1,0:T(2,128)S(1)} %get-tuple-element.41), channel_id=1, source_target_pairs={{0,32},{32,0},{64,96},{96,64},{128,160},{160,128},{192,224},{224,1... | collective-permute-start | bytes 3080 | tf_op jit(solution)/shard_map/ppermute | solution.py:352
  45.4 4.9 %collective-permute-start.9 = (f32[2,128]{1,0:T(2,128)S(1)}, f32[2,128]{1,0:T(2,128)S(1)}, u32[]{:S(2)}, u32[]{:S(2)}) collective-permute-start(f32[2,128]{1,0:T(2,128)S(1)} %get-tuple-element.42), channel_id=1, source_target_pairs={{32,64},{64,32},{96,128},{128,96},{160,192},{192,160},{33,65},{65,... | collective-permute-start | bytes 3080 | tf_op jit(solution)/shard_map/ppermute | solution.py:354
  52.2 9.6 %collective-permute-start.12 = (f32[2,128]{1,0:T(2,128)S(1)}, f32[2,128]{1,0:T(2,128)S(1)}, u32[]{:S(2)}, u32[]{:S(2)}) collective-permute-start(f32[2,128]{1,0:T(2,128)S(1)} %get-tuple-element.46), channel_id=1, source_target_pairs={{0,32},{32,0},{64,96},{96,64},{128,160},{160,128},{192,224},{224,1... | collective-permute-start | bytes 3080 | tf_op jit(solution)/shard_map/ppermute | solution.py:352
  52.3 9.5 %collective-permute-start.13 = (f32[2,128]{1,0:T(2,128)S(1)}, f32[2,128]{1,0:T(2,128)S(1)}, u32[]{:S(2)}, u32[]{:S(2)}) collective-permute-start(f32[2,128]{1,0:T(2,128)S(1)} %get-tuple-element.47), channel_id=1, source_target_pairs={{32,64},{64,32},{96,128},{128,96},{160,192},{192,160},{33,65},{65,... | collective-permute-start | bytes 3080 | tf_op jit(solution)/shard_map/ppermute | solution.py:354
  60.1 2.5 %collective-permute-start.14 = (f32[2,128]{1,0:T(2,128)S(1)}, f32[2,128]{1,0:T(2,128)S(1)}, u32[]{:S(2)}, u32[]{:S(2)}) collective-permute-start(f32[2,128]{1,0:T(2,128)S(1)} %get-tuple-element.48), channel_id=1, source_target_pairs={{0,1},{1,0},{2,3},{3,2},{4,5},{5,4},{6,7},{7,6},{8,9},{9,8},{10,11... | collective-permute-start | bytes 3080 | tf_op jit(solution)/shard_map/ppermute | solution.py:353
  61.1 1.5 %collective-permute-start.15 = (f32[2,128]{1,0:T(2,128)S(1)}, f32[2,128]{1,0:T(2,128)S(1)}, u32[]{:S(2)}, u32[]{:S(2)}) collective-permute-start(f32[2,128]{1,0:T(2,128)S(1)} %get-tuple-element.49), channel_id=1, source_target_pairs={{1,2},{2,1},{3,4},{4,3},{5,6},{6,5},{7,8},{8,7},{9,10},{10,9},{11,... | collective-permute-start | bytes 3080 | tf_op jit(solution)/shard_map/ppermute | solution.py:355
  63.5 9.8 %collective-permute-start.16 = (f32[2,128]{1,0:T(2,128)S(1)}, f32[2,128]{1,0:T(2,128)S(1)}, u32[]{:S(2)}, u32[]{:S(2)}) collective-permute-start(f32[2,128]{1,0:T(2,128)S(1)} %get-tuple-element.51), channel_id=1, source_target_pairs={{0,32},{32,0},{64,96},{96,64},{128,160},{160,128},{192,224},{224,1... | collective-permute-start | bytes 3080 | tf_op jit(solution)/shard_map/ppermute | solution.py:352
  63.6 9.7 %copy-start.7 = (s32[320]{0:T(512)S(1)}, s32[320]{0:T(512)}, u32[]{:S(2)}) copy-start(s32[320]{0:T(512)} %param.19) | copy-start | bytes 3844
  63.6 9.7 %collective-permute-start.17 = (f32[2,128]{1,0:T(2,128)S(1)}, f32[2,128]{1,0:T(2,128)S(1)}, u32[]{:S(2)}, u32[]{:S(2)}) collective-permute-start(f32[2,128]{1,0:T(2,128)S(1)} %get-tuple-element.52), channel_id=1, source_target_pairs={{32,64},{64,32},{96,128},{128,96},{160,192},{192,160},{33,65},{65,... | collective-permute-start | bytes 3080 | tf_op jit(solution)/shard_map/ppermute | solution.py:354
  69.2 4.4 %collective-permute-start.18 = (f32[2,128]{1,0:T(2,128)S(1)}, f32[2,128]{1,0:T(2,128)S(1)}, u32[]{:S(2)}, u32[]{:S(2)}) collective-permute-start(f32[2,128]{1,0:T(2,128)S(1)} %get-tuple-element.53), channel_id=1, source_target_pairs={{0,1},{1,0},{2,3},{3,2},{4,5},{5,4},{6,7},{7,6},{8,9},{9,8},{10,11... | collective-permute-start | bytes 3080 | tf_op jit(solution)/shard_map/ppermute | solution.py:353
  72.6 1.0 collective-permute-start.19
  (7 other events, 11.1 us)

commit v3 on v2

v3 whole, which is shorter than its diff:
```python
import math

import jax
import jax.numpy as jnp
from jax import lax
from jax.experimental import pallas as pl
from jax.experimental.pallas import tpu as pltpu
from jax.sharding import PartitionSpec as P


F32 = jnp.float32
BF16 = jnp.bfloat16
LANES = 128
NN_DEV = 2048
GH = 256
TGT_DEV = 32
OWN_ROWS = NN_DEV // LANES
EXT_ROWS = OWN_ROWS + 4 * GH // LANES
HIGH_ROWS = 32
ELEM_ROWS = 64
SLOTS = 320
PAD_SLOTS = 384
N_DEV = 256
TGT_ROWS = N_DEV // 4
CHUNKS = 4
GROUP = 4
KDIM = 32
SPLITS = 3
SCALE = 1.0 / 64.0
VMEM_GRANT = 16 << 20
smoothing = 0.0001
inverse_four_pi = 1.0 / (4.0 * math.pi)


def gather_rows(table, index):
    high = index >> 7
    low = index & 127
    out = jnp.zeros(index.shape, F32)
    for r in range(table.shape[0]):
        row = jnp.broadcast_to(table[r:r + 1, :], index.shape)
        out = jnp.where(high == r, jnp.take_along_axis(row, low, axis=1), out)
    return out


def split_terms(terms, count=SPLITS):
    parts = []
    for _ in range(count):
        parts.append(terms.astype(BF16))
        terms = terms - parts[-1].astype(F32)
    return parts


def scatter_block(index, terms, rows):
    rows = -(-rows // 16) * 16
    sub = lax.broadcasted_iota(jnp.int32, (LANES, LANES), 0).astype(F32).astype(BF16)
    sub_rows = lax.broadcasted_iota(jnp.int32, (rows, LANES), 0).astype(F32).astype(BF16)
    one = jnp.ones((LANES, LANES), BF16)
    zero = jnp.zeros((LANES, LANES), BF16)
    zero_rows = jnp.zeros((rows, LANES), BF16)
    low = (index & 127).astype(F32)
    high = (index >> 7).astype(F32)
    parts = [p.astype(F32) for p in split_terms(terms)]
    hot_blocks = []
    weight_blocks = []
    for s in range(8):
        at = slice(s, s + 1)
        low_row = jnp.broadcast_to(low[at], (LANES, LANES)).astype(BF16)
        hot_blocks.append(jnp.where(sub == low_row, one, zero))
        mine = sub_rows == jnp.broadcast_to(high[at], (rows, LANES)).astype(BF16)
        weight_blocks.append(jnp.concatenate(
            [jnp.where(mine, jnp.broadcast_to(p[at], (rows, LANES)).astype(BF16), zero_rows) for p in parts],
            axis=0,
        ))
    total = lax.dot_general(
        jnp.concatenate(weight_blocks, axis=1), jnp.concatenate(hot_blocks, axis=1),
        (((1,), (1,)), ((), ())), preferred_element_type=F32,
    )
    out = total[0:rows]
    for k in range(1, SPLITS):
        out = out + total[k * rows:(k + 1) * rows]
    return out


def conn_block(conn_ref, a, t):
    return conn_ref[pl.ds(32 * t + a, 8, stride=4), :]


def element_gradient(ext, conn_ref, grad_ref, last_ref, t):
    corner = [gather_rows(ext, conn_block(conn_ref, a, t)) for a in range(4)]
    grads = [grad_ref[pl.ds(64 * t + c, 8, stride=8), :] for c in range(8)]
    grads.append(last_ref[pl.ds(pl.multiple_of(8 * t, 8), 8), :])
    diff = [corner[a] - corner[3] for a in range(3)]
    field = [
        grads[k] * diff[0] + grads[3 + k] * diff[1] + grads[6 + k] * diff[2]
        for k in range(3)
    ]
    return grads, field


def block_volume(vol_ref, t):
    return vol_ref[pl.ds(pl.multiple_of(t * 8, 8), 8), :]


def odd(axis):
    return lax.rem(lax.axis_index(axis), 2) == 1


def inside(axis):
    me = lax.axis_index(axis)
    return (me > 0) & (me < lax.axis_size(axis) - 1)


def from_swaps(pieces):
    row_a, row_b, col_a, col_b = [p[...] for p in pieces]
    row_b = jnp.where(inside("row"), row_b, 0.0)
    col_b = jnp.where(inside("col"), col_b, 0.0)
    row_odd = odd("row")
    col_odd = odd("col")
    return [
        jnp.where(row_odd, row_b, row_a),
        jnp.where(row_odd, row_a, row_b),
        jnp.where(col_odd, col_b, col_a),
        jnp.where(col_odd, col_a, col_b),
    ]


def put_outgoing(blocks, out_refs):
    row_odd = odd("row")
    col_odd = odd("col")
    out_refs[0][...] = jnp.where(row_odd, blocks[1], blocks[0])
    out_refs[1][...] = jnp.where(row_odd, blocks[0], blocks[1])
    out_refs[2][...] = jnp.where(col_odd, blocks[3], blocks[2])
    out_refs[3][...] = jnp.where(col_odd, blocks[2], blocks[3])


def extend(v, pieces):
    up, down, right, left = from_swaps(pieces)
    return jnp.concatenate([v, down, up, left, right], axis=0)


def picked_blocks(v, lists):
    got = gather_rows(v, lists)
    return [jnp.concatenate([got[d:d + 1], got[4 + d:5 + d]], axis=0) for d in range(4)]


def pick_kernel(v_ref, list_ref, point_ref, target_ref, *out_refs):
    put_outgoing(picked_blocks(v_ref[...], list_ref[...]), out_refs)
    lane = lax.broadcasted_iota(jnp.int32, (1, LANES), 1)
    own = jnp.zeros((1, LANES), F32)
    for c in range(3):
        part = point_ref[c:c + 1, 0:LANES]
        if c:
            part = pltpu.roll(part, TGT_DEV * c, 1)
        own = jnp.where((lane >= TGT_DEV * c) & (lane < TGT_DEV * (c + 1)), part, own)
    target_ref[...] = jnp.broadcast_to(own, (N_DEV, LANES))


def apply_kernel(live_ref, v_ref, ga, gb, gc, gd, conn_ref, grad_ref, last_ref, vol_ref,
                 own_ref, oa, ob, oc, od, ext_ref, acc_ref):
    ext_ref[...] = extend(v_ref[...], [ga, gb, gc, gd])
    acc_ref[...] = jnp.zeros_like(acc_ref)

    def element_block(t, carry):
        grads, field = element_gradient(ext_ref[...], conn_ref, grad_ref, last_ref, t)
        vol = block_volume(vol_ref, t)
        field = [vol * f for f in field]
        terms = [
            grads[3 * a] * field[0] + grads[3 * a + 1] * field[1] + grads[3 * a + 2] * field[2]
            for a in range(3)
        ]
        terms.append(-(terms[0] + terms[1] + terms[2]))
        total = acc_ref[...]
        for a in range(4):
            total = total + scatter_block(conn_block(conn_ref, a, t), terms[a], EXT_ROWS)
        acc_ref[...] = total
        return carry

    lax.fori_loop(0, live_ref[0], element_block, 0)
    own_ref[...] = acc_ref[0:OWN_ROWS, :]
    down, up, left, right = [
        acc_ref[OWN_ROWS + 2 * d:OWN_ROWS + 2 * d + 2, :] for d in range(4)
    ]
    put_outgoing([up, down, right, left], (oa, ob, oc, od))


def combine_kernel(own_ref, ra, rb, rc, rd, list_ref, v_ref, mass_ref,
                   next_ref, oa, ob, oc, od):
    lists = list_ref[...]
    back = from_swaps([ra, rb, rc, rd])
    terms = jnp.concatenate([b[0:1] for b in back] + [b[1:2] for b in back], axis=0)
    added = scatter_block(lists, terms, OWN_ROWS)
    value = (mass_ref[...] * v_ref[...] + own_ref[...] + added) * SCALE
    next_ref[...] = value
    put_outgoing(picked_blocks(value, lists), (oa, ob, oc, od))


def prepare_kernel(src_ref, tgt_ref, wide_ref, left_ref, right_ref, row_ref):
    src = src_ref[...]
    cols = jnp.transpose(src)
    for c in range(6):
        wide_ref[c] = jnp.broadcast_to(cols[0:SLOTS, c:c + 1], (SLOTS, LANES))
    lane = lax.broadcasted_iota(jnp.int32, (TGT_ROWS, LANES), 1)
    for c in range(3):
        out = jnp.zeros((TGT_ROWS, LANES), F32)
        for j in range(4):
            part = tgt_ref[pl.ds(j, TGT_ROWS, stride=4), :]
            shift = (32 * j - 32 * c) % LANES
            if shift:
                part = pltpu.roll(part, shift, 1)
            out = jnp.where((lane >= 32 * j) & (lane < 32 * j + 32), part, out)
        row_ref[c] = out

    def factors(points, scale, extra, swap):
        norm = points[0] * points[0] + points[1] * points[1] + points[2] * points[2] + extra
        ones = jnp.ones_like(norm)
        lines = []
        for p in points:
            a = [q.astype(F32) for q in split_terms(p * scale)]
            order = (0, 1, 0, 1, 2, 0) if swap else (0, 0, 1, 1, 0, 2)
            lines += [a[k] for k in order]
        norms = [q.astype(F32) for q in split_terms(norm)]
        lines += [ones] * 3 + norms if swap else norms + [ones] * 3
        return lines

    left = factors([src[c:c + 1, :] - 0.5 for c in range(3)], 1.0, 0.0, False)
    left = jnp.concatenate(left + [jnp.zeros((KDIM - 24, PAD_SLOTS), F32)], axis=0)
    left_ref[...] = jnp.transpose(left)[0:SLOTS, :].astype(BF16)
    right = factors([row_ref[c] - 0.5 for c in range(3)], -2.0, smoothing, True)
    zero = jnp.zeros((1, LANES), F32)
    for g in range(TGT_ROWS):
        block = jnp.concatenate([r[g:g + 1, :] for r in right] + [zero] * (KDIM - 24), axis=0)
        right_ref[:, g * LANES:(g + 1) * LANES] = block.astype(BF16)


def entries_kernel(chunk, wide_ref, left_ref, right_ref, row_ref, entry_ref):
    base = chunk * (TGT_ROWS // CHUNKS)

    def target_group(g, carry):
        first = base + g * GROUP
        lanes = pl.ds(pl.multiple_of(first * LANES, GROUP * LANES), GROUP * LANES)
        square = jnp.dot(left_ref[...], right_ref[:, lanes], preferred_element_type=F32)
        for s in range(SLOTS // 16):
            rows = slice(16 * s, 16 * s + 16)
            sx, sy, sz, wx, wy, wz = [wide_ref[c, rows, :] for c in range(6)]
            for q in range(GROUP):
                at = pl.ds(first + q, 1)
                inverse = lax.rsqrt(square[rows, q * LANES:(q + 1) * LANES])
                numerator = (
                    (row_ref[0, at, :] - sx) * wx
                    + (row_ref[1, at, :] - sy) * wy
                    + (row_ref[2, at, :] - sz) * wz
                )
                value = (numerator * (inverse * inverse * inverse)).astype(BF16)
                out = pl.ds(pl.multiple_of((g * GROUP + q) * LANES, LANES), LANES)
                entry_ref[rows, out] = value
        return carry

    lax.fori_loop(0, TGT_ROWS // CHUNKS // GROUP, target_group, 0)


def far_kernel(live_ref, b_ref, v1_ref, v2_ref, ga, gb, gc, gd, conn_ref, grad_ref, last_ref, vol_ref,
               mass_ref, node_ref, e0, e1, e2, e3,
               out_ref, trace_ref, ext_ref, d0, d1, d2, lhs_ref):
    b = b_ref[...]
    v1 = v1_ref[...]
    v2 = v2_ref[...]
    ext_ref[...] = extend(v2, [ga, gb, gc, gd])

    def energy_block(t, total):
        _, field = element_gradient(ext_ref[...], conn_ref, grad_ref, last_ref, t)
        return total + block_volume(vol_ref, t) * (
            field[0] * field[0] + field[1] * field[1] + field[2] * field[2]
        )

    energy = lax.fori_loop(0, live_ref[0], energy_block, jnp.zeros((8, LANES), F32))
    products = [b * b, b * v1, v1 * v1, v1 * v2, v2 * v2, mass_ref[...] * v2 * v2]
    sums = [p[0:8] + p[8:16] for p in products]
    sums[5] = (sums[5] + energy) * SCALE
    sub = lax.broadcasted_iota(jnp.int32, (8, LANES), 0)
    lane_row = lax.broadcasted_iota(jnp.int32, (1, LANES), 1)
    moments = jnp.zeros((1, LANES), F32)
    for k in range(6):
        moments = jnp.where(lane_row == 96 + k, jnp.sum(sums[k]), moments)

    nodes = node_ref[...]
    traces = [gather_rows(table, nodes) for table in (b, v1, v2)]
    for k in range(3):
        trace_ref[k] = traces[k]
    for r in range(PAD_SLOTS // LANES):
        block = jnp.zeros((8, LANES), F32)
        for k in range(3):
            t = traces[k][r:r + 1, :]
            high = t.astype(BF16).astype(F32)
            block = jnp.where(sub == 2 * k, high, block)
            block = jnp.where(sub == 2 * k + 1, t - high, block)
        lhs_ref[:, r * LANES:(r + 1) * LANES] = block.astype(BF16)
    lhs = lhs_ref[:, 0:SLOTS]
    each = TGT_ROWS // CHUNKS
    for chunk, entry_ref in enumerate((e0, e1, e2, e3)):
        res = jnp.dot(lhs, entry_ref[...], preferred_element_type=F32)
        for q in range(each):
            at = slice(chunk * each + q, chunk * each + q + 1)
            part = res[:, q * LANES:(q + 1) * LANES]
            d0[at, :] = part[0:1] + part[1:2]
            d1[at, :] = part[2:3] + part[3:4]
            d2[at, :] = part[4:5] + part[5:6]

    lane = lax.broadcasted_iota(jnp.int32, (TGT_ROWS, LANES), 1)
    spread = jnp.broadcast_to(moments, (TGT_ROWS, LANES))
    for j in range(4):
        out = spread
        for k, ref in enumerate((d0, d1, d2)):
            part = ref[...]
            shift = (32 * k - 32 * j) % LANES
            if shift:
                part = pltpu.roll(part, shift, 1)
            out = jnp.where((lane >= 32 * k) & (lane < 32 * k + 32), part, out)
        out_ref[pl.ds(j, TGT_ROWS, stride=4), :] = out


def final_kernel(got_ref, b_ref, v1_ref, v2_ref, trace_ref, pot_ref, dir_ref):
    total = jnp.sum(got_ref[...], axis=0, keepdims=True)
    lane = lax.broadcasted_iota(jnp.int32, (1, LANES), 1)
    m = [jnp.sum(jnp.where(lane == 96 + k, total, 0.0), axis=1, keepdims=True) for k in range(6)]
    l1 = m[2] / m[1]
    l2 = m[3] / m[1]
    s11 = m[3] - l1 * m[2]
    s12 = m[4] - l1 * m[3]
    s22 = m[5] - l2 * m[3]
    y1 = m[1] - l1 * m[0]
    y2 = m[2] - l2 * m[0]
    keep1 = s11 > 4e-7 * m[3]
    safe11 = jnp.where(keep1, s11, 1.0)
    ratio = jnp.where(keep1, s12 / safe11, 0.0)
    d2 = s22 - ratio * s12
    keep2 = keep1 & (d2 > 4e-7 * m[5])
    c2 = jnp.where(keep2, (y2 - ratio * y1) / jnp.where(keep2, d2, 1.0), 0.0)
    c1 = jnp.where(keep1, (y1 - s12 * c2) / safe11, 0.0)
    c0 = (m[0] - m[2] * c1 - m[3] * c2) / m[1]
    c0 = c0 * SCALE
    c1 = c1 * SCALE
    c2 = c2 * SCALE
    pot_ref[...] = c0 * b_ref[...] + c1 * v1_ref[...] + c2 * v2_ref[...]
    out = jnp.zeros((1, LANES), F32)
    for k, c in enumerate((c0, c1, c2)):
        part = total
        if k:
            part = pltpu.roll(total, LANES - 32 * k, 1)
        out = out + c * (part - 0.5 * trace_ref[k, 0:1, :])
    dir_ref[...] = out[:, 0:TGT_DEV]


def call(body, out_shapes, args, smem=0, scratch=(), cost=2000000):
    specs = [pl.BlockSpec(memory_space=pltpu.SMEM)] * smem
    specs += [pl.BlockSpec(memory_space=pltpu.VMEM)] * (len(args) - smem)
    out_shapes = [o if isinstance(o, jax.ShapeDtypeStruct) else jax.ShapeDtypeStruct(o, F32) for o in out_shapes]
    return pl.pallas_call(
        body,
        out_shape=out_shapes,
        in_specs=specs,
        out_specs=[pl.BlockSpec(memory_space=pltpu.VMEM)] * len(out_shapes),
        scratch_shapes=list(scratch),
        compiler_params=pltpu.CompilerParams(vmem_limit_bytes=VMEM_GRANT),
        cost_estimate=pl.CostEstimate(flops=cost, bytes_accessed=1 << 20, transcendentals=0),
    )(*args)


PIECE = (2, LANES)


def first_pairs(count):
    return [(i, i ^ 1) for i in range(count)]


def second_pairs(count):
    return [(i, (((i + 1) ^ 1) - 1) % count) for i in range(count)]


def exchange(pieces):
    rows = lax.axis_size("row")
    cols = lax.axis_size("col")
    row_a = lax.ppermute(pieces[0], "row", first_pairs(rows))
    col_a = lax.ppermute(pieces[2], "col", first_pairs(cols))
    row_b = lax.ppermute(pieces[1], "row", second_pairs(rows))
    col_b = lax.ppermute(pieces[3], "col", second_pairs(cols))
    return [row_a, row_b, col_a, col_b]


def per_device(connectivity, gradients, volumes, live_blocks, send_lists, divergence, mass_shift,
               boundary_nodes, surface_points, normal_cos, normal_angle, node_areas):
    conn = connectivity.reshape(4, ELEM_ROWS, LANES).transpose(1, 0, 2).reshape(4 * ELEM_ROWS, LANES)
    grads = gradients[0:8].reshape(8, ELEM_ROWS, LANES).transpose(1, 0, 2).reshape(8 * ELEM_ROWS, LANES)
    last = gradients[8].reshape(ELEM_ROWS, LANES)
    vol = volumes.reshape(ELEM_ROWS, LANES)
    lists = send_lists.reshape(4, 2, LANES).transpose(1, 0, 2).reshape(8, LANES)
    b = divergence.reshape(OWN_ROWS, LANES)
    mass = mass_shift.reshape(OWN_ROWS, LANES)
    nodes = jnp.pad(boundary_nodes, (0, 8 * LANES - SLOTS)).reshape(8, LANES)
    elements = (conn, grads, last, vol)

    mine, *pieces = call(pick_kernel, [(N_DEV, LANES)] + [PIECE] * 4, (b, lists, surface_points))
    targets = lax.all_to_all(mine, ("row", "col"), 0, 0, tiled=True)
    sine = jnp.sqrt(1.0 - normal_cos * normal_cos)
    normals = jnp.stack([sine * jnp.cos(normal_angle), sine * jnp.sin(normal_angle), normal_cos])
    weighted = (node_areas * inverse_four_pi)[None, :] * normals
    sources = jnp.pad(
        jnp.concatenate([surface_points, weighted], axis=0), ((0, 2), (0, PAD_SLOTS - SLOTS))
    )
    prepared = None
    chunks = []

    def fill():
        nonlocal prepared
        if prepared is None:
            prepared = call(
                prepare_kernel,
                [
                    (6, SLOTS, LANES),
                    jax.ShapeDtypeStruct((SLOTS, KDIM), BF16),
                    jax.ShapeDtypeStruct((KDIM, TGT_ROWS * LANES), BF16),
                    (3, TGT_ROWS, LANES),
                ],
                (sources, targets),
            )
        chunk = len(chunks)
        chunks.append(call(
            lambda *refs: entries_kernel(chunk, *refs),
            [jax.ShapeDtypeStruct((SLOTS, TGT_ROWS // CHUNKS * LANES), BF16)],
            prepared,
        )[0])

    def swap(number, pieces):
        out = exchange(pieces)
        if number:
            fill()
        return out

    vectors = [b]
    for step in range(2):
        ghosts = swap(2 * step, pieces)
        own, *back = call(
            apply_kernel, [(OWN_ROWS, LANES)] + [PIECE] * 4,
            (live_blocks, vectors[-1], *ghosts, *elements), smem=1,
            scratch=[pltpu.VMEM((EXT_ROWS, LANES), F32), pltpu.VMEM((HIGH_ROWS, LANES), F32)],
        )
        returned = swap(2 * step + 1, back)
        new, *pieces = call(
            combine_kernel, [(OWN_ROWS, LANES)] + [PIECE] * 4,
            (own, *returned, lists, vectors[-1], mass),
        )
        vectors.append(new)
    ghosts = swap(4, pieces)
    partial, trace = call(
        far_kernel, [(N_DEV, LANES), (3, 8, LANES)],
        (live_blocks, *vectors, *ghosts, *elements, mass, nodes, *chunks), smem=1,
        scratch=[pltpu.VMEM((EXT_ROWS, LANES), F32)]
        + [pltpu.VMEM((TGT_ROWS, LANES), F32)] * 3
        + [pltpu.VMEM((8, PAD_SLOTS), BF16)],
    )
    got = lax.all_to_all(partial, ("row", "col"), 0, 0, tiled=True)
    potential, dirichlet = call(
        final_kernel, [(OWN_ROWS, LANES), (1, TGT_DEV)], (got, *vectors, trace)
    )
    return potential.reshape(NN_DEV), dirichlet.reshape(TGT_DEV)


def solution(mesh):
    both = ("row", "col")

    return jax.shard_map(
        per_device,
        mesh=mesh,
        in_specs=(
            P(None, both), P(None, both), P(both), P(both), P(None, both), P(both),
            P(both), P(both), P(None, both), P(both), P(both), P(both),
        ),
        out_specs=(P(both), P(both)),
        check_vma=False,
    )
```

time: 118 us -> 102 us (0.86)
  blocking collectives: 30.9 us -> 19.6 us
  starting transfers between devices: 57.4 us -> 53 us
  Pallas kernels: 19.4 us -> 15.2 us
  local copies, waits for them, and re-layouts: 3.46 us -> 7.12 us
  other arithmetic: 0.15 us -> 1.45 us
    all_to_all x1, blocking collectives: 30.9 us -> 19.6 us  [per_device(): got = lax.all_to_all(partial, ('row', 'col'), 0, 0, tiled=True)]
    all_to_all x1, starting transfers between devices: 14.9 us -> 7.32 us  [per_device(): targets = lax.all_to_all(mine, ('row', 'col'), 0, 0, tiled=True)]
    pallas_call x7 -> x12, Pallas kernels: 19.4 us -> 15.2 us  [call(): pl.pallas_call(body, out_shape=out_shapes, in_specs=specs, out_specs=[pl....]
    ppermute x20, starting transfers between devices: 42.5 us -> 45.7 us  [the longest x5 31 us: exchange(): col_b = lax.ppermute(pieces[3], 'col', second_pairs(cols))]
    unnamed x22 -> x26, local copies, waits for them, and re-layouts: 3.41 us -> 4.49 us
  transfers between devices with their start and end apart: 21 -> 21, of which waited for: 5 -> 3; matrix products, arithmetic and copies ran while one was open for 1% -> 4% of each run, Pallas kernels for 5% -> 12%
where the time goes in v3:
time: 102 us; the launch traced here: 101 us
  starting transfers between devices  53 us (52%)
  blocking collectives  19.6 us (19%)
  Pallas kernels  15.2 us (15%)
  local copies, waits for them, and re-layouts  7.12 us (7%)
  waiting for transfers between devices  3.13 us (3%)
  between operations  1.62 us (2%)
  other arithmetic  1.45 us (1%)
    ppermute x5, starting transfers between devices, exchange(): col_b = lax.ppermute(pieces[3], 'col', second_pairs(cols))  31 us
    all_to_all x1, blocking collectives, per_device(): got = lax.all_to_all(partial, ('row', 'col'), 0, 0, tiled=True)  19.6 us
    pallas_call x12, Pallas kernels, call(): pl.pallas_call(body, out_shape=out_shapes, in_specs=specs, out_specs=[pl....  15.2 us
    ppermute x5, starting transfers between devices, exchange(): row_a = lax.ppermute(pieces[0], 'row', first_pairs(rows))  10.7 us
    all_to_all x1, starting transfers between devices, per_device(): targets = lax.all_to_all(mine, ('row', 'col'), 0, 0, tiled=True)  7.32 us
    unnamed x26, local copies, waits for them, and re-layouts  4.49 us
    ppermute x5, starting transfers between devices, exchange(): row_b = lax.ppermute(pieces[1], 'row', second_pairs(rows))  2.85 us
  transfers between devices with their start and end apart: 21, of which 3 were waited for; matrix products, arithmetic and copies ran while one was open for 4% of the time, Pallas kernels for 12%

profile of v3, /device:TPU:1, one launch (start us, length us, event | category | flops | bytes accessed | tf_op | source)
XLA Modules:
  0.0 101.1 jit_solution(7633075354021330085)
XLA Ops:
  3.5 3.2 %collective-permute-start = (f32[2,128]{1,0:T(2,128)S(1)}, f32[2,128]{1,0:T(2,128)S(1)}, u32[]{:S(2)}, u32[]{:S(2)}) collective-permute-start(f32[2,128]{1,0:T(2,128)S(1)} %get-tuple-element.35), channel_id=1, source_target_pairs={{0,32},{32,0},{64,96},{96,64},{128,160},{160,128},{192,224},{224,1... | collective-permute-start | bytes 3080 | tf_op jit(solution)/shard_map/ppermute | solution.py:382
  6.7 1.0 %collective-permute-start.2 = (f32[2,128]{1,0:T(2,128)S(1)}, f32[2,128]{1,0:T(2,128)S(1)}, u32[]{:S(2)}, u32[]{:S(2)}) collective-permute-start(f32[2,128]{1,0:T(2,128)S(1)} %get-tuple-element.37), channel_id=1, source_target_pairs={{0,1},{1,0},{2,3},{3,2},{4,5},{5,4},{6,7},{7,6},{8,9},{9,8},{10,11... | collective-permute-start | bytes 3080 | tf_op jit(solution)/shard_map/ppermute | solution.py:383
  7.7 7.1 %collective-permute-start.3 = (f32[2,128]{1,0:T(2,128)S(1)}, f32[2,128]{1,0:T(2,128)S(1)}, u32[]{:S(2)}, u32[]{:S(2)}) collective-permute-start(f32[2,128]{1,0:T(2,128)S(1)} %get-tuple-element.38), channel_id=1, source_target_pairs={{0,31},{1,2},{2,1},{3,4},{4,3},{5,6},{6,5},{7,8},{8,7},{9,10},{10,... | collective-permute-start | bytes 3080 | tf_op jit(solution)/shard_map/ppermute | solution.py:385
  14.9 7.3 %all-to-all-start = ((f32[256,1,128]{2,1,0:T(1,128)}), f32[256,1,128]{2,1,0:T(1,128)S(1)}, u32[]{:S(2)}, u32[]{:S(2)}) async-start(f32[256,1,128]{2,1,0:T(1,128)} %bitcast.21), calls=%async_computation | async-start | bytes 262144 | tf_op jit(solution)/shard_map/all_to_all | solution.py:402
  22.2 1.0 slice_bitcast_fusion.grad_ref
  24.6 1.0 slice.7
  29.3 2.4 %shard_map.132 = (f32[16,128]{1,0:T(8,128)S(1)}, f32[2,128]{1,0:T(2,128)S(1)}, f32[2,128]{1,0:T(2,128)S(1)}, f32[2,128]{1,0:T(2,128)S(1)}, f32[2,128]{1,0:T(2,128)S(1)}) custom-call(s32[1]{0:T(128)S(6)} %copy.20.live_ref, f32[16,128]{1,0:T(8,128)S(1)} %bitcast.44, f32[2,128]{1,0:T(2,128)S(1)} %collective-permute-done.ga, ...), custom_call_target="tpu_custom_call" | custom-call | flops 2000000 | bytes 1048576 | tf_op jit(solution)/shard_map/pallas_call | solution.py:357
  31.7 3.2 %collective-permute-start.4 = (f32[2,128]{1,0:T(2,128)S(1)}, f32[2,128]{1,0:T(2,128)S(1)}, u32[]{:S(2)}, u32[]{:S(2)}) collective-permute-start(f32[2,128]{1,0:T(2,128)S(1)} %get-tuple-element.40), channel_id=1, source_target_pairs={{0,32},{32,0},{64,96},{96,64},{128,160},{160,128},{192,224},{224,1... | collective-permute-start | bytes 3080 | tf_op jit(solution)/shard_map/ppermute | solution.py:382
  34.9 10.1 %collective-permute-start.7 = (f32[2,128]{1,0:T(2,128)S(1)}, f32[2,128]{1,0:T(2,128)S(1)}, u32[]{:S(2)}, u32[]{:S(2)}) collective-permute-start(f32[2,128]{1,0:T(2,128)S(1)} %get-tuple-element.43), channel_id=1, source_target_pairs={{0,31},{1,2},{2,1},{3,4},{4,3},{5,6},{6,5},{7,8},{8,7},{9,10},{10,... | collective-permute-start | bytes 3080 | tf_op jit(solution)/shard_map/ppermute | solution.py:385
  46.4 4.9 %collective-permute-start.11 = (f32[2,128]{1,0:T(2,128)S(1)}, f32[2,128]{1,0:T(2,128)S(1)}, u32[]{:S(2)}, u32[]{:S(2)}) collective-permute-start(f32[2,128]{1,0:T(2,128)S(1)} %get-tuple-element.48), channel_id=1, source_target_pairs={{0,31},{1,2},{2,1},{3,4},{4,3},{5,6},{6,5},{7,8},{8,7},{9,10},{10,... | collective-permute-start | bytes 3080 | tf_op jit(solution)/shard_map/ppermute | solution.py:385
  51.3 1.7 %collective-permute-start.9 = (f32[2,128]{1,0:T(2,128)S(1)}, f32[2,128]{1,0:T(2,128)S(1)}, u32[]{:S(2)}, u32[]{:S(2)}) collective-permute-start(f32[2,128]{1,0:T(2,128)S(1)} %get-tuple-element.46), channel_id=1, source_target_pairs={{0,224},{32,64},{64,32},{96,128},{128,96},{160,192},{192,160},{224... | collective-permute-start | bytes 3080 | tf_op jit(solution)/shard_map/ppermute | solution.py:384
  53.0 1.2 %collective-permute-done.9.gb = f32[2,128]{1,0:T(2,128)S(1)} collective-permute-done((f32[2,128]{1,0:T(2,128)S(1)}, f32[2,128]{1,0:T(2,128)S(1)}, u32[]{:S(2)}, u32[]{:S(2)}) %collective-permute-start.9) | collective-permute-done | bytes 1056 | tf_op jit(solution)/shard_map/ppermute | solution.py:384
  54.3 2.4 %shard_map.134 = (f32[16,128]{1,0:T(8,128)S(1)}, f32[2,128]{1,0:T(2,128)S(1)}, f32[2,128]{1,0:T(2,128)S(1)}, f32[2,128]{1,0:T(2,128)S(1)}, f32[2,128]{1,0:T(2,128)S(1)}) custom-call(s32[1]{0:T(128)S(6)} %copy.20.live_ref, f32[16,128]{1,0:T(8,128)S(1)} %get-tuple-element.44.v_ref.v1_ref, f32[2,128]{1,0:T(2,128)S(1)} %collective-permute-done.8.ga, ...), custom_call_target="tpu_custom_call" | custom-call | flops 2000000 | bytes 1048576 | tf_op jit(solution)/shard_map/pallas_call | solution.py:357
  56.7 2.6 %collective-permute-start.12 = (f32[2,128]{1,0:T(2,128)S(1)}, f32[2,128]{1,0:T(2,128)S(1)}, u32[]{:S(2)}, u32[]{:S(2)}) collective-permute-start(f32[2,128]{1,0:T(2,128)S(1)} %get-tuple-element.50), channel_id=1, source_target_pairs={{0,32},{32,0},{64,96},{96,64},{128,160},{160,128},{192,224},{224,1... | collective-permute-start | bytes 3080 | tf_op jit(solution)/shard_map/ppermute | solution.py:382
  59.3 5.2 %collective-permute-start.15 = (f32[2,128]{1,0:T(2,128)S(1)}, f32[2,128]{1,0:T(2,128)S(1)}, u32[]{:S(2)}, u32[]{:S(2)}) collective-permute-start(f32[2,128]{1,0:T(2,128)S(1)} %get-tuple-element.53), channel_id=1, source_target_pairs={{0,31},{1,2},{2,1},{3,4},{4,3},{5,6},{6,5},{7,8},{8,7},{9,10},{10,... | collective-permute-start | bytes 3080 | tf_op jit(solution)/shard_map/ppermute | solution.py:385
  65.7 1.7 %collective-permute-start.16 = (f32[2,128]{1,0:T(2,128)S(1)}, f32[2,128]{1,0:T(2,128)S(1)}, u32[]{:S(2)}, u32[]{:S(2)}) collective-permute-start(f32[2,128]{1,0:T(2,128)S(1)} %get-tuple-element.55), channel_id=1, source_target_pairs={{0,32},{32,0},{64,96},{96,64},{128,160},{160,128},{192,224},{224,1... | collective-permute-start | bytes 3080 | tf_op jit(solution)/shard_map/ppermute | solution.py:382
  67.4 1.1 %collective-permute-start.17 = (f32[2,128]{1,0:T(2,128)S(1)}, f32[2,128]{1,0:T(2,128)S(1)}, u32[]{:S(2)}, u32[]{:S(2)}) collective-permute-start(f32[2,128]{1,0:T(2,128)S(1)} %get-tuple-element.56), channel_id=1, source_target_pairs={{0,224},{32,64},{64,32},{96,128},{128,96},{160,192},{192,160},{224... | collective-permute-start | bytes 3080 | tf_op jit(solution)/shard_map/ppermute | solution.py:384
  68.6 3.7 %collective-permute-start.19 = (f32[2,128]{1,0:T(2,128)S(1)}, f32[2,128]{1,0:T(2,128)S(1)}, u32[]{:S(2)}, u32[]{:S(2)}) collective-permute-start(f32[2,128]{1,0:T(2,128)S(1)} %get-tuple-element.58), channel_id=1, source_target_pairs={{0,31},{1,2},{2,1},{3,4},{4,3},{5,6},{6,5},{7,8},{8,7},{9,10},{10,... | collective-permute-start | bytes 3080 | tf_op jit(solution)/shard_map/ppermute | solution.py:385
  73.2 1.4 %shard_map.140.e3 = bf16[320,2048]{1,0:T(8,128)(2,1)S(1)} custom-call(f32[6,320,128]{2,1,0:T(8,128)S(1)} %get-tuple-element.60.refs_0_, bf16[320,32]{1,0:T(8,128)(2,1)S(1)} %get-tuple-element.61.refs_1_, bf16[32,8192]{1,0:T(8,128)(2,1)S(1)} %get-tuple-element.62.refs_2_, f32[3,64,128]{2,1,0:T(8,128)S(1)} %get-tuple-element.63.refs_3_), custom_call_target="tpu_custom_call" | custom-call | flops 2000000 | bytes 1048576 | tf_op jit(solution)/shard_map/pallas_call | solution.py:357
  74.6 1.5 %shard_map.139.e2 = bf16[320,2048]{1,0:T(8,128)(2,1)S(1)} custom-call(f32[6,320,128]{2,1,0:T(8,128)S(1)} %get-tuple-element.60.refs_0_, bf16[320,32]{1,0:T(8,128)(2,1)S(1)} %get-tuple-element.61.refs_1_, bf16[32,8192]{1,0:T(8,128)(2,1)S(1)} %get-tuple-element.62.refs_2_, f32[3,64,128]{2,1,0:T(8,128)S(1)} %get-tuple-element.63.refs_3_), custom_call_target="tpu_custom_call" | custom-call | flops 2000000 | bytes 1048576 | tf_op jit(solution)/shard_map/pallas_call | solution.py:357
  76.1 1.4 %shard_map.138.e1 = bf16[320,2048]{1,0:T(8,128)(2,1)S(1)} custom-call(f32[6,320,128]{2,1,0:T(8,128)S(1)} %get-tuple-element.60.refs_0_, bf16[320,32]{1,0:T(8,128)(2,1)S(1)} %get-tuple-element.61.refs_1_, bf16[32,8192]{1,0:T(8,128)(2,1)S(1)} %get-tuple-element.62.refs_2_, f32[3,64,128]{2,1,0:T(8,128)S(1)} %get-tuple-element.63.refs_3_), custom_call_target="tpu_custom_call" | custom-call | flops 2000000 | bytes 1048576 | tf_op jit(solution)/shard_map/pallas_call | solution.py:357
  77.6 1.5 %shard_map.137.e0 = bf16[320,2048]{1,0:T(8,128)(2,1)S(1)} custom-call(f32[6,320,128]{2,1,0:T(8,128)S(1)} %get-tuple-element.60.refs_0_, bf16[320,32]{1,0:T(8,128)(2,1)S(1)} %get-tuple-element.61.refs_1_, bf16[32,8192]{1,0:T(8,128)(2,1)S(1)} %get-tuple-element.62.refs_2_, f32[3,64,128]{2,1,0:T(8,128)S(1)} %get-tuple-element.63.refs_3_), custom_call_target="tpu_custom_call" | custom-call | flops 2000000 | bytes 1048576 | tf_op jit(solution)/shard_map/pallas_call | solution.py:357
  79.1 1.7 %shard_map.141 = (f32[256,128]{1,0:T(8,128)S(1)}, f32[3,8,128]{2,1,0:T(8,128)S(1)}) custom-call(s32[1]{0:T(128)S(6)} %copy.20.live_ref, f32[16,128]{1,0:T(8,128)S(1)} %bitcast.46, f32[16,128]{1,0:T(8,128)S(1)} %get-tuple-element.44.v_ref.v1_ref, f32[16,128]{1,0:T(8,128)S(1)} %get-tuple-element.54.v2_ref, f32[2,128]{1,0:T(2,128)S(1)} %collective-permute-done.16.ga, ...), custom_call_target="tpu_custom_call" | custom-call | flops 2000000 | bytes 1048576 | tf_op jit(solution)/shard_map/pallas_call | solution.py:357
  80.8 19.6 %all_to_all.22 = f32[256,1,128]{2,1,0:T(1,128)S(1)} all-to-all(f32[256,1,128]{2,1,0:T(1,128)S(1)} %bitcast.48), channel_id=1, replica_groups=mesh['row'=8,'col'=32] {'row','col'}, dimensions={0} | all-to-all | bytes 262144 | tf_op jit(solution)/shard_map/all_to_all | solution.py:460
  (67 shorter events, 11.6 us)
Async XLA Ops:
  0.6 53.6 %copy-start.1 = (s32[4,8192]{1,0:T(4,128)S(1)}, s32[4,8192]{1,0:T(4,128)}, u32[]{:S(2)}) copy-start(s32[4,8192]{1,0:T(4,128)} %param.12) | copy-start | bytes 393220
  2.8 50.2 %copy-start.11 = (f32[3,320]{1,0:T(4,128)S(1)}, f32[3,320]{1,0:T(4,128)}, u32[]{:S(2)}) copy-start(f32[3,320]{1,0:T(4,128)} %point_ref.1) | copy-start | bytes 11524
  2.8 61.7 %copy-start.12 = (s32[320]{0:T(512)S(1)}, s32[320]{0:T(512)}, u32[]{:S(2)}) copy-start(s32[320]{0:T(512)} %param.19) | copy-start | bytes 3844
  3.5 23.4 %collective-permute-start = (f32[2,128]{1,0:T(2,128)S(1)}, f32[2,128]{1,0:T(2,128)S(1)}, u32[]{:S(2)}, u32[]{:S(2)}) collective-permute-start(f32[2,128]{1,0:T(2,128)S(1)} %get-tuple-element.35), channel_id=1, source_target_pairs={{0,32},{32,0},{64,96},{96,64},{128,160},{160,128},{192,224},{224,1... | collective-permute-start | bytes 3080 | tf_op jit(solution)/shard_map/ppermute | solution.py:382
  6.7 20.2 %collective-permute-start.1 = (f32[2,128]{1,0:T(2,128)S(1)}, f32[2,128]{1,0:T(2,128)S(1)}, u32[]{:S(2)}, u32[]{:S(2)}) collective-permute-start(f32[2,128]{1,0:T(2,128)S(1)} %get-tuple-element.36), channel_id=1, source_target_pairs={{0,224},{32,64},{64,32},{96,128},{128,96},{160,192},{192,160},{224... | collective-permute-start | bytes 3080 | tf_op jit(solution)/shard_map/ppermute | solution.py:384
  6.7 20.2 %collective-permute-start.2 = (f32[2,128]{1,0:T(2,128)S(1)}, f32[2,128]{1,0:T(2,128)S(1)}, u32[]{:S(2)}, u32[]{:S(2)}) collective-permute-start(f32[2,128]{1,0:T(2,128)S(1)} %get-tuple-element.37), channel_id=1, source_target_pairs={{0,1},{1,0},{2,3},{3,2},{4,5},{5,4},{6,7},{7,6},{8,9},{9,8},{10,11... | collective-permute-start | bytes 3080 | tf_op jit(solution)/shard_map/ppermute | solution.py:383
  7.7 19.2 %collective-permute-start.3 = (f32[2,128]{1,0:T(2,128)S(1)}, f32[2,128]{1,0:T(2,128)S(1)}, u32[]{:S(2)}, u32[]{:S(2)}) collective-permute-start(f32[2,128]{1,0:T(2,128)S(1)} %get-tuple-element.38), channel_id=1, source_target_pairs={{0,31},{1,2},{2,1},{3,4},{4,3},{5,6},{6,5},{7,8},{8,7},{9,10},{10,... | collective-permute-start | bytes 3080 | tf_op jit(solution)/shard_map/ppermute | solution.py:385
  14.9 57.4 %all-to-all-start = ((f32[256,1,128]{2,1,0:T(1,128)}), f32[256,1,128]{2,1,0:T(1,128)S(1)}, u32[]{:S(2)}, u32[]{:S(2)}) async-start(f32[256,1,128]{2,1,0:T(1,128)} %bitcast.21), calls=%async_computation | async-start | bytes 262144 | tf_op jit(solution)/shard_map/all_to_all | solution.py:402
  31.7 13.3 %collective-permute-start.4 = (f32[2,128]{1,0:T(2,128)S(1)}, f32[2,128]{1,0:T(2,128)S(1)}, u32[]{:S(2)}, u32[]{:S(2)}) collective-permute-start(f32[2,128]{1,0:T(2,128)S(1)} %get-tuple-element.40), channel_id=1, source_target_pairs={{0,32},{32,0},{64,96},{96,64},{128,160},{160,128},{192,224},{224,1... | collective-permute-start | bytes 3080 | tf_op jit(solution)/shard_map/ppermute | solution.py:382
  34.9 10.2 %collective-permute-start.5 = (f32[2,128]{1,0:T(2,128)S(1)}, f32[2,128]{1,0:T(2,128)S(1)}, u32[]{:S(2)}, u32[]{:S(2)}) collective-permute-start(f32[2,128]{1,0:T(2,128)S(1)} %get-tuple-element.41), channel_id=1, source_target_pairs={{0,224},{32,64},{64,32},{96,128},{128,96},{160,192},{192,160},{224... | collective-permute-start | bytes 3080 | tf_op jit(solution)/shard_map/ppermute | solution.py:384
  34.9 10.2 %collective-permute-start.6 = (f32[2,128]{1,0:T(2,128)S(1)}, f32[2,128]{1,0:T(2,128)S(1)}, u32[]{:S(2)}, u32[]{:S(2)}) collective-permute-start(f32[2,128]{1,0:T(2,128)S(1)} %get-tuple-element.42), channel_id=1, source_target_pairs={{0,1},{1,0},{2,3},{3,2},{4,5},{5,4},{6,7},{7,6},{8,9},{9,8},{10,11... | collective-permute-start | bytes 3080 | tf_op jit(solution)/shard_map/ppermute | solution.py:383
  34.9 11.1 %collective-permute-start.7 = (f32[2,128]{1,0:T(2,128)S(1)}, f32[2,128]{1,0:T(2,128)S(1)}, u32[]{:S(2)}, u32[]{:S(2)}) collective-permute-start(f32[2,128]{1,0:T(2,128)S(1)} %get-tuple-element.43), channel_id=1, source_target_pairs={{0,31},{1,2},{2,1},{3,4},{4,3},{5,6},{6,5},{7,8},{8,7},{9,10},{10,... | collective-permute-start | bytes 3080 | tf_op jit(solution)/shard_map/ppermute | solution.py:385
  46.3 6.7 %collective-permute-start.10 = (f32[2,128]{1,0:T(2,128)S(1)}, f32[2,128]{1,0:T(2,128)S(1)}, u32[]{:S(2)}, u32[]{:S(2)}) collective-permute-start(f32[2,128]{1,0:T(2,128)S(1)} %get-tuple-element.47), channel_id=1, source_target_pairs={{0,1},{1,0},{2,3},{3,2},{4,5},{5,4},{6,7},{7,6},{8,9},{9,8},{10,11... | collective-permute-start | bytes 3080 | tf_op jit(solution)/shard_map/ppermute | solution.py:383
  46.4 6.6 %collective-permute-start.11 = (f32[2,128]{1,0:T(2,128)S(1)}, f32[2,128]{1,0:T(2,128)S(1)}, u32[]{:S(2)}, u32[]{:S(2)}) collective-permute-start(f32[2,128]{1,0:T(2,128)S(1)} %get-tuple-element.48), channel_id=1, source_target_pairs={{0,31},{1,2},{2,1},{3,4},{4,3},{5,6},{6,5},{7,8},{8,7},{9,10},{10,... | collective-permute-start | bytes 3080 | tf_op jit(solution)/shard_map/ppermute | solution.py:385
  51.3 1.8 %collective-permute-start.8 = (f32[2,128]{1,0:T(2,128)S(1)}, f32[2,128]{1,0:T(2,128)S(1)}, u32[]{:S(2)}, u32[]{:S(2)}) collective-permute-start(f32[2,128]{1,0:T(2,128)S(1)} %get-tuple-element.45), channel_id=1, source_target_pairs={{0,32},{32,0},{64,96},{96,64},{128,160},{160,128},{192,224},{224,1... | collective-permute-start | bytes 3080 | tf_op jit(solution)/shard_map/ppermute | solution.py:382
  51.3 3.0 %collective-permute-start.9 = (f32[2,128]{1,0:T(2,128)S(1)}, f32[2,128]{1,0:T(2,128)S(1)}, u32[]{:S(2)}, u32[]{:S(2)}) collective-permute-start(f32[2,128]{1,0:T(2,128)S(1)} %get-tuple-element.46), channel_id=1, source_target_pairs={{0,224},{32,64},{64,32},{96,128},{128,96},{160,192},{192,160},{224... | collective-permute-start | bytes 3080 | tf_op jit(solution)/shard_map/ppermute | solution.py:384
  56.7 7.8 %collective-permute-start.12 = (f32[2,128]{1,0:T(2,128)S(1)}, f32[2,128]{1,0:T(2,128)S(1)}, u32[]{:S(2)}, u32[]{:S(2)}) collective-permute-start(f32[2,128]{1,0:T(2,128)S(1)} %get-tuple-element.50), channel_id=1, source_target_pairs={{0,32},{32,0},{64,96},{96,64},{128,160},{160,128},{192,224},{224,1... | collective-permute-start | bytes 3080 | tf_op jit(solution)/shard_map/ppermute | solution.py:382
  59.3 5.2 %collective-permute-start.13 = (f32[2,128]{1,0:T(2,128)S(1)}, f32[2,128]{1,0:T(2,128)S(1)}, u32[]{:S(2)}, u32[]{:S(2)}) collective-permute-start(f32[2,128]{1,0:T(2,128)S(1)} %get-tuple-element.51), channel_id=1, source_target_pairs={{0,224},{32,64},{64,32},{96,128},{128,96},{160,192},{192,160},{224... | collective-permute-start | bytes 3080 | tf_op jit(solution)/shard_map/ppermute | solution.py:384
  59.3 5.2 %collective-permute-start.14 = (f32[2,128]{1,0:T(2,128)S(1)}, f32[2,128]{1,0:T(2,128)S(1)}, u32[]{:S(2)}, u32[]{:S(2)}) collective-permute-start(f32[2,128]{1,0:T(2,128)S(1)} %get-tuple-element.52), channel_id=1, source_target_pairs={{0,1},{1,0},{2,3},{3,2},{4,5},{5,4},{6,7},{7,6},{8,9},{9,8},{10,11... | collective-permute-start | bytes 3080 | tf_op jit(solution)/shard_map/ppermute | solution.py:383
  59.3 6.2 %collective-permute-start.15 = (f32[2,128]{1,0:T(2,128)S(1)}, f32[2,128]{1,0:T(2,128)S(1)}, u32[]{:S(2)}, u32[]{:S(2)}) collective-permute-start(f32[2,128]{1,0:T(2,128)S(1)} %get-tuple-element.53), channel_id=1, source_target_pairs={{0,31},{1,2},{2,1},{3,4},{4,3},{5,6},{6,5},{7,8},{8,7},{9,10},{10,... | collective-permute-start | bytes 3080 | tf_op jit(solution)/shard_map/ppermute | solution.py:385
  65.7 13.3 %collective-permute-start.16 = (f32[2,128]{1,0:T(2,128)S(1)}, f32[2,128]{1,0:T(2,128)S(1)}, u32[]{:S(2)}, u32[]{:S(2)}) collective-permute-start(f32[2,128]{1,0:T(2,128)S(1)} %get-tuple-element.55), channel_id=1, source_target_pairs={{0,32},{32,0},{64,96},{96,64},{128,160},{160,128},{192,224},{224,1... | collective-permute-start | bytes 3080 | tf_op jit(solution)/shard_map/ppermute | solution.py:382
  67.4 11.6 %collective-permute-start.17 = (f32[2,128]{1,0:T(2,128)S(1)}, f32[2,128]{1,0:T(2,128)S(1)}, u32[]{:S(2)}, u32[]{:S(2)}) collective-permute-start(f32[2,128]{1,0:T(2,128)S(1)} %get-tuple-element.56), channel_id=1, source_target_pairs={{0,224},{32,64},{64,32},{96,128},{128,96},{160,192},{192,160},{224... | collective-permute-start | bytes 3080 | tf_op jit(solution)/shard_map/ppermute | solution.py:384
  68.6 10.5 %collective-permute-start.18 = (f32[2,128]{1,0:T(2,128)S(1)}, f32[2,128]{1,0:T(2,128)S(1)}, u32[]{:S(2)}, u32[]{:S(2)}) collective-permute-start(f32[2,128]{1,0:T(2,128)S(1)} %get-tuple-element.57), channel_id=1, source_target_pairs={{0,1},{1,0},{2,3},{3,2},{4,5},{5,4},{6,7},{7,6},{8,9},{9,8},{10,11... | collective-permute-start | bytes 3080 | tf_op jit(solution)/shard_map/ppermute | solution.py:383
  68.6 10.5 %collective-permute-start.19 = (f32[2,128]{1,0:T(2,128)S(1)}, f32[2,128]{1,0:T(2,128)S(1)}, u32[]{:S(2)}, u32[]{:S(2)}) collective-permute-start(f32[2,128]{1,0:T(2,128)S(1)} %get-tuple-element.58), channel_id=1, source_target_pairs={{0,31},{1,2},{2,1},{3,4},{4,3},{5,6},{6,5},{7,8},{8,7},{9,10},{10,... | collective-permute-start | bytes 3080 | tf_op jit(solution)/shard_map/ppermute | solution.py:385
  (10 other events, 94.0 us)

commit v4 on v3

--- a/solution.py
+++ b/solution.py
@@ -12,6 +12,7 @@
 BF16 = jnp.bfloat16
 LANES = 128
 NN_DEV = 2048
+EBLK = 1024
 GH = 256
 TGT_DEV = 32
 OWN_ROWS = NN_DEV // LANES
@@ -22,7 +23,7 @@
 PAD_SLOTS = 384
 N_DEV = 256
 TGT_ROWS = N_DEV // 4
-CHUNKS = 4
+CHUNKS = (20, 24, 20)
 GROUP = 4
 KDIM = 32
 SPLITS = 3
@@ -85,10 +86,13 @@
     return conn_ref[pl.ds(32 * t + a, 8, stride=4), :]
 
 
-def element_gradient(ext, conn_ref, grad_ref, last_ref, t):
+def element_gradient(ext, conn_ref, grad_ref, turn_ref, t):
     corner = [gather_rows(ext, conn_block(conn_ref, a, t)) for a in range(4)]
-    grads = [grad_ref[pl.ds(64 * t + c, 8, stride=8), :] for c in range(8)]
-    grads.append(last_ref[pl.ds(pl.multiple_of(8 * t, 8), 8), :])
+    for k in range(8):
+        lanes = pl.ds(pl.multiple_of(EBLK * t + LANES * k, LANES), LANES)
+        turn_ref[8 * k:8 * k + 8, :] = grad_ref[0:8, lanes]
+        turn_ref[64 + k:65 + k, :] = grad_ref[8:9, lanes]
+    grads = [turn_ref[pl.ds(c, 8, stride=8), :] for c in range(8)] + [turn_ref[64:72, :]]
     diff = [corner[a] - corner[3] for a in range(3)]
     field = [
         grads[k] * diff[0] + grads[3 + k] * diff[1] + grads[6 + k] * diff[2]
@@ -143,7 +147,9 @@
     return [jnp.concatenate([got[d:d + 1], got[4 + d:5 + d]], axis=0) for d in range(4)]
 
 
-def pick_kernel(v_ref, list_ref, point_ref, target_ref, *out_refs):
+def pick_kernel(v_ref, list_ref, point_ref, target_ref, same_ref, same_list_ref, *out_refs):
+    same_ref[...] = v_ref[...]
+    same_list_ref[...] = list_ref[...]
     put_outgoing(picked_blocks(v_ref[...], list_ref[...]), out_refs)
     lane = lax.broadcasted_iota(jnp.int32, (1, LANES), 1)
     own = jnp.zeros((1, LANES), F32)
@@ -155,13 +161,13 @@
     target_ref[...] = jnp.broadcast_to(own, (N_DEV, LANES))
 
 
-def apply_kernel(live_ref, v_ref, ga, gb, gc, gd, conn_ref, grad_ref, last_ref, vol_ref,
-                 own_ref, oa, ob, oc, od, ext_ref, acc_ref):
+def apply_kernel(live_ref, v_ref, ga, gb, gc, gd, conn_ref, grad_ref, vol_ref,
+                 own_ref, oa, ob, oc, od, ext_ref, acc_ref, turn_ref):
     ext_ref[...] = extend(v_ref[...], [ga, gb, gc, gd])
     acc_ref[...] = jnp.zeros_like(acc_ref)
 
     def element_block(t, carry):
-        grads, field = element_gradient(ext_ref[...], conn_ref, grad_ref, last_ref, t)
+        grads, field = element_gradient(ext_ref[...], conn_ref, grad_ref, turn_ref, t)
         vol = block_volume(vol_ref, t)
         field = [vol * f for f in field]
         terms = [
@@ -194,8 +200,18 @@
     put_outgoing(picked_blocks(value, lists), (oa, ob, oc, od))
 
 
-def prepare_kernel(src_ref, tgt_ref, wide_ref, left_ref, right_ref, row_ref):
-    src = src_ref[...]
+def prepare_kernel(point_ref, cos_ref, angle_ref, area_ref, mass_ref, tgt_ref,
+                   wide_ref, left_ref, right_ref, row_ref, same_mass_ref):
+    same_mass_ref[...] = mass_ref[...]
+    third = cos_ref[...].reshape(1, SLOTS)
+    angle = angle_ref[...].reshape(1, SLOTS)
+    area = area_ref[...].reshape(1, SLOTS) * inverse_four_pi
+    sine = area * jnp.sqrt(1.0 - third * third)
+    src = jnp.concatenate(
+        [point_ref[...], sine * jnp.cos(angle), sine * jnp.sin(angle), area * third,
+         jnp.zeros((2, SLOTS), F32)], axis=0,
+    )
+    src = jnp.concatenate([src, jnp.zeros((8, PAD_SLOTS - SLOTS), F32)], axis=1)
     cols = jnp.transpose(src)
     for c in range(6):
         wide_ref[c] = jnp.broadcast_to(cols[0:SLOTS, c:c + 1], (SLOTS, LANES))
@@ -232,9 +248,7 @@
         right_ref[:, g * LANES:(g + 1) * LANES] = block.astype(BF16)
 
 
-def entries_kernel(chunk, wide_ref, left_ref, right_ref, row_ref, entry_ref):
-    base = chunk * (TGT_ROWS // CHUNKS)
-
+def entries_kernel(base, wide_ref, left_ref, right_ref, row_ref, entry_ref):
     def target_group(g, carry):
         first = base + g * GROUP
         lanes = pl.ds(pl.multiple_of(first * LANES, GROUP * LANES), GROUP * LANES)
@@ -255,19 +269,19 @@
                 entry_ref[rows, out] = value
         return carry
 
-    lax.fori_loop(0, TGT_ROWS // CHUNKS // GROUP, target_group, 0)
-
-
-def far_kernel(live_ref, b_ref, v1_ref, v2_ref, ga, gb, gc, gd, conn_ref, grad_ref, last_ref, vol_ref,
-               mass_ref, node_ref, e0, e1, e2, e3,
-               out_ref, trace_ref, ext_ref, d0, d1, d2, lhs_ref):
+    lax.fori_loop(0, entry_ref.shape[1] // (GROUP * LANES), target_group, 0)
+
+
+def far_kernel(live_ref, b_ref, v1_ref, v2_ref, ga, gb, gc, gd, conn_ref, grad_ref, vol_ref,
+               mass_ref, node_ref, e0, e1, e2,
+               out_ref, trace_ref, ext_ref, d0, d1, d2, lhs_ref, turn_ref):
     b = b_ref[...]
     v1 = v1_ref[...]
     v2 = v2_ref[...]
     ext_ref[...] = extend(v2, [ga, gb, gc, gd])
 
     def energy_block(t, total):
-        _, field = element_gradient(ext_ref[...], conn_ref, grad_ref, last_ref, t)
+        _, field = element_gradient(ext_ref[...], conn_ref, grad_ref, turn_ref, t)
         return total + block_volume(vol_ref, t) * (
             field[0] * field[0] + field[1] * field[1] + field[2] * field[2]
         )
@@ -295,11 +309,12 @@
             block = jnp.where(sub == 2 * k + 1, t - high, block)
         lhs_ref[:, r * LANES:(r + 1) * LANES] = block.astype(BF16)
     lhs = lhs_ref[:, 0:SLOTS]
-    each = TGT_ROWS // CHUNKS
-    for chunk, entry_ref in enumerate((e0, e1, e2, e3)):
+    base = 0
+    for each, entry_ref in zip(CHUNKS, (e0, e1, e2)):
         res = jnp.dot(lhs, entry_ref[...], preferred_element_type=F32)
+        base += each
         for q in range(each):
-            at = slice(chunk * each + q, chunk * each + q + 1)
+            at = slice(base - each + q, base - each + q + 1)
             part = res[:, q * LANES:(q + 1) * LANES]
             d0[at, :] = part[0:1] + part[1:2]
             d1[at, :] = part[2:3] + part[3:4]
@@ -366,51 +381,59 @@
 
 
 PIECE = (2, LANES)
-
-
-def first_pairs(count):
-    return [(i, i ^ 1) for i in range(count)]
-
-
-def second_pairs(count):
-    return [(i, (((i + 1) ^ 1) - 1) % count) for i in range(count)]
+TURN = pltpu.VMEM((72, LANES), F32)
+
+
+def swap_partners(rows, cols, axis, second):
+    out = []
+    for r in range(rows):
+        for c in range(cols):
+            me, count = (r, rows) if axis == "row" else (c, cols)
+            if not second:
+                other = me ^ 1
+            elif 0 < me < count - 1:
+                other = ((me + 1) ^ 1) - 1
+            else:
+                other = None
+            if axis == "row":
+                pair = (other, c) if other is not None else (r, c ^ 1)
+            else:
+                pair = (r, other) if other is not None else (r ^ 1, c)
+            out.append((r * cols + c, pair[0] * cols + pair[1]))
+    return out
 
 
 def exchange(pieces):
     rows = lax.axis_size("row")
     cols = lax.axis_size("col")
-    row_a = lax.ppermute(pieces[0], "row", first_pairs(rows))
-    col_a = lax.ppermute(pieces[2], "col", first_pairs(cols))
-    row_b = lax.ppermute(pieces[1], "row", second_pairs(rows))
-    col_b = lax.ppermute(pieces[3], "col", second_pairs(cols))
-    return [row_a, row_b, col_a, col_b]
+    got = []
+    for k in range(4):
+        axis = "row" if k < 2 else "col"
+        got.append(lax.ppermute(pieces[k], ("row", "col"), swap_partners(rows, cols, axis, k % 2 == 1)))
+    return got
 
 
 def per_device(connectivity, gradients, volumes, live_blocks, send_lists, divergence, mass_shift,
                boundary_nodes, surface_points, normal_cos, normal_angle, node_areas):
     conn = connectivity.reshape(4, ELEM_ROWS, LANES).transpose(1, 0, 2).reshape(4 * ELEM_ROWS, LANES)
-    grads = gradients[0:8].reshape(8, ELEM_ROWS, LANES).transpose(1, 0, 2).reshape(8 * ELEM_ROWS, LANES)
-    last = gradients[8].reshape(ELEM_ROWS, LANES)
     vol = volumes.reshape(ELEM_ROWS, LANES)
     lists = send_lists.reshape(4, 2, LANES).transpose(1, 0, 2).reshape(8, LANES)
     b = divergence.reshape(OWN_ROWS, LANES)
     mass = mass_shift.reshape(OWN_ROWS, LANES)
     nodes = jnp.pad(boundary_nodes, (0, 8 * LANES - SLOTS)).reshape(8, LANES)
-    elements = (conn, grads, last, vol)
-
-    mine, *pieces = call(pick_kernel, [(N_DEV, LANES)] + [PIECE] * 4, (b, lists, surface_points))
+    elements = (conn, gradients, vol)
+
+    mine, b, lists, *pieces = call(
+        pick_kernel,
+        [(N_DEV, LANES), b.shape, jax.ShapeDtypeStruct(lists.shape, lists.dtype)] + [PIECE] * 4,
+        (b, lists, surface_points),
+    )
     targets = lax.all_to_all(mine, ("row", "col"), 0, 0, tiled=True)
-    sine = jnp.sqrt(1.0 - normal_cos * normal_cos)
-    normals = jnp.stack([sine * jnp.cos(normal_angle), sine * jnp.sin(normal_angle), normal_cos])
-    weighted = (node_areas * inverse_four_pi)[None, :] * normals
-    sources = jnp.pad(
-        jnp.concatenate([surface_points, weighted], axis=0), ((0, 2), (0, PAD_SLOTS - SLOTS))
-    )
     prepared = None
     chunks = []
 
     def fill():
-        nonlocal prepared
+        nonlocal prepared, mass
         if prepared is None:
             prepared = call(
                 prepare_kernel,
@@ -419,13 +442,17 @@
                     jax.ShapeDtypeStruct((SLOTS, KDIM), BF16),
                     jax.ShapeDtypeStruct((KDIM, TGT_ROWS * LANES), BF16),
                     (3, TGT_ROWS, LANES),
+                    mass.shape,
                 ],
-                (sources, targets),
+                (surface_points, normal_cos, normal_angle, node_areas, mass, targets),
             )
-        chunk = len(chunks)
+            *prepared, mass = prepared
+            return
+        done = len(chunks)
+        base = sum(CHUNKS[:done])
         chunks.append(call(
-            lambda *refs: entries_kernel(chunk, *refs),
-            [jax.ShapeDtypeStruct((SLOTS, TGT_ROWS // CHUNKS * LANES), BF16)],
+            lambda *refs: entries_kernel(base, *refs),
+            [jax.ShapeDtypeStruct((SLOTS, CHUNKS[done] * LANES), BF16)],
             prepared,
         )[0])
 
@@ -441,7 +468,7 @@
         own, *back = call(
             apply_kernel, [(OWN_ROWS, LANES)] + [PIECE] * 4,
             (live_blocks, vectors[-1], *ghosts, *elements), smem=1,
-            scratch=[pltpu.VMEM((EXT_ROWS, LANES), F32), pltpu.VMEM((HIGH_ROWS, LANES), F32)],
+            scratch=[pltpu.VMEM((EXT_ROWS, LANES), F32), pltpu.VMEM((HIGH_ROWS, LANES), F32), TURN],
         )
         returned = swap(2 * step + 1, back)
         new, *pieces = call(
@@ -455,7 +482,7 @@
         (live_blocks, *vectors, *ghosts, *elements, mass, nodes, *chunks), smem=1,
         scratch=[pltpu.VMEM((EXT_ROWS, LANES), F32)]
         + [pltpu.VMEM((TGT_ROWS, LANES), F32)] * 3
-        + [pltpu.VMEM((8, PAD_SLOTS), BF16)],
+        + [pltpu.VMEM((8, PAD_SLOTS), BF16), TURN],
     )
     got = lax.all_to_all(partial, ("row", "col"), 0, 0, tiled=True)
     potential, dirichlet = call(

time: 102 us -> 97.9 us (0.960)
  starting transfers between devices: 53 us -> 39.4 us
  blocking collectives: 19.6 us -> 26 us
  local copies, waits for them, and re-layouts: 7.12 us -> 10.9 us
  other arithmetic: 1.45 us -> 0 us
    ppermute x20, starting transfers between devices: 45.7 us -> 23.8 us  [exchange(): lax.ppermute(pieces[k], ('row', 'col'), swap_partners(rows, cols, axis, k...]
    all_to_all x1, starting transfers between devices: 7.32 us -> 15.6 us  [per_device(): targets = lax.all_to_all(mine, ('row', 'col'), 0, 0, tiled=True)]
    all_to_all x1, blocking collectives: 19.6 us -> 26 us  [per_device(): got = lax.all_to_all(partial, ('row', 'col'), 0, 0, tiled=True)]
    unnamed x26 -> x36, local copies, waits for them, and re-layouts: 4.49 us -> 10.9 us
    mul x3 -> x0, other arithmetic: 1.44 us -> none  [the longest x1 0.74 us: per_device(): sine * jnp.cos(normal_angle)]
    pallas_call x12 -> x11, Pallas kernels: 15.2 us -> 15.3 us  [call(): pl.pallas_call(body, out_shape=out_shapes, in_specs=specs, out_specs=[pl....]
  transfers between devices with their start and end apart: 21 -> 21, of which waited for: 3 -> 5; matrix products, arithmetic and copies ran while one was open for 4% -> 0% of each run, Pallas kernels for 12% -> 9%
where the time goes in v4:
time: 97.9 us; the launch traced here: 97.2 us
  starting transfers between devices  39.4 us (40%)
  blocking collectives  26 us (27%)
  Pallas kernels  15.3 us (16%)
  local copies, waits for them, and re-layouts  10.9 us (11%)
  waiting for transfers between devices  4 us (4%)
  between operations  1.53 us (2%)
    all_to_all x1, blocking collectives, per_device(): got = lax.all_to_all(partial, ('row', 'col'), 0, 0, tiled=True)  26 us
    ppermute x20, starting transfers between devices, exchange(): lax.ppermute(pieces[k], ('row', 'col'), swap_partners(rows, cols, axis, k...  23.8 us
    all_to_all x1, starting transfers between devices, per_device(): targets = lax.all_to_all(mine, ('row', 'col'), 0, 0, tiled=True)  15.6 us
    pallas_call x11, Pallas kernels, call(): pl.pallas_call(body, out_shape=out_shapes, in_specs=specs, out_specs=[pl....  15.3 us
    unnamed x36, local copies, waits for them, and re-layouts  10.9 us
    ppermute x20, waiting for transfers between devices, exchange(): lax.ppermute(pieces[k], ('row', 'col'), swap_partners(rows, cols, axis, k...  4 us
  transfers between devices with their start and end apart: 21, of which 5 were waited for; matrix products, arithmetic and copies ran while one was open for 0% of the time, Pallas kernels for 9%

profile of v4, /device:TPU:1, one launch (start us, length us, event | category | flops | bytes accessed | tf_op | source)
XLA Modules:
  0.0 97.2 jit_solution(4959340569662961261)
XLA Ops:
  3.5 15.6 %all-to-all-start = ((f32[256,1,128]{2,1,0:T(1,128)}), f32[256,1,128]{2,1,0:T(1,128)S(1)}, u32[]{:S(2)}, u32[]{:S(2)}) async-start(f32[256,1,128]{2,1,0:T(1,128)} %bitcast.10), calls=%async_computation | async-start | bytes 262144 | tf_op jit(solution)/shard_map/all_to_all | solution.py:431
  19.1 2.2 %collective-permute-start = (f32[2,128]{1,0:T(2,128)S(1)}, f32[2,128]{1,0:T(2,128)S(1)}, u32[]{:S(2)}, u32[]{:S(2)}) collective-permute-start(f32[2,128]{1,0:T(2,128)S(1)} %get-tuple-element.39), channel_id=1, source_target_pairs={{0,32},{1,33},{2,34},{3,35},{4,36},{5,37},{6,38},{7,39},{8,40},{9,... | collective-permute-start | bytes 3080 | tf_op jit(solution)/shard_map/ppermute | solution.py:412
  21.4 0.9 collective-permute-start.2
  22.3 1.2 %collective-permute-start.3 = (f32[2,128]{1,0:T(2,128)S(1)}, f32[2,128]{1,0:T(2,128)S(1)}, u32[]{:S(2)}, u32[]{:S(2)}) collective-permute-start(f32[2,128]{1,0:T(2,128)S(1)} %get-tuple-element.42), channel_id=1, source_target_pairs={{0,32},{1,2},{2,1},{3,4},{4,3},{5,6},{6,5},{7,8},{8,7},{9,10},{10,... | collective-permute-start | bytes 3080 | tf_op jit(solution)/shard_map/ppermute | solution.py:412
  24.7 1.0 %copy-done = f32[9,8192]{1,0:T(8,128)S(1)} copy-done((f32[9,8192]{1,0:T(8,128)S(1)}, f32[9,8192]{1,0:T(8,128)}, u32[]{:S(2)}) %copy-start) | copy-done | bytes 294936
  27.4 2.4 %shard_map.132 = (f32[16,128]{1,0:T(8,128)S(1)}, f32[2,128]{1,0:T(2,128)S(1)}, f32[2,128]{1,0:T(2,128)S(1)}, f32[2,128]{1,0:T(2,128)S(1)}, f32[2,128]{1,0:T(2,128)S(1)}) custom-call(s32[1]{0:T(128)S(6)} %copy.20.live_ref, f32[16,128]{1,0:T(8,128)S(1)} %get-tuple-element.38.v_ref.b_ref, f32[2,128]{1,0:T(2,128)S(1)} %collective-permute-done.ga, ...), custom_call_target="tpu_custom_call" | custom-call | flops 2000000 | bytes 1048576 | tf_op jit(solution)/shard_map/pallas_call | solution.py:372
  29.7 1.4 %collective-permute-start.4 = (f32[2,128]{1,0:T(2,128)S(1)}, f32[2,128]{1,0:T(2,128)S(1)}, u32[]{:S(2)}, u32[]{:S(2)}) collective-permute-start(f32[2,128]{1,0:T(2,128)S(1)} %get-tuple-element.44), channel_id=1, source_target_pairs={{0,32},{1,33},{2,34},{3,35},{4,36},{5,37},{6,38},{7,39},{8,40},{9,... | collective-permute-start | bytes 3080 | tf_op jit(solution)/shard_map/ppermute | solution.py:412
  31.1 1.0 %collective-permute-start.6 = (f32[2,128]{1,0:T(2,128)S(1)}, f32[2,128]{1,0:T(2,128)S(1)}, u32[]{:S(2)}, u32[]{:S(2)}) collective-permute-start(f32[2,128]{1,0:T(2,128)S(1)} %get-tuple-element.46), channel_id=1, source_target_pairs={{0,1},{1,0},{2,3},{3,2},{4,5},{5,4},{6,7},{7,6},{8,9},{9,8},{10,11... | collective-permute-start | bytes 3080 | tf_op jit(solution)/shard_map/ppermute | solution.py:412
  32.1 1.1 %collective-permute-start.7 = (f32[2,128]{1,0:T(2,128)S(1)}, f32[2,128]{1,0:T(2,128)S(1)}, u32[]{:S(2)}, u32[]{:S(2)}) collective-permute-start(f32[2,128]{1,0:T(2,128)S(1)} %get-tuple-element.47), channel_id=1, source_target_pairs={{0,32},{1,2},{2,1},{3,4},{4,3},{5,6},{6,5},{7,8},{8,7},{9,10},{10,... | collective-permute-start | bytes 3080 | tf_op jit(solution)/shard_map/ppermute | solution.py:412
  38.0 2.4 %collective-permute-start.10 = (f32[2,128]{1,0:T(2,128)S(1)}, f32[2,128]{1,0:T(2,128)S(1)}, u32[]{:S(2)}, u32[]{:S(2)}) collective-permute-start(f32[2,128]{1,0:T(2,128)S(1)} %get-tuple-element.54), channel_id=1, source_target_pairs={{0,1},{1,0},{2,3},{3,2},{4,5},{5,4},{6,7},{7,6},{8,9},{9,8},{10,11... | collective-permute-start | bytes 3080 | tf_op jit(solution)/shard_map/ppermute | solution.py:412
  40.4 2.2 %collective-permute-start.11 = (f32[2,128]{1,0:T(2,128)S(1)}, f32[2,128]{1,0:T(2,128)S(1)}, u32[]{:S(2)}, u32[]{:S(2)}) collective-permute-start(f32[2,128]{1,0:T(2,128)S(1)} %get-tuple-element.55), channel_id=1, source_target_pairs={{0,32},{1,2},{2,1},{3,4},{4,3},{5,6},{6,5},{7,8},{8,7},{9,10},{10,... | collective-permute-start | bytes 3080 | tf_op jit(solution)/shard_map/ppermute | solution.py:412
  43.7 1.8 %collective-permute-done.9.gb = f32[2,128]{1,0:T(2,128)S(1)} collective-permute-done((f32[2,128]{1,0:T(2,128)S(1)}, f32[2,128]{1,0:T(2,128)S(1)}, u32[]{:S(2)}, u32[]{:S(2)}) %collective-permute-start.9) | collective-permute-done | bytes 1056 | tf_op jit(solution)/shard_map/ppermute | solution.py:412
  45.5 1.0 %copy-done.1 = f32[9,8192]{1,0:T(8,128)S(1)} copy-done((f32[9,8192]{1,0:T(8,128)S(1)}, f32[9,8192]{1,0:T(8,128)}, u32[]{:S(2)}) %copy-start.1) | copy-done | bytes 294936
  48.3 2.4 %shard_map.135 = (f32[16,128]{1,0:T(8,128)S(1)}, f32[2,128]{1,0:T(2,128)S(1)}, f32[2,128]{1,0:T(2,128)S(1)}, f32[2,128]{1,0:T(2,128)S(1)}, f32[2,128]{1,0:T(2,128)S(1)}) custom-call(s32[1]{0:T(128)S(6)} %copy.20.live_ref, f32[16,128]{1,0:T(8,128)S(1)} %get-tuple-element.51.v_ref.v1_ref, f32[2,128]{1,0:T(2,128)S(1)} %collective-permute-done.8.ga, ...), custom_call_target="tpu_custom_call" | custom-call | flops 2000000 | bytes 1048576 | tf_op jit(solution)/shard_map/pallas_call | solution.py:372
  50.6 4.6 %collective-permute-start.12 = (f32[2,128]{1,0:T(2,128)S(1)}, f32[2,128]{1,0:T(2,128)S(1)}, u32[]{:S(2)}, u32[]{:S(2)}) collective-permute-start(f32[2,128]{1,0:T(2,128)S(1)} %get-tuple-element.57), channel_id=1, source_target_pairs={{0,32},{1,33},{2,34},{3,35},{4,36},{5,37},{6,38},{7,39},{8,40},{9,... | collective-permute-start | bytes 3080 | tf_op jit(solution)/shard_map/ppermute | solution.py:412
  56.1 1.3 %collective-permute-start.15 = (f32[2,128]{1,0:T(2,128)S(1)}, f32[2,128]{1,0:T(2,128)S(1)}, u32[]{:S(2)}, u32[]{:S(2)}) collective-permute-start(f32[2,128]{1,0:T(2,128)S(1)} %get-tuple-element.60), channel_id=1, source_target_pairs={{0,32},{1,2},{2,1},{3,4},{4,3},{5,6},{6,5},{7,8},{8,7},{9,10},{10,... | collective-permute-start | bytes 3080 | tf_op jit(solution)/shard_map/ppermute | solution.py:412
  57.3 1.1 %collective-permute-done.13.rb = f32[2,128]{1,0:T(2,128)S(1)} collective-permute-done((f32[2,128]{1,0:T(2,128)S(1)}, f32[2,128]{1,0:T(2,128)S(1)}, u32[]{:S(2)}, u32[]{:S(2)}) %collective-permute-start.13) | collective-permute-done | bytes 1056 | tf_op jit(solution)/shard_map/ppermute | solution.py:412
  59.4 1.6 %collective-permute-start.17 = (f32[2,128]{1,0:T(2,128)S(1)}, f32[2,128]{1,0:T(2,128)S(1)}, u32[]{:S(2)}, u32[]{:S(2)}) collective-permute-start(f32[2,128]{1,0:T(2,128)S(1)} %get-tuple-element.63), channel_id=1, source_target_pairs={{0,1},{1,0},{2,3},{3,2},{4,5},{5,4},{6,7},{7,6},{8,9},{9,8},{10,11... | collective-permute-start | bytes 3080 | tf_op jit(solution)/shard_map/ppermute | solution.py:412
  61.0 1.7 %collective-permute-start.18 = (f32[2,128]{1,0:T(2,128)S(1)}, f32[2,128]{1,0:T(2,128)S(1)}, u32[]{:S(2)}, u32[]{:S(2)}) collective-permute-start(f32[2,128]{1,0:T(2,128)S(1)} %get-tuple-element.64), channel_id=1, source_target_pairs={{0,1},{1,0},{2,3},{3,2},{4,5},{5,4},{6,7},{7,6},{8,9},{9,8},{10,11... | collective-permute-start | bytes 3080 | tf_op jit(solution)/shard_map/ppermute | solution.py:412
  62.8 1.8 %shard_map.139.e2 = bf16[320,2560]{1,0:T(8,128)(2,1)S(1)} custom-call(f32[6,320,128]{2,1,0:T(8,128)S(1)} %get-tuple-element.66.refs_0_, bf16[320,32]{1,0:T(8,128)(2,1)S(1)} %get-tuple-element.67.refs_1_, bf16[32,8192]{1,0:T(8,128)(2,1)S(1)} %get-tuple-element.68.refs_2_, f32[3,64,128]{2,1,0:T(8,128)S(1)} %get-tuple-element.69.refs_3_), custom_call_target="tpu_custom_call" | custom-call | flops 2000000 | bytes 1048576 | tf_op jit(solution)/shard_map/pallas_call | solution.py:372
  64.6 2.2 %shard_map.138.e1 = bf16[320,3072]{1,0:T(8,128)(2,1)S(1)} custom-call(f32[6,320,128]{2,1,0:T(8,128)S(1)} %get-tuple-element.66.refs_0_, bf16[320,32]{1,0:T(8,128)(2,1)S(1)} %get-tuple-element.67.refs_1_, bf16[32,8192]{1,0:T(8,128)(2,1)S(1)} %get-tuple-element.68.refs_2_, f32[3,64,128]{2,1,0:T(8,128)S(1)} %get-tuple-element.69.refs_3_), custom_call_target="tpu_custom_call" | custom-call | flops 2000000 | bytes 1048576 | tf_op jit(solution)/shard_map/pallas_call | solution.py:372
  66.9 1.8 %shard_map.137.e0 = bf16[320,2560]{1,0:T(8,128)(2,1)S(1)} custom-call(f32[6,320,128]{2,1,0:T(8,128)S(1)} %get-tuple-element.66.refs_0_, bf16[320,32]{1,0:T(8,128)(2,1)S(1)} %get-tuple-element.67.refs_1_, bf16[32,8192]{1,0:T(8,128)(2,1)S(1)} %get-tuple-element.68.refs_2_, f32[3,64,128]{2,1,0:T(8,128)S(1)} %get-tuple-element.69.refs_3_), custom_call_target="tpu_custom_call" | custom-call | flops 2000000 | bytes 1048576 | tf_op jit(solution)/shard_map/pallas_call | solution.py:372
  68.8 1.7 %shard_map.140 = (f32[256,128]{1,0:T(8,128)S(1)}, f32[3,8,128]{2,1,0:T(8,128)S(1)}) custom-call(s32[1]{0:T(128)S(6)} %copy.20.live_ref, f32[16,128]{1,0:T(8,128)S(1)} %get-tuple-element.38.v_ref.b_ref, f32[16,128]{1,0:T(8,128)S(1)} %get-tuple-element.51.v_ref.v1_ref, f32[16,128]{1,0:T(8,128)S(1)} %get-tuple-element.61.v2_ref, ...), custom_call_target="tpu_custom_call" | custom-call | flops 2000000 | bytes 1048576 | tf_op jit(solution)/shard_map/pallas_call | solution.py:372
  70.5 26.0 %all_to_all.22 = f32[256,1,128]{2,1,0:T(1,128)S(1)} all-to-all(f32[256,1,128]{2,1,0:T(1,128)S(1)} %bitcast.33), channel_id=1, replica_groups=mesh['row'=8,'col'=32] {'row','col'}, dimensions={0} | all-to-all | bytes 262144 | tf_op jit(solution)/shard_map/all_to_all | solution.py:487
  (67 shorter events, 15.0 us)
Async XLA Ops:
  0.6 62.1 %copy-start.17 = (s32[320]{0:T(512)S(1)}, s32[320]{0:T(512)}, u32[]{:S(2)}) copy-start(s32[320]{0:T(512)} %param.19) | copy-start | bytes 3844
  3.5 29.8 %all-to-all-start = ((f32[256,1,128]{2,1,0:T(1,128)}), f32[256,1,128]{2,1,0:T(1,128)S(1)}, u32[]{:S(2)}, u32[]{:S(2)}) async-start(f32[256,1,128]{2,1,0:T(1,128)} %bitcast.10), calls=%async_computation | async-start | bytes 262144 | tf_op jit(solution)/shard_map/all_to_all | solution.py:431
  19.1 5.0 %collective-permute-start = (f32[2,128]{1,0:T(2,128)S(1)}, f32[2,128]{1,0:T(2,128)S(1)}, u32[]{:S(2)}, u32[]{:S(2)}) collective-permute-start(f32[2,128]{1,0:T(2,128)S(1)} %get-tuple-element.39), channel_id=1, source_target_pairs={{0,32},{1,33},{2,34},{3,35},{4,36},{5,37},{6,38},{7,39},{8,40},{9,... | collective-permute-start | bytes 3080 | tf_op jit(solution)/shard_map/ppermute | solution.py:412
  21.4 3.3 %collective-permute-start.1 = (f32[2,128]{1,0:T(2,128)S(1)}, f32[2,128]{1,0:T(2,128)S(1)}, u32[]{:S(2)}, u32[]{:S(2)}) collective-permute-start(f32[2,128]{1,0:T(2,128)S(1)} %get-tuple-element.40), channel_id=1, source_target_pairs={{0,1},{1,0},{2,3},{3,2},{4,5},{5,4},{6,7},{7,6},{8,9},{9,8},{10,11... | collective-permute-start | bytes 3080 | tf_op jit(solution)/shard_map/ppermute | solution.py:412
  21.4 3.3 %collective-permute-start.2 = (f32[2,128]{1,0:T(2,128)S(1)}, f32[2,128]{1,0:T(2,128)S(1)}, u32[]{:S(2)}, u32[]{:S(2)}) collective-permute-start(f32[2,128]{1,0:T(2,128)S(1)} %get-tuple-element.41), channel_id=1, source_target_pairs={{0,1},{1,0},{2,3},{3,2},{4,5},{5,4},{6,7},{7,6},{8,9},{9,8},{10,11... | collective-permute-start | bytes 3080 | tf_op jit(solution)/shard_map/ppermute | solution.py:412
  22.3 2.4 %collective-permute-start.3 = (f32[2,128]{1,0:T(2,128)S(1)}, f32[2,128]{1,0:T(2,128)S(1)}, u32[]{:S(2)}, u32[]{:S(2)}) collective-permute-start(f32[2,128]{1,0:T(2,128)S(1)} %get-tuple-element.42), channel_id=1, source_target_pairs={{0,32},{1,2},{2,1},{3,4},{4,3},{5,6},{6,5},{7,8},{8,7},{9,10},{10,... | collective-permute-start | bytes 3080 | tf_op jit(solution)/shard_map/ppermute | solution.py:412
  29.7 7.9 %collective-permute-start.4 = (f32[2,128]{1,0:T(2,128)S(1)}, f32[2,128]{1,0:T(2,128)S(1)}, u32[]{:S(2)}, u32[]{:S(2)}) collective-permute-start(f32[2,128]{1,0:T(2,128)S(1)} %get-tuple-element.44), channel_id=1, source_target_pairs={{0,32},{1,33},{2,34},{3,35},{4,36},{5,37},{6,38},{7,39},{8,40},{9,... | collective-permute-start | bytes 3080 | tf_op jit(solution)/shard_map/ppermute | solution.py:412
  31.1 6.5 %collective-permute-start.5 = (f32[2,128]{1,0:T(2,128)S(1)}, f32[2,128]{1,0:T(2,128)S(1)}, u32[]{:S(2)}, u32[]{:S(2)}) collective-permute-start(f32[2,128]{1,0:T(2,128)S(1)} %get-tuple-element.45), channel_id=1, source_target_pairs={{0,1},{1,0},{2,3},{3,2},{4,5},{5,4},{6,7},{7,6},{8,9},{9,8},{10,11... | collective-permute-start | bytes 3080 | tf_op jit(solution)/shard_map/ppermute | solution.py:412
  31.1 6.5 %collective-permute-start.6 = (f32[2,128]{1,0:T(2,128)S(1)}, f32[2,128]{1,0:T(2,128)S(1)}, u32[]{:S(2)}, u32[]{:S(2)}) collective-permute-start(f32[2,128]{1,0:T(2,128)S(1)} %get-tuple-element.46), channel_id=1, source_target_pairs={{0,1},{1,0},{2,3},{3,2},{4,5},{5,4},{6,7},{7,6},{8,9},{9,8},{10,11... | collective-permute-start | bytes 3080 | tf_op jit(solution)/shard_map/ppermute | solution.py:412
  32.1 5.5 %collective-permute-start.7 = (f32[2,128]{1,0:T(2,128)S(1)}, f32[2,128]{1,0:T(2,128)S(1)}, u32[]{:S(2)}, u32[]{:S(2)}) collective-permute-start(f32[2,128]{1,0:T(2,128)S(1)} %get-tuple-element.47), channel_id=1, source_target_pairs={{0,32},{1,2},{2,1},{3,4},{4,3},{5,6},{6,5},{7,8},{8,7},{9,10},{10,... | collective-permute-start | bytes 3080 | tf_op jit(solution)/shard_map/ppermute | solution.py:412
  38.0 5.3 %collective-permute-start.10 = (f32[2,128]{1,0:T(2,128)S(1)}, f32[2,128]{1,0:T(2,128)S(1)}, u32[]{:S(2)}, u32[]{:S(2)}) collective-permute-start(f32[2,128]{1,0:T(2,128)S(1)} %get-tuple-element.54), channel_id=1, source_target_pairs={{0,1},{1,0},{2,3},{3,2},{4,5},{5,4},{6,7},{7,6},{8,9},{9,8},{10,11... | collective-permute-start | bytes 3080 | tf_op jit(solution)/shard_map/ppermute | solution.py:412
  40.4 3.0 %collective-permute-start.11 = (f32[2,128]{1,0:T(2,128)S(1)}, f32[2,128]{1,0:T(2,128)S(1)}, u32[]{:S(2)}, u32[]{:S(2)}) collective-permute-start(f32[2,128]{1,0:T(2,128)S(1)} %get-tuple-element.55), channel_id=1, source_target_pairs={{0,32},{1,2},{2,1},{3,4},{4,3},{5,6},{6,5},{7,8},{8,7},{9,10},{10,... | collective-permute-start | bytes 3080 | tf_op jit(solution)/shard_map/ppermute | solution.py:412
  42.5 1.2 %collective-permute-start.8 = (f32[2,128]{1,0:T(2,128)S(1)}, f32[2,128]{1,0:T(2,128)S(1)}, u32[]{:S(2)}, u32[]{:S(2)}) collective-permute-start(f32[2,128]{1,0:T(2,128)S(1)} %get-tuple-element.52), channel_id=1, source_target_pairs={{0,32},{1,33},{2,34},{3,35},{4,36},{5,37},{6,38},{7,39},{8,40},{9,... | collective-permute-start | bytes 3080 | tf_op jit(solution)/shard_map/ppermute | solution.py:412
  42.5 3.0 %collective-permute-start.9 = (f32[2,128]{1,0:T(2,128)S(1)}, f32[2,128]{1,0:T(2,128)S(1)}, u32[]{:S(2)}, u32[]{:S(2)}) collective-permute-start(f32[2,128]{1,0:T(2,128)S(1)} %get-tuple-element.53), channel_id=1, source_target_pairs={{0,1},{1,0},{2,3},{3,2},{4,5},{5,4},{6,7},{7,6},{8,9},{9,8},{10,11... | collective-permute-start | bytes 3080 | tf_op jit(solution)/shard_map/ppermute | solution.py:412
  50.6 6.7 %collective-permute-start.12 = (f32[2,128]{1,0:T(2,128)S(1)}, f32[2,128]{1,0:T(2,128)S(1)}, u32[]{:S(2)}, u32[]{:S(2)}) collective-permute-start(f32[2,128]{1,0:T(2,128)S(1)} %get-tuple-element.57), channel_id=1, source_target_pairs={{0,32},{1,33},{2,34},{3,35},{4,36},{5,37},{6,38},{7,39},{8,40},{9,... | collective-permute-start | bytes 3080 | tf_op jit(solution)/shard_map/ppermute | solution.py:412
  55.2 3.3 %collective-permute-start.13 = (f32[2,128]{1,0:T(2,128)S(1)}, f32[2,128]{1,0:T(2,128)S(1)}, u32[]{:S(2)}, u32[]{:S(2)}) collective-permute-start(f32[2,128]{1,0:T(2,128)S(1)} %get-tuple-element.58), channel_id=1, source_target_pairs={{0,1},{1,0},{2,3},{3,2},{4,5},{5,4},{6,7},{7,6},{8,9},{9,8},{10,11... | collective-permute-start | bytes 3080 | tf_op jit(solution)/shard_map/ppermute | solution.py:412
  55.2 3.3 %collective-permute-start.14 = (f32[2,128]{1,0:T(2,128)S(1)}, f32[2,128]{1,0:T(2,128)S(1)}, u32[]{:S(2)}, u32[]{:S(2)}) collective-permute-start(f32[2,128]{1,0:T(2,128)S(1)} %get-tuple-element.59), channel_id=1, source_target_pairs={{0,1},{1,0},{2,3},{3,2},{4,5},{5,4},{6,7},{7,6},{8,9},{9,8},{10,11... | collective-permute-start | bytes 3080 | tf_op jit(solution)/shard_map/ppermute | solution.py:412
  56.1 2.4 %collective-permute-start.15 = (f32[2,128]{1,0:T(2,128)S(1)}, f32[2,128]{1,0:T(2,128)S(1)}, u32[]{:S(2)}, u32[]{:S(2)}) collective-permute-start(f32[2,128]{1,0:T(2,128)S(1)} %get-tuple-element.60), channel_id=1, source_target_pairs={{0,32},{1,2},{2,1},{3,4},{4,3},{5,6},{6,5},{7,8},{8,7},{9,10},{10,... | collective-permute-start | bytes 3080 | tf_op jit(solution)/shard_map/ppermute | solution.py:412
  58.8 9.9 %collective-permute-start.16 = (f32[2,128]{1,0:T(2,128)S(1)}, f32[2,128]{1,0:T(2,128)S(1)}, u32[]{:S(2)}, u32[]{:S(2)}) collective-permute-start(f32[2,128]{1,0:T(2,128)S(1)} %get-tuple-element.62), channel_id=1, source_target_pairs={{0,32},{1,33},{2,34},{3,35},{4,36},{5,37},{6,38},{7,39},{8,40},{9,... | collective-permute-start | bytes 3080 | tf_op jit(solution)/shard_map/ppermute | solution.py:412
  59.4 9.3 %collective-permute-start.17 = (f32[2,128]{1,0:T(2,128)S(1)}, f32[2,128]{1,0:T(2,128)S(1)}, u32[]{:S(2)}, u32[]{:S(2)}) collective-permute-start(f32[2,128]{1,0:T(2,128)S(1)} %get-tuple-element.63), channel_id=1, source_target_pairs={{0,1},{1,0},{2,3},{3,2},{4,5},{5,4},{6,7},{7,6},{8,9},{9,8},{10,11... | collective-permute-start | bytes 3080 | tf_op jit(solution)/shard_map/ppermute | solution.py:412
  61.0 7.7 %collective-permute-start.18 = (f32[2,128]{1,0:T(2,128)S(1)}, f32[2,128]{1,0:T(2,128)S(1)}, u32[]{:S(2)}, u32[]{:S(2)}) collective-permute-start(f32[2,128]{1,0:T(2,128)S(1)} %get-tuple-element.64), channel_id=1, source_target_pairs={{0,1},{1,0},{2,3},{3,2},{4,5},{5,4},{6,7},{7,6},{8,9},{9,8},{10,11... | collective-permute-start | bytes 3080 | tf_op jit(solution)/shard_map/ppermute | solution.py:412
  62.8 6.0 %collective-permute-start.19 = (f32[2,128]{1,0:T(2,128)S(1)}, f32[2,128]{1,0:T(2,128)S(1)}, u32[]{:S(2)}, u32[]{:S(2)}) collective-permute-start(f32[2,128]{1,0:T(2,128)S(1)} %get-tuple-element.65), channel_id=1, source_target_pairs={{0,32},{1,2},{2,1},{3,4},{4,3},{5,6},{6,5},{7,8},{8,7},{9,10},{10,... | collective-permute-start | bytes 3080 | tf_op jit(solution)/shard_map/ppermute | solution.py:412
  66.8 1.9 %copy-start.2 = (f32[9,8192]{1,0:T(8,128)S(1)}, f32[9,8192]{1,0:T(8,128)}, u32[]{:S(2)}) copy-start(f32[9,8192]{1,0:T(8,128)} %grad_ref.5) | copy-start | bytes 884740
  66.9 1.9 %copy-start.5 = (s32[4,8192]{1,0:T(4,128)S(1)}, s32[4,8192]{1,0:T(4,128)}, u32[]{:S(2)}) copy-start(s32[4,8192]{1,0:T(4,128)} %param.12) | copy-start | bytes 393220
  (15 other events, 12.8 us)

commit v5 on v4

--- a/solution.py
+++ b/solution.py
@@ -18,7 +18,6 @@
 OWN_ROWS = NN_DEV // LANES
 EXT_ROWS = OWN_ROWS + 4 * GH // LANES
 HIGH_ROWS = 32
-ELEM_ROWS = 64
 SLOTS = 320
 PAD_SLOTS = 384
 N_DEV = 256
@@ -28,6 +27,11 @@
 KDIM = 32
 SPLITS = 3
 SCALE = 1.0 / 64.0
+B_ROWS = slice(0, 16)
+MASS_ROWS = slice(16, 32)
+COS_ROWS = slice(32, 35)
+ANGLE_ROWS = slice(35, 38)
+AREA_ROWS = slice(38, 41)
 VMEM_GRANT = 16 << 20
 smoothing = 0.0001
 inverse_four_pi = 1.0 / (4.0 * math.pi)
@@ -82,27 +86,24 @@
     return out
 
 
-def conn_block(conn_ref, a, t):
-    return conn_ref[pl.ds(32 * t + a, 8, stride=4), :]
-
-
-def element_gradient(ext, conn_ref, grad_ref, turn_ref, t):
-    corner = [gather_rows(ext, conn_block(conn_ref, a, t)) for a in range(4)]
+def turn_block(data_ref, turn_ref, t):
     for k in range(8):
         lanes = pl.ds(pl.multiple_of(EBLK * t + LANES * k, LANES), LANES)
-        turn_ref[8 * k:8 * k + 8, :] = grad_ref[0:8, lanes]
-        turn_ref[64 + k:65 + k, :] = grad_ref[8:9, lanes]
-    grads = [turn_ref[pl.ds(c, 8, stride=8), :] for c in range(8)] + [turn_ref[64:72, :]]
+        turn_ref[16 * k:16 * k + 8, :] = data_ref[0:8, lanes]
+        turn_ref[16 * k + 8:16 * k + 14, :] = data_ref[8:14, lanes]
+    rows = [turn_ref[pl.ds(q, 8, stride=16), :] for q in range(14)]
+    return rows[0:9], [r.astype(jnp.int32) for r in rows[9:13]], rows[13]
+
+
+def element_gradient(ext, data_ref, turn_ref, t):
+    grads, index, volume = turn_block(data_ref, turn_ref, t)
+    corner = [gather_rows(ext, i) for i in index]
     diff = [corner[a] - corner[3] for a in range(3)]
     field = [
         grads[k] * diff[0] + grads[3 + k] * diff[1] + grads[6 + k] * diff[2]
         for k in range(3)
     ]
-    return grads, field
-
-
-def block_volume(vol_ref, t):
-    return vol_ref[pl.ds(pl.multiple_of(t * 8, 8), 8), :]
+    return grads, index, volume, field
 
 
 def odd(axis):
@@ -147,10 +148,10 @@
     return [jnp.concatenate([got[d:d + 1], got[4 + d:5 + d]], axis=0) for d in range(4)]
 
 
-def pick_kernel(v_ref, list_ref, point_ref, target_ref, same_ref, same_list_ref, *out_refs):
-    same_ref[...] = v_ref[...]
+def pick_kernel(small_ref, list_ref, point_ref, target_ref, same_list_ref, same_point_ref, *out_refs):
     same_list_ref[...] = list_ref[...]
-    put_outgoing(picked_blocks(v_ref[...], list_ref[...]), out_refs)
+    same_point_ref[...] = point_ref[...]
+    put_outgoing(picked_blocks(small_ref[B_ROWS, :], list_ref[...]), out_refs)
     lane = lax.broadcasted_iota(jnp.int32, (1, LANES), 1)
     own = jnp.zeros((1, LANES), F32)
     for c in range(3):
@@ -161,15 +162,14 @@
     target_ref[...] = jnp.broadcast_to(own, (N_DEV, LANES))
 
 
-def apply_kernel(live_ref, v_ref, ga, gb, gc, gd, conn_ref, grad_ref, vol_ref,
+def apply_kernel(live_ref, v_ref, ga, gb, gc, gd, data_ref,
                  own_ref, oa, ob, oc, od, ext_ref, acc_ref, turn_ref):
-    ext_ref[...] = extend(v_ref[...], [ga, gb, gc, gd])
+    ext_ref[...] = extend(v_ref[0:OWN_ROWS, :], [ga, gb, gc, gd])
     acc_ref[...] = jnp.zeros_like(acc_ref)
 
     def element_block(t, carry):
-        grads, field = element_gradient(ext_ref[...], conn_ref, grad_ref, turn_ref, t)
-        vol = block_volume(vol_ref, t)
-        field = [vol * f for f in field]
+        grads, index, volume, field = element_gradient(ext_ref[...], data_ref, turn_ref, t)
+        field = [volume * f for f in field]
         terms = [
             grads[3 * a] * field[0] + grads[3 * a + 1] * field[1] + grads[3 * a + 2] * field[2]
             for a in range(3)
@@ -177,7 +177,7 @@
         terms.append(-(terms[0] + terms[1] + terms[2]))
         total = acc_ref[...]
         for a in range(4):
-            total = total + scatter_block(conn_block(conn_ref, a, t), terms[a], EXT_ROWS)
+            total = total + scatter_block(index[a], terms[a], EXT_ROWS)
         acc_ref[...] = total
         return carry
 
@@ -189,29 +189,30 @@
     put_outgoing([up, down, right, left], (oa, ob, oc, od))
 
 
-def combine_kernel(own_ref, ra, rb, rc, rd, list_ref, v_ref, mass_ref,
+def combine_kernel(own_ref, ra, rb, rc, rd, list_ref, v_ref, small_ref,
                    next_ref, oa, ob, oc, od):
     lists = list_ref[...]
     back = from_swaps([ra, rb, rc, rd])
     terms = jnp.concatenate([b[0:1] for b in back] + [b[1:2] for b in back], axis=0)
     added = scatter_block(lists, terms, OWN_ROWS)
-    value = (mass_ref[...] * v_ref[...] + own_ref[...] + added) * SCALE
+    value = (small_ref[MASS_ROWS, :] * v_ref[0:OWN_ROWS, :] + own_ref[...] + added) * SCALE
     next_ref[...] = value
     put_outgoing(picked_blocks(value, lists), (oa, ob, oc, od))
 
 
-def prepare_kernel(point_ref, cos_ref, angle_ref, area_ref, mass_ref, tgt_ref,
-                   wide_ref, left_ref, right_ref, row_ref, same_mass_ref):
-    same_mass_ref[...] = mass_ref[...]
-    third = cos_ref[...].reshape(1, SLOTS)
-    angle = angle_ref[...].reshape(1, SLOTS)
-    area = area_ref[...].reshape(1, SLOTS) * inverse_four_pi
+def prepare_kernel(small_ref, point_ref, tgt_ref, wide_ref, left_ref, right_ref, row_ref):
+    def line(rows):
+        return jnp.concatenate([small_ref[r:r + 1, :] for r in range(rows.start, rows.stop)], axis=1)
+
+    third = line(COS_ROWS)
+    angle = line(ANGLE_ROWS)
+    area = line(AREA_ROWS) * inverse_four_pi
     sine = area * jnp.sqrt(1.0 - third * third)
+    points = jnp.concatenate([point_ref[...], jnp.zeros((3, PAD_SLOTS - SLOTS), F32)], axis=1)
     src = jnp.concatenate(
-        [point_ref[...], sine * jnp.cos(angle), sine * jnp.sin(angle), area * third,
-         jnp.zeros((2, SLOTS), F32)], axis=0,
+        [points, sine * jnp.cos(angle), sine * jnp.sin(angle), area * third, jnp.zeros((2, PAD_SLOTS), F32)],
+        axis=0,
     )
-    src = jnp.concatenate([src, jnp.zeros((8, PAD_SLOTS - SLOTS), F32)], axis=1)
     cols = jnp.transpose(src)
     for c in range(6):
         wide_ref[c] = jnp.broadcast_to(cols[0:SLOTS, c:c + 1], (SLOTS, LANES))
@@ -272,22 +273,21 @@
     lax.fori_loop(0, entry_ref.shape[1] // (GROUP * LANES), target_group, 0)
 
 
-def far_kernel(live_ref, b_ref, v1_ref, v2_ref, ga, gb, gc, gd, conn_ref, grad_ref, vol_ref,
-               mass_ref, node_ref, e0, e1, e2,
+def far_kernel(live_ref, small_ref, v1_ref, v2_ref, ga, gb, gc, gd, data_ref, node_ref, e0, e1, e2,
                out_ref, trace_ref, ext_ref, d0, d1, d2, lhs_ref, turn_ref):
-    b = b_ref[...]
+    b = small_ref[B_ROWS, :]
     v1 = v1_ref[...]
     v2 = v2_ref[...]
     ext_ref[...] = extend(v2, [ga, gb, gc, gd])
 
     def energy_block(t, total):
-        _, field = element_gradient(ext_ref[...], conn_ref, grad_ref, turn_ref, t)
-        return total + block_volume(vol_ref, t) * (
+        _, _, volume, field = element_gradient(ext_ref[...], data_ref, turn_ref, t)
+        return total + volume * (
             field[0] * field[0] + field[1] * field[1] + field[2] * field[2]
         )
 
     energy = lax.fori_loop(0, live_ref[0], energy_block, jnp.zeros((8, LANES), F32))
-    products = [b * b, b * v1, v1 * v1, v1 * v2, v2 * v2, mass_ref[...] * v2 * v2]
+    products = [b * b, b * v1, v1 * v1, v1 * v2, v2 * v2, small_ref[MASS_ROWS, :] * v2 * v2]
     sums = [p[0:8] + p[8:16] for p in products]
     sums[5] = (sums[5] + energy) * SCALE
     sub = lax.broadcasted_iota(jnp.int32, (8, LANES), 0)
@@ -333,7 +333,7 @@
         out_ref[pl.ds(j, TGT_ROWS, stride=4), :] = out
 
 
-def final_kernel(got_ref, b_ref, v1_ref, v2_ref, trace_ref, pot_ref, dir_ref):
+def final_kernel(got_ref, small_ref, v1_ref, v2_ref, trace_ref, pot_ref, dir_ref):
     total = jnp.sum(got_ref[...], axis=0, keepdims=True)
     lane = lax.broadcasted_iota(jnp.int32, (1, LANES), 1)
     m = [jnp.sum(jnp.where(lane == 96 + k, total, 0.0), axis=1, keepdims=True) for k in range(6)]
@@ -355,7 +355,7 @@
     c0 = c0 * SCALE
     c1 = c1 * SCALE
     c2 = c2 * SCALE
-    pot_ref[...] = c0 * b_ref[...] + c1 * v1_ref[...] + c2 * v2_ref[...]
+    pot_ref[...] = c0 * small_ref[B_ROWS, :] + c1 * v1_ref[...] + c2 * v2_ref[...]
     out = jnp.zeros((1, LANES), F32)
     for k, c in enumerate((c0, c1, c2)):
         part = total
@@ -381,7 +381,7 @@
 
 
 PIECE = (2, LANES)
-TURN = pltpu.VMEM((72, LANES), F32)
+TURN = pltpu.VMEM((128, LANES), F32)
 
 
 def swap_partners(rows, cols, axis, second):
@@ -415,25 +415,24 @@
 
 def per_device(connectivity, gradients, volumes, live_blocks, send_lists, divergence, mass_shift,
                boundary_nodes, surface_points, normal_cos, normal_angle, node_areas):
-    conn = connectivity.reshape(4, ELEM_ROWS, LANES).transpose(1, 0, 2).reshape(4 * ELEM_ROWS, LANES)
-    vol = volumes.reshape(ELEM_ROWS, LANES)
     lists = send_lists.reshape(4, 2, LANES).transpose(1, 0, 2).reshape(8, LANES)
-    b = divergence.reshape(OWN_ROWS, LANES)
-    mass = mass_shift.reshape(OWN_ROWS, LANES)
     nodes = jnp.pad(boundary_nodes, (0, 8 * LANES - SLOTS)).reshape(8, LANES)
-    elements = (conn, gradients, vol)
-
-    mine, b, lists, *pieces = call(
+    gap = jnp.zeros(PAD_SLOTS - SLOTS, F32)
+    small = jnp.concatenate([
+        divergence, mass_shift, normal_cos, gap, normal_angle, gap, node_areas, gap,
+    ]).reshape(-1, LANES)
+    data = jnp.concatenate([gradients, connectivity.astype(F32), volumes[None]], axis=0)
+    mine, lists, points, *pieces = call(
         pick_kernel,
-        [(N_DEV, LANES), b.shape, jax.ShapeDtypeStruct(lists.shape, lists.dtype)] + [PIECE] * 4,
-        (b, lists, surface_points),
+        [(N_DEV, LANES), jax.ShapeDtypeStruct(lists.shape, lists.dtype), surface_points.shape] + [PIECE] * 4,
+        (small, lists, surface_points),
     )
     targets = lax.all_to_all(mine, ("row", "col"), 0, 0, tiled=True)
     prepared = None
     chunks = []
 
     def fill():
-        nonlocal prepared, mass
+        nonlocal prepared
         if prepared is None:
             prepared = call(
                 prepare_kernel,
@@ -442,11 +441,9 @@
                     jax.ShapeDtypeStruct((SLOTS, KDIM), BF16),
                     jax.ShapeDtypeStruct((KDIM, TGT_ROWS * LANES), BF16),
                     (3, TGT_ROWS, LANES),
-                    mass.shape,
                 ],
-                (surface_points, normal_cos, normal_angle, node_areas, mass, targets),
+                (small, points, targets),
             )
-            *prepared, mass = prepared
             return
         done = len(chunks)
         base = sum(CHUNKS[:done])
@@ -462,24 +459,24 @@
             fill()
         return out
 
-    vectors = [b]
+    vectors = [small]
     for step in range(2):
         ghosts = swap(2 * step, pieces)
         own, *back = call(
             apply_kernel, [(OWN_ROWS, LANES)] + [PIECE] * 4,
-            (live_blocks, vectors[-1], *ghosts, *elements), smem=1,
+            (live_blocks, vectors[-1], *ghosts, data), smem=1,
             scratch=[pltpu.VMEM((EXT_ROWS, LANES), F32), pltpu.VMEM((HIGH_ROWS, LANES), F32), TURN],
         )
         returned = swap(2 * step + 1, back)
         new, *pieces = call(
             combine_kernel, [(OWN_ROWS, LANES)] + [PIECE] * 4,
-            (own, *returned, lists, vectors[-1], mass),
+            (own, *returned, lists, vectors[-1], small),
         )
         vectors.append(new)
     ghosts = swap(4, pieces)
     partial, trace = call(
         far_kernel, [(N_DEV, LANES), (3, 8, LANES)],
-        (live_blocks, *vectors, *ghosts, *elements, mass, nodes, *chunks), smem=1,
+        (live_blocks, *vectors, *ghosts, data, nodes, *chunks), smem=1,
         scratch=[pltpu.VMEM((EXT_ROWS, LANES), F32)]
         + [pltpu.VMEM((TGT_ROWS, LANES), F32)] * 3
         + [pltpu.VMEM((8, PAD_SLOTS), BF16), TURN],

time: 97.9 us -> 93.2 us (0.952)
  local copies, waits for them, and re-layouts: 10.9 us -> 2.21 us
  blocking collectives: 26 us -> 28.1 us
  other arithmetic: 0 us -> 2.09 us
    unnamed x36 -> x6, local copies, waits for them, and re-layouts: 10.9 us -> 1.38 us
    all_to_all x1, blocking collectives: 26 us -> 28.1 us  [per_device(): got = lax.all_to_all(partial, ('row', 'col'), 0, 0, tiled=True)]
    concatenate x0 -> x1, other arithmetic: none -> 1.16 us  [per_device(): jnp.concatenate([gradients, connectivity.astype(F32), volumes[None]], axi...]
  transfers between devices with their start and end apart: 21 -> 21, of which waited for: 5 -> 3; matrix products, arithmetic and copies ran while one was open for 0% -> 2% of each run, Pallas kernels for 9% -> 13%
where the time goes in v5:
time: 93.2 us; the launch traced here: 92.9 us
  starting transfers between devices  39.6 us (42%)
  blocking collectives  28.1 us (30%)
  Pallas kernels  15.5 us (17%)
  waiting for transfers between devices  3.86 us (4%)
  local copies, waits for them, and re-layouts  2.21 us (2%)
  other arithmetic  2.09 us (2%)
  between operations  1.47 us (2%)
    all_to_all x1, blocking collectives, per_device(): got = lax.all_to_all(partial, ('row', 'col'), 0, 0, tiled=True)  28.1 us
    ppermute x20, starting transfers between devices, exchange(): lax.ppermute(pieces[k], ('row', 'col'), swap_partners(rows, cols, axis, k...  23.9 us
    all_to_all x1, starting transfers between devices, per_device(): targets = lax.all_to_all(mine, ('row', 'col'), 0, 0, tiled=True)  15.6 us
    pallas_call x11, Pallas kernels, call(): pl.pallas_call(body, out_shape=out_shapes, in_specs=specs, out_specs=[pl....  15.5 us
    ppermute x20, waiting for transfers between devices, exchange(): lax.ppermute(pieces[k], ('row', 'col'), swap_partners(rows, cols, axis, k...  3.86 us
  transfers between devices with their start and end apart: 21, of which 3 were waited for; matrix products, arithmetic and copies ran while one was open for 2% of the time, Pallas kernels for 13%

profile of v5, /device:TPU:1, one launch (start us, length us, event | category | flops | bytes accessed | tf_op | source)
XLA Modules:
  0.0 92.9 jit_solution(13993480566015539699)
XLA Ops:
  3.6 15.6 %all-to-all-start = ((f32[256,1,128]{2,1,0:T(1,128)}), f32[256,1,128]{2,1,0:T(1,128)S(1)}, u32[]{:S(2)}, u32[]{:S(2)}) async-start(f32[256,1,128]{2,1,0:T(1,128)} %bitcast.7), calls=%async_computation | async-start | bytes 262144 | tf_op jit(solution)/shard_map/all_to_all | solution.py:430
  19.3 2.2 %collective-permute-start = (f32[2,128]{1,0:T(2,128)S(1)}, f32[2,128]{1,0:T(2,128)S(1)}, u32[]{:S(2)}, u32[]{:S(2)}) collective-permute-start(f32[2,128]{1,0:T(2,128)S(1)} %get-tuple-element.37), channel_id=1, source_target_pairs={{0,32},{1,33},{2,34},{3,35},{4,36},{5,37},{6,38},{7,39},{8,40},{9,... | collective-permute-start | bytes 3080 | tf_op jit(solution)/shard_map/ppermute | solution.py:412
  21.5 0.9 collective-permute-start.2
  22.4 1.2 %collective-permute-start.3 = (f32[2,128]{1,0:T(2,128)S(1)}, f32[2,128]{1,0:T(2,128)S(1)}, u32[]{:S(2)}, u32[]{:S(2)}) collective-permute-start(f32[2,128]{1,0:T(2,128)S(1)} %get-tuple-element.40), channel_id=1, source_target_pairs={{0,32},{1,2},{2,1},{3,4},{4,3},{5,6},{6,5},{7,8},{8,7},{9,10},{10,... | collective-permute-start | bytes 3080 | tf_op jit(solution)/shard_map/ppermute | solution.py:412
  24.6 1.2 %pad_maximum_fusion.data_ref = f32[14,8192]{1,0:T(8,128)S(1)} fusion(f32[1,8192]{1,0:T(1,128)} %bitcast.31, f32[4,8192]{1,0:T(4,128)S(1)} %convert_element_type.3, f32[9,8192]{1,0:T(8,128)} %param.13), kind=kLoop, calls=%fused_computation | loop fusion | flops 229376 | bytes 917504 | tf_op jit(solution)/shard_map/concatenate | solution.py:424
  26.4 2.5 %shard_map.132 = (f32[16,128]{1,0:T(8,128)S(1)}, f32[2,128]{1,0:T(2,128)S(1)}, f32[2,128]{1,0:T(2,128)S(1)}, f32[2,128]{1,0:T(2,128)S(1)}, f32[2,128]{1,0:T(2,128)S(1)}) custom-call(s32[1]{0:T(128)S(6)} %copy.18.live_ref, f32[41,128]{1,0:T(8,128)S(1)} %bitcast.20, f32[2,128]{1,0:T(2,128)S(1)} %collective-permute-done.ga, ...), custom_call_target="tpu_custom_call" | custom-call | flops 2000000 | bytes 1048576 | tf_op jit(solution)/shard_map/pallas_call | solution.py:372
  30.6 1.2 %collective-permute-start.7 = (f32[2,128]{1,0:T(2,128)S(1)}, f32[2,128]{1,0:T(2,128)S(1)}, u32[]{:S(2)}, u32[]{:S(2)}) collective-permute-start(f32[2,128]{1,0:T(2,128)S(1)} %get-tuple-element.45), channel_id=1, source_target_pairs={{0,32},{1,2},{2,1},{3,4},{4,3},{5,6},{6,5},{7,8},{8,7},{9,10},{10,... | collective-permute-start | bytes 3080 | tf_op jit(solution)/shard_map/ppermute | solution.py:412
  31.9 1.1 %collective-permute-done.5.rb = f32[2,128]{1,0:T(2,128)S(1)} collective-permute-done((f32[2,128]{1,0:T(2,128)S(1)}, f32[2,128]{1,0:T(2,128)S(1)}, u32[]{:S(2)}, u32[]{:S(2)}) %collective-permute-start.5) | collective-permute-done | bytes 1056 | tf_op jit(solution)/shard_map/ppermute | solution.py:412
  33.4 2.7 %collective-permute-start.10 = (f32[2,128]{1,0:T(2,128)S(1)}, f32[2,128]{1,0:T(2,128)S(1)}, u32[]{:S(2)}, u32[]{:S(2)}) collective-permute-start(f32[2,128]{1,0:T(2,128)S(1)} %get-tuple-element.50), channel_id=1, source_target_pairs={{0,1},{1,0},{2,3},{3,2},{4,5},{5,4},{6,7},{7,6},{8,9},{9,8},{10,11... | collective-permute-start | bytes 3080 | tf_op jit(solution)/shard_map/ppermute | solution.py:412
  36.0 1.3 %collective-permute-start.11 = (f32[2,128]{1,0:T(2,128)S(1)}, f32[2,128]{1,0:T(2,128)S(1)}, u32[]{:S(2)}, u32[]{:S(2)}) collective-permute-start(f32[2,128]{1,0:T(2,128)S(1)} %get-tuple-element.51), channel_id=1, source_target_pairs={{0,32},{1,2},{2,1},{3,4},{4,3},{5,6},{6,5},{7,8},{8,7},{9,10},{10,... | collective-permute-start | bytes 3080 | tf_op jit(solution)/shard_map/ppermute | solution.py:412
  37.3 1.5 %collective-permute-start.9 = (f32[2,128]{1,0:T(2,128)S(1)}, f32[2,128]{1,0:T(2,128)S(1)}, u32[]{:S(2)}, u32[]{:S(2)}) collective-permute-start(f32[2,128]{1,0:T(2,128)S(1)} %get-tuple-element.49), channel_id=1, source_target_pairs={{0,1},{1,0},{2,3},{3,2},{4,5},{5,4},{6,7},{7,6},{8,9},{9,8},{10,11... | collective-permute-start | bytes 3080 | tf_op jit(solution)/shard_map/ppermute | solution.py:412
  38.8 1.5 %collective-permute-done.9.gb = f32[2,128]{1,0:T(2,128)S(1)} collective-permute-done((f32[2,128]{1,0:T(2,128)S(1)}, f32[2,128]{1,0:T(2,128)S(1)}, u32[]{:S(2)}, u32[]{:S(2)}) %collective-permute-start.9) | collective-permute-done | bytes 1056 | tf_op jit(solution)/shard_map/ppermute | solution.py:412
  40.3 2.4 %shard_map.134 = (f32[16,128]{1,0:T(8,128)S(1)}, f32[2,128]{1,0:T(2,128)S(1)}, f32[2,128]{1,0:T(2,128)S(1)}, f32[2,128]{1,0:T(2,128)S(1)}, f32[2,128]{1,0:T(2,128)S(1)}) custom-call(s32[1]{0:T(128)S(6)} %copy.18.live_ref, f32[16,128]{1,0:T(8,128)S(1)} %get-tuple-element.47.v_ref.v1_ref, f32[2,128]{1,0:T(2,128)S(1)} %collective-permute-done.8.ga, ...), custom_call_target="tpu_custom_call" | custom-call | flops 2000000 | bytes 1048576 | tf_op jit(solution)/shard_map/pallas_call | solution.py:372
  42.8 4.6 %collective-permute-start.12 = (f32[2,128]{1,0:T(2,128)S(1)}, f32[2,128]{1,0:T(2,128)S(1)}, u32[]{:S(2)}, u32[]{:S(2)}) collective-permute-start(f32[2,128]{1,0:T(2,128)S(1)} %get-tuple-element.53), channel_id=1, source_target_pairs={{0,32},{1,33},{2,34},{3,35},{4,36},{5,37},{6,38},{7,39},{8,40},{9,... | collective-permute-start | bytes 3080 | tf_op jit(solution)/shard_map/ppermute | solution.py:412
  48.1 1.3 %collective-permute-start.15 = (f32[2,128]{1,0:T(2,128)S(1)}, f32[2,128]{1,0:T(2,128)S(1)}, u32[]{:S(2)}, u32[]{:S(2)}) collective-permute-start(f32[2,128]{1,0:T(2,128)S(1)} %get-tuple-element.56), channel_id=1, source_target_pairs={{0,32},{1,2},{2,1},{3,4},{4,3},{5,6},{6,5},{7,8},{8,7},{9,10},{10,... | collective-permute-start | bytes 3080 | tf_op jit(solution)/shard_map/ppermute | solution.py:412
  49.5 1.1 %collective-permute-done.13.rb = f32[2,128]{1,0:T(2,128)S(1)} collective-permute-done((f32[2,128]{1,0:T(2,128)S(1)}, f32[2,128]{1,0:T(2,128)S(1)}, u32[]{:S(2)}, u32[]{:S(2)}) %collective-permute-start.13) | collective-permute-done | bytes 1056 | tf_op jit(solution)/shard_map/ppermute | solution.py:412
  51.5 1.8 %collective-permute-start.17 = (f32[2,128]{1,0:T(2,128)S(1)}, f32[2,128]{1,0:T(2,128)S(1)}, u32[]{:S(2)}, u32[]{:S(2)}) collective-permute-start(f32[2,128]{1,0:T(2,128)S(1)} %get-tuple-element.59), channel_id=1, source_target_pairs={{0,1},{1,0},{2,3},{3,2},{4,5},{5,4},{6,7},{7,6},{8,9},{9,8},{10,11... | collective-permute-start | bytes 3080 | tf_op jit(solution)/shard_map/ppermute | solution.py:412
  53.3 2.0 %collective-permute-start.18 = (f32[2,128]{1,0:T(2,128)S(1)}, f32[2,128]{1,0:T(2,128)S(1)}, u32[]{:S(2)}, u32[]{:S(2)}) collective-permute-start(f32[2,128]{1,0:T(2,128)S(1)} %get-tuple-element.60), channel_id=1, source_target_pairs={{0,1},{1,0},{2,3},{3,2},{4,5},{5,4},{6,7},{7,6},{8,9},{9,8},{10,11... | collective-permute-start | bytes 3080 | tf_op jit(solution)/shard_map/ppermute | solution.py:412
  55.4 0.9 %shard_map.136 = (f32[6,320,128]{2,1,0:T(8,128)S(1)}, bf16[320,32]{1,0:T(8,128)(2,1)S(1)}, bf16[32,8192]{1,0:T(8,128)(2,1)S(1)}, f32[3,64,128]{2,1,0:T(8,128)S(1)}) custom-call(f32[41,128]{1,0:T(8,128)S(1)} %bitcast.24, f32[3,320]{1,0:T(4,128)S(1)} %get-tuple-element.62.point_ref, f32[256,128]{1,0:T(8,128)S(1)} %bitcast.27), custom_call_target="tpu_custom_call" | custom-call | flops 2000000 | bytes 1048576 | tf_op jit(solution)/shard_map/pallas_call | solution.py:372
  56.3 1.8 %shard_map.139.e2 = bf16[320,2560]{1,0:T(8,128)(2,1)S(1)} custom-call(f32[6,320,128]{2,1,0:T(8,128)S(1)} %get-tuple-element.64.refs_0_, bf16[320,32]{1,0:T(8,128)(2,1)S(1)} %get-tuple-element.65.refs_1_, bf16[32,8192]{1,0:T(8,128)(2,1)S(1)} %get-tuple-element.66.refs_2_, f32[3,64,128]{2,1,0:T(8,128)S(1)} %get-tuple-element.67.refs_3_), custom_call_target="tpu_custom_call" | custom-call | flops 2000000 | bytes 1048576 | tf_op jit(solution)/shard_map/pallas_call | solution.py:372
  58.1 2.2 %shard_map.138.e1 = bf16[320,3072]{1,0:T(8,128)(2,1)S(1)} custom-call(f32[6,320,128]{2,1,0:T(8,128)S(1)} %get-tuple-element.64.refs_0_, bf16[320,32]{1,0:T(8,128)(2,1)S(1)} %get-tuple-element.65.refs_1_, bf16[32,8192]{1,0:T(8,128)(2,1)S(1)} %get-tuple-element.66.refs_2_, f32[3,64,128]{2,1,0:T(8,128)S(1)} %get-tuple-element.67.refs_3_), custom_call_target="tpu_custom_call" | custom-call | flops 2000000 | bytes 1048576 | tf_op jit(solution)/shard_map/pallas_call | solution.py:372
  60.4 1.8 %shard_map.137.e0 = bf16[320,2560]{1,0:T(8,128)(2,1)S(1)} custom-call(f32[6,320,128]{2,1,0:T(8,128)S(1)} %get-tuple-element.64.refs_0_, bf16[320,32]{1,0:T(8,128)(2,1)S(1)} %get-tuple-element.65.refs_1_, bf16[32,8192]{1,0:T(8,128)(2,1)S(1)} %get-tuple-element.66.refs_2_, f32[3,64,128]{2,1,0:T(8,128)S(1)} %get-tuple-element.67.refs_3_), custom_call_target="tpu_custom_call" | custom-call | flops 2000000 | bytes 1048576 | tf_op jit(solution)/shard_map/pallas_call | solution.py:372
  62.2 1.8 %shard_map.140 = (f32[256,128]{1,0:T(8,128)S(1)}, f32[3,8,128]{2,1,0:T(8,128)S(1)}) custom-call(s32[1]{0:T(128)S(6)} %copy.18.live_ref, f32[41,128]{1,0:T(8,128)S(1)} %bitcast.25, f32[16,128]{1,0:T(8,128)S(1)} %get-tuple-element.47.v_ref.v1_ref, f32[16,128]{1,0:T(8,128)S(1)} %get-tuple-element.57.v2_ref, f32[2,128]{1,0:T(2,128)S(1)} %collective-permute-done.16.ga, ...), custom_call_target="tpu_custom_call" | custom-call | flops 2000000 | bytes 1048576 | tf_op jit(solution)/shard_map/pallas_call | solution.py:372
  64.0 28.1 %all_to_all.22 = f32[256,1,128]{2,1,0:T(1,128)S(1)} all-to-all(f32[256,1,128]{2,1,0:T(1,128)S(1)} %bitcast.29), channel_id=1, replica_groups=mesh['row'=8,'col'=32] {'row','col'}, dimensions={0} | all-to-all | bytes 262144 | tf_op jit(solution)/shard_map/all_to_all | solution.py:484
  (41 shorter events, 8.4 us)
Async XLA Ops:
  0.6 48.8 %copy-start.2 = (s32[320]{0:T(512)S(1)}, s32[320]{0:T(512)}, u32[]{:S(2)}) copy-start(s32[320]{0:T(512)} %param.19) | copy-start | bytes 3844
  1.5 0.7 copy-start
  2.2 0.7 copy-start.1
  3.6 51.8 %all-to-all-start = ((f32[256,1,128]{2,1,0:T(1,128)}), f32[256,1,128]{2,1,0:T(1,128)S(1)}, u32[]{:S(2)}, u32[]{:S(2)}) async-start(f32[256,1,128]{2,1,0:T(1,128)} %bitcast.7), calls=%async_computation | async-start | bytes 262144 | tf_op jit(solution)/shard_map/all_to_all | solution.py:430
  19.3 7.1 %collective-permute-start = (f32[2,128]{1,0:T(2,128)S(1)}, f32[2,128]{1,0:T(2,128)S(1)}, u32[]{:S(2)}, u32[]{:S(2)}) collective-permute-start(f32[2,128]{1,0:T(2,128)S(1)} %get-tuple-element.37), channel_id=1, source_target_pairs={{0,32},{1,33},{2,34},{3,35},{4,36},{5,37},{6,38},{7,39},{8,40},{9,... | collective-permute-start | bytes 3080 | tf_op jit(solution)/shard_map/ppermute | solution.py:412
  21.5 4.9 %collective-permute-start.1 = (f32[2,128]{1,0:T(2,128)S(1)}, f32[2,128]{1,0:T(2,128)S(1)}, u32[]{:S(2)}, u32[]{:S(2)}) collective-permute-start(f32[2,128]{1,0:T(2,128)S(1)} %get-tuple-element.38), channel_id=1, source_target_pairs={{0,1},{1,0},{2,3},{3,2},{4,5},{5,4},{6,7},{7,6},{8,9},{9,8},{10,11... | collective-permute-start | bytes 3080 | tf_op jit(solution)/shard_map/ppermute | solution.py:412
  21.5 4.9 %collective-permute-start.2 = (f32[2,128]{1,0:T(2,128)S(1)}, f32[2,128]{1,0:T(2,128)S(1)}, u32[]{:S(2)}, u32[]{:S(2)}) collective-permute-start(f32[2,128]{1,0:T(2,128)S(1)} %get-tuple-element.39), channel_id=1, source_target_pairs={{0,1},{1,0},{2,3},{3,2},{4,5},{5,4},{6,7},{7,6},{8,9},{9,8},{10,11... | collective-permute-start | bytes 3080 | tf_op jit(solution)/shard_map/ppermute | solution.py:412
  22.4 4.0 %collective-permute-start.3 = (f32[2,128]{1,0:T(2,128)S(1)}, f32[2,128]{1,0:T(2,128)S(1)}, u32[]{:S(2)}, u32[]{:S(2)}) collective-permute-start(f32[2,128]{1,0:T(2,128)S(1)} %get-tuple-element.40), channel_id=1, source_target_pairs={{0,32},{1,2},{2,1},{3,4},{4,3},{5,6},{6,5},{7,8},{8,7},{9,10},{10,... | collective-permute-start | bytes 3080 | tf_op jit(solution)/shard_map/ppermute | solution.py:412
  28.9 3.0 %collective-permute-start.4 = (f32[2,128]{1,0:T(2,128)S(1)}, f32[2,128]{1,0:T(2,128)S(1)}, u32[]{:S(2)}, u32[]{:S(2)}) collective-permute-start(f32[2,128]{1,0:T(2,128)S(1)} %get-tuple-element.42), channel_id=1, source_target_pairs={{0,32},{1,33},{2,34},{3,35},{4,36},{5,37},{6,38},{7,39},{8,40},{9,... | collective-permute-start | bytes 3080 | tf_op jit(solution)/shard_map/ppermute | solution.py:412
  29.8 3.3 %collective-permute-start.5 = (f32[2,128]{1,0:T(2,128)S(1)}, f32[2,128]{1,0:T(2,128)S(1)}, u32[]{:S(2)}, u32[]{:S(2)}) collective-permute-start(f32[2,128]{1,0:T(2,128)S(1)} %get-tuple-element.43), channel_id=1, source_target_pairs={{0,1},{1,0},{2,3},{3,2},{4,5},{5,4},{6,7},{7,6},{8,9},{9,8},{10,11... | collective-permute-start | bytes 3080 | tf_op jit(solution)/shard_map/ppermute | solution.py:412
  29.8 3.3 %collective-permute-start.6 = (f32[2,128]{1,0:T(2,128)S(1)}, f32[2,128]{1,0:T(2,128)S(1)}, u32[]{:S(2)}, u32[]{:S(2)}) collective-permute-start(f32[2,128]{1,0:T(2,128)S(1)} %get-tuple-element.44), channel_id=1, source_target_pairs={{0,1},{1,0},{2,3},{3,2},{4,5},{5,4},{6,7},{7,6},{8,9},{9,8},{10,11... | collective-permute-start | bytes 3080 | tf_op jit(solution)/shard_map/ppermute | solution.py:412
  30.6 2.4 %collective-permute-start.7 = (f32[2,128]{1,0:T(2,128)S(1)}, f32[2,128]{1,0:T(2,128)S(1)}, u32[]{:S(2)}, u32[]{:S(2)}) collective-permute-start(f32[2,128]{1,0:T(2,128)S(1)} %get-tuple-element.45), channel_id=1, source_target_pairs={{0,32},{1,2},{2,1},{3,4},{4,3},{5,6},{6,5},{7,8},{8,7},{9,10},{10,... | collective-permute-start | bytes 3080 | tf_op jit(solution)/shard_map/ppermute | solution.py:412
  33.4 5.4 %collective-permute-start.10 = (f32[2,128]{1,0:T(2,128)S(1)}, f32[2,128]{1,0:T(2,128)S(1)}, u32[]{:S(2)}, u32[]{:S(2)}) collective-permute-start(f32[2,128]{1,0:T(2,128)S(1)} %get-tuple-element.50), channel_id=1, source_target_pairs={{0,1},{1,0},{2,3},{3,2},{4,5},{5,4},{6,7},{7,6},{8,9},{9,8},{10,11... | collective-permute-start | bytes 3080 | tf_op jit(solution)/shard_map/ppermute | solution.py:412
  36.0 2.8 %collective-permute-start.11 = (f32[2,128]{1,0:T(2,128)S(1)}, f32[2,128]{1,0:T(2,128)S(1)}, u32[]{:S(2)}, u32[]{:S(2)}) collective-permute-start(f32[2,128]{1,0:T(2,128)S(1)} %get-tuple-element.51), channel_id=1, source_target_pairs={{0,32},{1,2},{2,1},{3,4},{4,3},{5,6},{6,5},{7,8},{8,7},{9,10},{10,... | collective-permute-start | bytes 3080 | tf_op jit(solution)/shard_map/ppermute | solution.py:412
  37.3 1.5 %collective-permute-start.8 = (f32[2,128]{1,0:T(2,128)S(1)}, f32[2,128]{1,0:T(2,128)S(1)}, u32[]{:S(2)}, u32[]{:S(2)}) collective-permute-start(f32[2,128]{1,0:T(2,128)S(1)} %get-tuple-element.48), channel_id=1, source_target_pairs={{0,32},{1,33},{2,34},{3,35},{4,36},{5,37},{6,38},{7,39},{8,40},{9,... | collective-permute-start | bytes 3080 | tf_op jit(solution)/shard_map/ppermute | solution.py:412
  37.3 3.0 %collective-permute-start.9 = (f32[2,128]{1,0:T(2,128)S(1)}, f32[2,128]{1,0:T(2,128)S(1)}, u32[]{:S(2)}, u32[]{:S(2)}) collective-permute-start(f32[2,128]{1,0:T(2,128)S(1)} %get-tuple-element.49), channel_id=1, source_target_pairs={{0,1},{1,0},{2,3},{3,2},{4,5},{5,4},{6,7},{7,6},{8,9},{9,8},{10,11... | collective-permute-start | bytes 3080 | tf_op jit(solution)/shard_map/ppermute | solution.py:412
  42.8 6.7 %collective-permute-start.12 = (f32[2,128]{1,0:T(2,128)S(1)}, f32[2,128]{1,0:T(2,128)S(1)}, u32[]{:S(2)}, u32[]{:S(2)}) collective-permute-start(f32[2,128]{1,0:T(2,128)S(1)} %get-tuple-element.53), channel_id=1, source_target_pairs={{0,32},{1,33},{2,34},{3,35},{4,36},{5,37},{6,38},{7,39},{8,40},{9,... | collective-permute-start | bytes 3080 | tf_op jit(solution)/shard_map/ppermute | solution.py:412
  47.3 3.3 %collective-permute-start.13 = (f32[2,128]{1,0:T(2,128)S(1)}, f32[2,128]{1,0:T(2,128)S(1)}, u32[]{:S(2)}, u32[]{:S(2)}) collective-permute-start(f32[2,128]{1,0:T(2,128)S(1)} %get-tuple-element.54), channel_id=1, source_target_pairs={{0,1},{1,0},{2,3},{3,2},{4,5},{5,4},{6,7},{7,6},{8,9},{9,8},{10,11... | collective-permute-start | bytes 3080 | tf_op jit(solution)/shard_map/ppermute | solution.py:412
  47.3 3.3 %collective-permute-start.14 = (f32[2,128]{1,0:T(2,128)S(1)}, f32[2,128]{1,0:T(2,128)S(1)}, u32[]{:S(2)}, u32[]{:S(2)}) collective-permute-start(f32[2,128]{1,0:T(2,128)S(1)} %get-tuple-element.55), channel_id=1, source_target_pairs={{0,1},{1,0},{2,3},{3,2},{4,5},{5,4},{6,7},{7,6},{8,9},{9,8},{10,11... | collective-permute-start | bytes 3080 | tf_op jit(solution)/shard_map/ppermute | solution.py:412
  48.1 2.5 %collective-permute-start.15 = (f32[2,128]{1,0:T(2,128)S(1)}, f32[2,128]{1,0:T(2,128)S(1)}, u32[]{:S(2)}, u32[]{:S(2)}) collective-permute-start(f32[2,128]{1,0:T(2,128)S(1)} %get-tuple-element.56), channel_id=1, source_target_pairs={{0,32},{1,2},{2,1},{3,4},{4,3},{5,6},{6,5},{7,8},{8,7},{9,10},{10,... | collective-permute-start | bytes 3080 | tf_op jit(solution)/shard_map/ppermute | solution.py:412
  50.9 11.3 %collective-permute-start.16 = (f32[2,128]{1,0:T(2,128)S(1)}, f32[2,128]{1,0:T(2,128)S(1)}, u32[]{:S(2)}, u32[]{:S(2)}) collective-permute-start(f32[2,128]{1,0:T(2,128)S(1)} %get-tuple-element.58), channel_id=1, source_target_pairs={{0,32},{1,33},{2,34},{3,35},{4,36},{5,37},{6,38},{7,39},{8,40},{9,... | collective-permute-start | bytes 3080 | tf_op jit(solution)/shard_map/ppermute | solution.py:412
  51.5 10.7 %collective-permute-start.17 = (f32[2,128]{1,0:T(2,128)S(1)}, f32[2,128]{1,0:T(2,128)S(1)}, u32[]{:S(2)}, u32[]{:S(2)}) collective-permute-start(f32[2,128]{1,0:T(2,128)S(1)} %get-tuple-element.59), channel_id=1, source_target_pairs={{0,1},{1,0},{2,3},{3,2},{4,5},{5,4},{6,7},{7,6},{8,9},{9,8},{10,11... | collective-permute-start | bytes 3080 | tf_op jit(solution)/shard_map/ppermute | solution.py:412
  53.3 8.9 %collective-permute-start.18 = (f32[2,128]{1,0:T(2,128)S(1)}, f32[2,128]{1,0:T(2,128)S(1)}, u32[]{:S(2)}, u32[]{:S(2)}) collective-permute-start(f32[2,128]{1,0:T(2,128)S(1)} %get-tuple-element.60), channel_id=1, source_target_pairs={{0,1},{1,0},{2,3},{3,2},{4,5},{5,4},{6,7},{7,6},{8,9},{9,8},{10,11... | collective-permute-start | bytes 3080 | tf_op jit(solution)/shard_map/ppermute | solution.py:412
  55.4 6.9 %collective-permute-start.19 = (f32[2,128]{1,0:T(2,128)S(1)}, f32[2,128]{1,0:T(2,128)S(1)}, u32[]{:S(2)}, u32[]{:S(2)}) collective-permute-start(f32[2,128]{1,0:T(2,128)S(1)} %get-tuple-element.61), channel_id=1, source_target_pairs={{0,32},{1,2},{2,1},{3,4},{4,3},{5,6},{6,5},{7,8},{8,7},{9,10},{10,... | collective-permute-start | bytes 3080 | tf_op jit(solution)/shard_map/ppermute | solution.py:412

commit v6 on v5

--- a/solution.py
+++ b/solution.py
@@ -13,6 +13,7 @@
 LANES = 128
 NN_DEV = 2048
 EBLK = 1024
+BLOCKS = 8
 GH = 256
 TGT_DEV = 32
 OWN_ROWS = NN_DEV // LANES
@@ -25,7 +26,7 @@
 CHUNKS = (20, 24, 20)
 GROUP = 4
 KDIM = 32
-SPLITS = 3
+SPLITS = 2
 SCALE = 1.0 / 64.0
 B_ROWS = slice(0, 16)
 MASS_ROWS = slice(16, 32)
@@ -47,7 +48,7 @@
     return out
 
 
-def split_terms(terms, count=SPLITS):
+def split_terms(terms, count):
     parts = []
     for _ in range(count):
         parts.append(terms.astype(BF16))
@@ -64,7 +65,7 @@
     zero_rows = jnp.zeros((rows, LANES), BF16)
     low = (index & 127).astype(F32)
     high = (index >> 7).astype(F32)
-    parts = [p.astype(F32) for p in split_terms(terms)]
+    parts = [p.astype(F32) for p in split_terms(terms, SPLITS)]
     hot_blocks = []
     weight_blocks = []
     for s in range(8):
@@ -167,21 +168,28 @@
     ext_ref[...] = extend(v_ref[0:OWN_ROWS, :], [ga, gb, gc, gd])
     acc_ref[...] = jnp.zeros_like(acc_ref)
 
-    def element_block(t, carry):
-        grads, index, volume, field = element_gradient(ext_ref[...], data_ref, turn_ref, t)
+    def element_terms(t):
+        grads, index, volume, field = element_gradient(
+            ext_ref[...], data_ref, turn_ref, jnp.minimum(t, BLOCKS - 1)
+        )
         field = [volume * f for f in field]
         terms = [
             grads[3 * a] * field[0] + grads[3 * a + 1] * field[1] + grads[3 * a + 2] * field[2]
             for a in range(3)
         ]
         terms.append(-(terms[0] + terms[1] + terms[2]))
+        return tuple(index), tuple(terms)
+
+    def element_block(t, carry):
+        index, terms = carry
+        following = element_terms(t + 1)
         total = acc_ref[...]
         for a in range(4):
             total = total + scatter_block(index[a], terms[a], EXT_ROWS)
         acc_ref[...] = total
-        return carry
-
-    lax.fori_loop(0, live_ref[0], element_block, 0)
+        return following
+
+    lax.fori_loop(0, live_ref[0], element_block, element_terms(0))
     own_ref[...] = acc_ref[0:OWN_ROWS, :]
     down, up, left, right = [
         acc_ref[OWN_ROWS + 2 * d:OWN_ROWS + 2 * d + 2, :] for d in range(4)
@@ -232,10 +240,10 @@
         ones = jnp.ones_like(norm)
         lines = []
         for p in points:
-            a = [q.astype(F32) for q in split_terms(p * scale)]
+            a = [q.astype(F32) for q in split_terms(p * scale, 3)]
             order = (0, 1, 0, 1, 2, 0) if swap else (0, 0, 1, 1, 0, 2)
             lines += [a[k] for k in order]
-        norms = [q.astype(F32) for q in split_terms(norm)]
+        norms = [q.astype(F32) for q in split_terms(norm, 3)]
         lines += [ones] * 3 + norms if swap else norms + [ones] * 3
         return lines
 
@@ -273,23 +281,35 @@
     lax.fori_loop(0, entry_ref.shape[1] // (GROUP * LANES), target_group, 0)
 
 
-def far_kernel(live_ref, small_ref, v1_ref, v2_ref, ga, gb, gc, gd, data_ref, node_ref, e0, e1, e2,
-               out_ref, trace_ref, ext_ref, d0, d1, d2, lhs_ref, turn_ref):
+def energy_kernel(live_ref, v2_ref, ga, gb, gc, gd, data_ref, partial_ref, out_ref, ext_ref, turn_ref):
+    ext_ref[...] = extend(v2_ref[...], [ga, gb, gc, gd])
+    live = live_ref[0]
+
+    def energy_of(t, slot):
+        _, _, volume, field = element_gradient(
+            ext_ref[...], data_ref, turn_ref.at[slot], jnp.minimum(t, BLOCKS - 1)
+        )
+        return jnp.where(t < live, volume, 0.0) * (
+            field[0] * field[0] + field[1] * field[1] + field[2] * field[2]
+        )
+
+    def energy_pair(i, total):
+        return total + energy_of(2 * i, 0) + energy_of(2 * i + 1, 1)
+
+    energy = lax.fori_loop(0, (live + 1) // 2, energy_pair, jnp.zeros((8, LANES), F32))
+    lane = lax.broadcasted_iota(jnp.int32, (1, LANES), 1)
+    share = jnp.where(lane == 101, jnp.sum(energy) * SCALE, 0.0)
+    out_ref[...] = partial_ref[...] + share
+
+
+def far_kernel(small_ref, v1_ref, v2_ref, node_ref, e0, e1, e2,
+               out_ref, trace_ref, d0, d1, d2, lhs_ref):
     b = small_ref[B_ROWS, :]
     v1 = v1_ref[...]
     v2 = v2_ref[...]
-    ext_ref[...] = extend(v2, [ga, gb, gc, gd])
-
-    def energy_block(t, total):
-        _, _, volume, field = element_gradient(ext_ref[...], data_ref, turn_ref, t)
-        return total + volume * (
-            field[0] * field[0] + field[1] * field[1] + field[2] * field[2]
-        )
-
-    energy = lax.fori_loop(0, live_ref[0], energy_block, jnp.zeros((8, LANES), F32))
     products = [b * b, b * v1, v1 * v1, v1 * v2, v2 * v2, small_ref[MASS_ROWS, :] * v2 * v2]
     sums = [p[0:8] + p[8:16] for p in products]
-    sums[5] = (sums[5] + energy) * SCALE
+    sums[5] = sums[5] * SCALE
     sub = lax.broadcasted_iota(jnp.int32, (8, LANES), 0)
     lane_row = lax.broadcasted_iota(jnp.int32, (1, LANES), 1)
     moments = jnp.zeros((1, LANES), F32)
@@ -473,13 +493,15 @@
             (own, *returned, lists, vectors[-1], small),
         )
         vectors.append(new)
-    ghosts = swap(4, pieces)
+    ghosts = exchange(pieces)
+    fill()
     partial, trace = call(
-        far_kernel, [(N_DEV, LANES), (3, 8, LANES)],
-        (live_blocks, *vectors, *ghosts, data, nodes, *chunks), smem=1,
-        scratch=[pltpu.VMEM((EXT_ROWS, LANES), F32)]
-        + [pltpu.VMEM((TGT_ROWS, LANES), F32)] * 3
-        + [pltpu.VMEM((8, PAD_SLOTS), BF16), TURN],
+        far_kernel, [(N_DEV, LANES), (3, 8, LANES)], (*vectors, nodes, *chunks),
+        scratch=[pltpu.VMEM((TGT_ROWS, LANES), F32)] * 3 + [pltpu.VMEM((8, PAD_SLOTS), BF16)],
+    )
+    partial, = call(
+        energy_kernel, [(N_DEV, LANES)], (live_blocks, vectors[-1], *ghosts, data, partial), smem=1,
+        scratch=[pltpu.VMEM((EXT_ROWS, LANES), F32), pltpu.VMEM((2, 128, LANES), F32)],
     )
     got = lax.all_to_all(partial, ("row", "col"), 0, 0, tiled=True)
     potential, dirichlet = call(

time: 93.2 us -> 89.8 us (0.964)
  Pallas kernels: 15.5 us -> 14.1 us
  blocking collectives: 28.1 us -> 27 us
    pallas_call x11 -> x12, Pallas kernels: 15.5 us -> 14.1 us  [call(): pl.pallas_call(body, out_shape=out_shapes, in_specs=specs, out_specs=[pl....]
    all_to_all x1, blocking collectives: 28.1 us -> 27 us  [per_device(): got = lax.all_to_all(partial, ('row', 'col'), 0, 0, tiled=True)]
where the time goes in v6:
time: 89.8 us; the launch traced here: 89.5 us
  starting transfers between devices  39 us (43%)
  blocking collectives  27 us (30%)
  Pallas kernels  14.1 us (16%)
  waiting for transfers between devices  3.58 us (4%)
  local copies, waits for them, and re-layouts  2.21 us (2%)
  other arithmetic  2.09 us (2%)
  between operations  1.48 us (2%)
    all_to_all x1, blocking collectives, per_device(): got = lax.all_to_all(partial, ('row', 'col'), 0, 0, tiled=True)  27 us
    ppermute x20, starting transfers between devices, exchange(): lax.ppermute(pieces[k], ('row', 'col'), swap_partners(rows, cols, axis, k...  23.4 us
    all_to_all x1, starting transfers between devices, per_device(): targets = lax.all_to_all(mine, ('row', 'col'), 0, 0, tiled=True)  15.6 us
    pallas_call x12, Pallas kernels, call(): pl.pallas_call(body, out_shape=out_shapes, in_specs=specs, out_specs=[pl....  14.1 us
    ppermute x20, waiting for transfers between devices, exchange(): lax.ppermute(pieces[k], ('row', 'col'), swap_partners(rows, cols, axis, k...  3.58 us
  transfers between devices with their start and end apart: 21, of which 3 were waited for; matrix products, arithmetic and copies ran while one was open for 2% of the time, Pallas kernels for 13%

profile of v6, /device:TPU:1, one launch (start us, length us, event | category | flops | bytes accessed | tf_op | source)
XLA Modules:
  0.0 89.5 jit_solution(10672695086640704676)
XLA Ops:
  3.6 15.6 %all-to-all-start = ((f32[256,1,128]{2,1,0:T(1,128)}), f32[256,1,128]{2,1,0:T(1,128)S(1)}, u32[]{:S(2)}, u32[]{:S(2)}) async-start(f32[256,1,128]{2,1,0:T(1,128)} %bitcast.7), calls=%async_computation | async-start | bytes 262144 | tf_op jit(solution)/shard_map/all_to_all | solution.py:450
  19.3 2.2 %collective-permute-start = (f32[2,128]{1,0:T(2,128)S(1)}, f32[2,128]{1,0:T(2,128)S(1)}, u32[]{:S(2)}, u32[]{:S(2)}) collective-permute-start(f32[2,128]{1,0:T(2,128)S(1)} %get-tuple-element.37), channel_id=1, source_target_pairs={{0,32},{1,33},{2,34},{3,35},{4,36},{5,37},{6,38},{7,39},{8,40},{9,... | collective-permute-start | bytes 3080 | tf_op jit(solution)/shard_map/ppermute | solution.py:432
  21.5 0.9 %collective-permute-start.2 = (f32[2,128]{1,0:T(2,128)S(1)}, f32[2,128]{1,0:T(2,128)S(1)}, u32[]{:S(2)}, u32[]{:S(2)}) collective-permute-start(f32[2,128]{1,0:T(2,128)S(1)} %get-tuple-element.39), channel_id=1, source_target_pairs={{0,1},{1,0},{2,3},{3,2},{4,5},{5,4},{6,7},{7,6},{8,9},{9,8},{10,11... | collective-permute-start | bytes 3080 | tf_op jit(solution)/shard_map/ppermute | solution.py:432
  22.4 1.2 %collective-permute-start.3 = (f32[2,128]{1,0:T(2,128)S(1)}, f32[2,128]{1,0:T(2,128)S(1)}, u32[]{:S(2)}, u32[]{:S(2)}) collective-permute-start(f32[2,128]{1,0:T(2,128)S(1)} %get-tuple-element.40), channel_id=1, source_target_pairs={{0,32},{1,2},{2,1},{3,4},{4,3},{5,6},{6,5},{7,8},{8,7},{9,10},{10,... | collective-permute-start | bytes 3080 | tf_op jit(solution)/shard_map/ppermute | solution.py:432
  24.6 1.2 %pad_maximum_fusion.data_ref = f32[14,8192]{1,0:T(8,128)S(1)} fusion(f32[1,8192]{1,0:T(1,128)} %bitcast.31, f32[4,8192]{1,0:T(4,128)S(1)} %convert_element_type.3, f32[9,8192]{1,0:T(8,128)} %param.13), kind=kLoop, calls=%fused_computation | loop fusion | flops 229376 | bytes 917504 | tf_op jit(solution)/shard_map/concatenate | solution.py:444
  26.4 1.7 %shard_map.132 = (f32[16,128]{1,0:T(8,128)S(1)}, f32[2,128]{1,0:T(2,128)S(1)}, f32[2,128]{1,0:T(2,128)S(1)}, f32[2,128]{1,0:T(2,128)S(1)}, f32[2,128]{1,0:T(2,128)S(1)}) custom-call(s32[1]{0:T(128)S(6)} %copy.18.live_ref, f32[41,128]{1,0:T(8,128)S(1)} %bitcast.20, f32[2,128]{1,0:T(2,128)S(1)} %collective-permute-done.ga, ...), custom_call_target="tpu_custom_call" | custom-call | flops 2000000 | bytes 1048576 | tf_op jit(solution)/shard_map/pallas_call | solution.py:392
  28.7 1.8 %collective-permute-start.6 = (f32[2,128]{1,0:T(2,128)S(1)}, f32[2,128]{1,0:T(2,128)S(1)}, u32[]{:S(2)}, u32[]{:S(2)}) collective-permute-start(f32[2,128]{1,0:T(2,128)S(1)} %get-tuple-element.44), channel_id=1, source_target_pairs={{0,1},{1,0},{2,3},{3,2},{4,5},{5,4},{6,7},{7,6},{8,9},{9,8},{10,11... | collective-permute-start | bytes 3080 | tf_op jit(solution)/shard_map/ppermute | solution.py:432
  30.8 1.1 %collective-permute-done.5.rb = f32[2,128]{1,0:T(2,128)S(1)} collective-permute-done((f32[2,128]{1,0:T(2,128)S(1)}, f32[2,128]{1,0:T(2,128)S(1)}, u32[]{:S(2)}, u32[]{:S(2)}) %collective-permute-start.5) | collective-permute-done | bytes 1056 | tf_op jit(solution)/shard_map/ppermute | solution.py:432
  32.3 3.3 %collective-permute-start.10 = (f32[2,128]{1,0:T(2,128)S(1)}, f32[2,128]{1,0:T(2,128)S(1)}, u32[]{:S(2)}, u32[]{:S(2)}) collective-permute-start(f32[2,128]{1,0:T(2,128)S(1)} %get-tuple-element.50), channel_id=1, source_target_pairs={{0,1},{1,0},{2,3},{3,2},{4,5},{5,4},{6,7},{7,6},{8,9},{9,8},{10,11... | collective-permute-start | bytes 3080 | tf_op jit(solution)/shard_map/ppermute | solution.py:432
  36.3 2.1 %collective-permute-start.9 = (f32[2,128]{1,0:T(2,128)S(1)}, f32[2,128]{1,0:T(2,128)S(1)}, u32[]{:S(2)}, u32[]{:S(2)}) collective-permute-start(f32[2,128]{1,0:T(2,128)S(1)} %get-tuple-element.49), channel_id=1, source_target_pairs={{0,1},{1,0},{2,3},{3,2},{4,5},{5,4},{6,7},{7,6},{8,9},{9,8},{10,11... | collective-permute-start | bytes 3080 | tf_op jit(solution)/shard_map/ppermute | solution.py:432
  38.3 1.2 %collective-permute-done.9.gb = f32[2,128]{1,0:T(2,128)S(1)} collective-permute-done((f32[2,128]{1,0:T(2,128)S(1)}, f32[2,128]{1,0:T(2,128)S(1)}, u32[]{:S(2)}, u32[]{:S(2)}) %collective-permute-start.9) | collective-permute-done | bytes 1056 | tf_op jit(solution)/shard_map/ppermute | solution.py:432
  39.6 1.7 %shard_map.134 = (f32[16,128]{1,0:T(8,128)S(1)}, f32[2,128]{1,0:T(2,128)S(1)}, f32[2,128]{1,0:T(2,128)S(1)}, f32[2,128]{1,0:T(2,128)S(1)}, f32[2,128]{1,0:T(2,128)S(1)}) custom-call(s32[1]{0:T(128)S(6)} %copy.18.live_ref, f32[16,128]{1,0:T(8,128)S(1)} %get-tuple-element.47.v_ref.v1_ref, f32[2,128]{1,0:T(2,128)S(1)} %collective-permute-done.8.ga, ...), custom_call_target="tpu_custom_call" | custom-call | flops 2000000 | bytes 1048576 | tf_op jit(solution)/shard_map/pallas_call | solution.py:392
  41.3 4.0 %collective-permute-start.12 = (f32[2,128]{1,0:T(2,128)S(1)}, f32[2,128]{1,0:T(2,128)S(1)}, u32[]{:S(2)}, u32[]{:S(2)}) collective-permute-start(f32[2,128]{1,0:T(2,128)S(1)} %get-tuple-element.53), channel_id=1, source_target_pairs={{0,32},{1,33},{2,34},{3,35},{4,36},{5,37},{6,38},{7,39},{8,40},{9,... | collective-permute-start | bytes 3080 | tf_op jit(solution)/shard_map/ppermute | solution.py:432
  45.9 1.4 %collective-permute-start.15 = (f32[2,128]{1,0:T(2,128)S(1)}, f32[2,128]{1,0:T(2,128)S(1)}, u32[]{:S(2)}, u32[]{:S(2)}) collective-permute-start(f32[2,128]{1,0:T(2,128)S(1)} %get-tuple-element.56), channel_id=1, source_target_pairs={{0,32},{1,2},{2,1},{3,4},{4,3},{5,6},{6,5},{7,8},{8,7},{9,10},{10,... | collective-permute-start | bytes 3080 | tf_op jit(solution)/shard_map/ppermute | solution.py:432
  47.4 1.1 %collective-permute-done.13.rb = f32[2,128]{1,0:T(2,128)S(1)} collective-permute-done((f32[2,128]{1,0:T(2,128)S(1)}, f32[2,128]{1,0:T(2,128)S(1)}, u32[]{:S(2)}, u32[]{:S(2)}) %collective-permute-start.13) | collective-permute-done | bytes 1056 | tf_op jit(solution)/shard_map/ppermute | solution.py:432
  48.8 1.1 %collective-permute-start.16 = (f32[2,128]{1,0:T(2,128)S(1)}, f32[2,128]{1,0:T(2,128)S(1)}, u32[]{:S(2)}, u32[]{:S(2)}) collective-permute-start(f32[2,128]{1,0:T(2,128)S(1)} %get-tuple-element.58), channel_id=1, source_target_pairs={{0,32},{1,33},{2,34},{3,35},{4,36},{5,37},{6,38},{7,39},{8,40},{9,... | collective-permute-start | bytes 3080 | tf_op jit(solution)/shard_map/ppermute | solution.py:432
  49.9 1.4 %collective-permute-start.17 = (f32[2,128]{1,0:T(2,128)S(1)}, f32[2,128]{1,0:T(2,128)S(1)}, u32[]{:S(2)}, u32[]{:S(2)}) collective-permute-start(f32[2,128]{1,0:T(2,128)S(1)} %get-tuple-element.59), channel_id=1, source_target_pairs={{0,1},{1,0},{2,3},{3,2},{4,5},{5,4},{6,7},{7,6},{8,9},{9,8},{10,11... | collective-permute-start | bytes 3080 | tf_op jit(solution)/shard_map/ppermute | solution.py:432
  51.2 1.7 %collective-permute-start.18 = (f32[2,128]{1,0:T(2,128)S(1)}, f32[2,128]{1,0:T(2,128)S(1)}, u32[]{:S(2)}, u32[]{:S(2)}) collective-permute-start(f32[2,128]{1,0:T(2,128)S(1)} %get-tuple-element.60), channel_id=1, source_target_pairs={{0,1},{1,0},{2,3},{3,2},{4,5},{5,4},{6,7},{7,6},{8,9},{9,8},{10,11... | collective-permute-start | bytes 3080 | tf_op jit(solution)/shard_map/ppermute | solution.py:432
  53.0 0.9 %shard_map.136 = (f32[6,320,128]{2,1,0:T(8,128)S(1)}, bf16[320,32]{1,0:T(8,128)(2,1)S(1)}, bf16[32,8192]{1,0:T(8,128)(2,1)S(1)}, f32[3,64,128]{2,1,0:T(8,128)S(1)}) custom-call(f32[41,128]{1,0:T(8,128)S(1)} %bitcast.24, f32[3,320]{1,0:T(4,128)S(1)} %get-tuple-element.62.point_ref, f32[256,128]{1,0:T(8,128)S(1)} %bitcast.27), custom_call_target="tpu_custom_call" | custom-call | flops 2000000 | bytes 1048576 | tf_op jit(solution)/shard_map/pallas_call | solution.py:392
  53.9 1.8 %shard_map.139.e2 = bf16[320,2560]{1,0:T(8,128)(2,1)S(1)} custom-call(f32[6,320,128]{2,1,0:T(8,128)S(1)} %get-tuple-element.64.refs_0_, bf16[320,32]{1,0:T(8,128)(2,1)S(1)} %get-tuple-element.65.refs_1_, bf16[32,8192]{1,0:T(8,128)(2,1)S(1)} %get-tuple-element.66.refs_2_, f32[3,64,128]{2,1,0:T(8,128)S(1)} %get-tuple-element.67.refs_3_), custom_call_target="tpu_custom_call" | custom-call | flops 2000000 | bytes 1048576 | tf_op jit(solution)/shard_map/pallas_call | solution.py:392
  55.7 2.2 %shard_map.138.e1 = bf16[320,3072]{1,0:T(8,128)(2,1)S(1)} custom-call(f32[6,320,128]{2,1,0:T(8,128)S(1)} %get-tuple-element.64.refs_0_, bf16[320,32]{1,0:T(8,128)(2,1)S(1)} %get-tuple-element.65.refs_1_, bf16[32,8192]{1,0:T(8,128)(2,1)S(1)} %get-tuple-element.66.refs_2_, f32[3,64,128]{2,1,0:T(8,128)S(1)} %get-tuple-element.67.refs_3_), custom_call_target="tpu_custom_call" | custom-call | flops 2000000 | bytes 1048576 | tf_op jit(solution)/shard_map/pallas_call | solution.py:392
  58.0 1.8 %shard_map.137.e0 = bf16[320,2560]{1,0:T(8,128)(2,1)S(1)} custom-call(f32[6,320,128]{2,1,0:T(8,128)S(1)} %get-tuple-element.64.refs_0_, bf16[320,32]{1,0:T(8,128)(2,1)S(1)} %get-tuple-element.65.refs_1_, bf16[32,8192]{1,0:T(8,128)(2,1)S(1)} %get-tuple-element.66.refs_2_, f32[3,64,128]{2,1,0:T(8,128)S(1)} %get-tuple-element.67.refs_3_), custom_call_target="tpu_custom_call" | custom-call | flops 2000000 | bytes 1048576 | tf_op jit(solution)/shard_map/pallas_call | solution.py:392
  59.8 1.1 %shard_map.140 = (f32[256,128]{1,0:T(8,128)S(1)}, f32[3,8,128]{2,1,0:T(8,128)S(1)}) custom-call(f32[41,128]{1,0:T(8,128)S(1)} %bitcast.25, f32[16,128]{1,0:T(8,128)S(1)} %get-tuple-element.47.v_ref.v1_ref, f32[16,128]{1,0:T(8,128)S(1)} %get-tuple-element.57.v2_ref, s32[8,128]{1,0:T(8,128)S(1)} %pad_bitcast_fusion.node_ref, ...), custom_call_target="tpu_custom_call" | custom-call | flops 2000000 | bytes 1048576 | tf_op jit(solution)/shard_map/pallas_call | solution.py:392
  61.7 27.0 %all_to_all.22 = f32[256,1,128]{2,1,0:T(1,128)S(1)} all-to-all(f32[256,1,128]{2,1,0:T(1,128)S(1)} %bitcast.29), channel_id=1, replica_groups=mesh['row'=8,'col'=32] {'row','col'}, dimensions={0} | all-to-all | bytes 262144 | tf_op jit(solution)/shard_map/all_to_all | solution.py:506
  (42 shorter events, 8.4 us)
Async XLA Ops:
  0.6 46.7 %copy-start.2 = (s32[320]{0:T(512)S(1)}, s32[320]{0:T(512)}, u32[]{:S(2)}) copy-start(s32[320]{0:T(512)} %param.19) | copy-start | bytes 3844
  1.5 0.7 copy-start
  2.2 0.7 copy-start.1
  3.6 49.4 %all-to-all-start = ((f32[256,1,128]{2,1,0:T(1,128)}), f32[256,1,128]{2,1,0:T(1,128)S(1)}, u32[]{:S(2)}, u32[]{:S(2)}) async-start(f32[256,1,128]{2,1,0:T(1,128)} %bitcast.7), calls=%async_computation | async-start | bytes 262144 | tf_op jit(solution)/shard_map/all_to_all | solution.py:450
  19.3 7.1 %collective-permute-start = (f32[2,128]{1,0:T(2,128)S(1)}, f32[2,128]{1,0:T(2,128)S(1)}, u32[]{:S(2)}, u32[]{:S(2)}) collective-permute-start(f32[2,128]{1,0:T(2,128)S(1)} %get-tuple-element.37), channel_id=1, source_target_pairs={{0,32},{1,33},{2,34},{3,35},{4,36},{5,37},{6,38},{7,39},{8,40},{9,... | collective-permute-start | bytes 3080 | tf_op jit(solution)/shard_map/ppermute | solution.py:432
  21.5 4.9 %collective-permute-start.1 = (f32[2,128]{1,0:T(2,128)S(1)}, f32[2,128]{1,0:T(2,128)S(1)}, u32[]{:S(2)}, u32[]{:S(2)}) collective-permute-start(f32[2,128]{1,0:T(2,128)S(1)} %get-tuple-element.38), channel_id=1, source_target_pairs={{0,1},{1,0},{2,3},{3,2},{4,5},{5,4},{6,7},{7,6},{8,9},{9,8},{10,11... | collective-permute-start | bytes 3080 | tf_op jit(solution)/shard_map/ppermute | solution.py:432
  21.5 4.9 %collective-permute-start.2 = (f32[2,128]{1,0:T(2,128)S(1)}, f32[2,128]{1,0:T(2,128)S(1)}, u32[]{:S(2)}, u32[]{:S(2)}) collective-permute-start(f32[2,128]{1,0:T(2,128)S(1)} %get-tuple-element.39), channel_id=1, source_target_pairs={{0,1},{1,0},{2,3},{3,2},{4,5},{5,4},{6,7},{7,6},{8,9},{9,8},{10,11... | collective-permute-start | bytes 3080 | tf_op jit(solution)/shard_map/ppermute | solution.py:432
  22.4 4.0 %collective-permute-start.3 = (f32[2,128]{1,0:T(2,128)S(1)}, f32[2,128]{1,0:T(2,128)S(1)}, u32[]{:S(2)}, u32[]{:S(2)}) collective-permute-start(f32[2,128]{1,0:T(2,128)S(1)} %get-tuple-element.40), channel_id=1, source_target_pairs={{0,32},{1,2},{2,1},{3,4},{4,3},{5,6},{6,5},{7,8},{8,7},{9,10},{10,... | collective-permute-start | bytes 3080 | tf_op jit(solution)/shard_map/ppermute | solution.py:432
  28.1 2.7 %collective-permute-start.4 = (f32[2,128]{1,0:T(2,128)S(1)}, f32[2,128]{1,0:T(2,128)S(1)}, u32[]{:S(2)}, u32[]{:S(2)}) collective-permute-start(f32[2,128]{1,0:T(2,128)S(1)} %get-tuple-element.42), channel_id=1, source_target_pairs={{0,32},{1,33},{2,34},{3,35},{4,36},{5,37},{6,38},{7,39},{8,40},{9,... | collective-permute-start | bytes 3080 | tf_op jit(solution)/shard_map/ppermute | solution.py:432
  28.7 3.3 %collective-permute-start.5 = (f32[2,128]{1,0:T(2,128)S(1)}, f32[2,128]{1,0:T(2,128)S(1)}, u32[]{:S(2)}, u32[]{:S(2)}) collective-permute-start(f32[2,128]{1,0:T(2,128)S(1)} %get-tuple-element.43), channel_id=1, source_target_pairs={{0,1},{1,0},{2,3},{3,2},{4,5},{5,4},{6,7},{7,6},{8,9},{9,8},{10,11... | collective-permute-start | bytes 3080 | tf_op jit(solution)/shard_map/ppermute | solution.py:432
  28.7 3.3 %collective-permute-start.6 = (f32[2,128]{1,0:T(2,128)S(1)}, f32[2,128]{1,0:T(2,128)S(1)}, u32[]{:S(2)}, u32[]{:S(2)}) collective-permute-start(f32[2,128]{1,0:T(2,128)S(1)} %get-tuple-element.44), channel_id=1, source_target_pairs={{0,1},{1,0},{2,3},{3,2},{4,5},{5,4},{6,7},{7,6},{8,9},{9,8},{10,11... | collective-permute-start | bytes 3080 | tf_op jit(solution)/shard_map/ppermute | solution.py:432
  30.5 1.4 %collective-permute-start.7 = (f32[2,128]{1,0:T(2,128)S(1)}, f32[2,128]{1,0:T(2,128)S(1)}, u32[]{:S(2)}, u32[]{:S(2)}) collective-permute-start(f32[2,128]{1,0:T(2,128)S(1)} %get-tuple-element.45), channel_id=1, source_target_pairs={{0,32},{1,2},{2,1},{3,4},{4,3},{5,6},{6,5},{7,8},{8,7},{9,10},{10,... | collective-permute-start | bytes 3080 | tf_op jit(solution)/shard_map/ppermute | solution.py:432
  32.3 6.1 %collective-permute-start.10 = (f32[2,128]{1,0:T(2,128)S(1)}, f32[2,128]{1,0:T(2,128)S(1)}, u32[]{:S(2)}, u32[]{:S(2)}) collective-permute-start(f32[2,128]{1,0:T(2,128)S(1)} %get-tuple-element.50), channel_id=1, source_target_pairs={{0,1},{1,0},{2,3},{3,2},{4,5},{5,4},{6,7},{7,6},{8,9},{9,8},{10,11... | collective-permute-start | bytes 3080 | tf_op jit(solution)/shard_map/ppermute | solution.py:432
  35.6 2.7 %collective-permute-start.11 = (f32[2,128]{1,0:T(2,128)S(1)}, f32[2,128]{1,0:T(2,128)S(1)}, u32[]{:S(2)}, u32[]{:S(2)}) collective-permute-start(f32[2,128]{1,0:T(2,128)S(1)} %get-tuple-element.51), channel_id=1, source_target_pairs={{0,32},{1,2},{2,1},{3,4},{4,3},{5,6},{6,5},{7,8},{8,7},{9,10},{10,... | collective-permute-start | bytes 3080 | tf_op jit(solution)/shard_map/ppermute | solution.py:432
  36.3 2.1 %collective-permute-start.8 = (f32[2,128]{1,0:T(2,128)S(1)}, f32[2,128]{1,0:T(2,128)S(1)}, u32[]{:S(2)}, u32[]{:S(2)}) collective-permute-start(f32[2,128]{1,0:T(2,128)S(1)} %get-tuple-element.48), channel_id=1, source_target_pairs={{0,32},{1,33},{2,34},{3,35},{4,36},{5,37},{6,38},{7,39},{8,40},{9,... | collective-permute-start | bytes 3080 | tf_op jit(solution)/shard_map/ppermute | solution.py:432
  36.3 3.3 %collective-permute-start.9 = (f32[2,128]{1,0:T(2,128)S(1)}, f32[2,128]{1,0:T(2,128)S(1)}, u32[]{:S(2)}, u32[]{:S(2)}) collective-permute-start(f32[2,128]{1,0:T(2,128)S(1)} %get-tuple-element.49), channel_id=1, source_target_pairs={{0,1},{1,0},{2,3},{3,2},{4,5},{5,4},{6,7},{7,6},{8,9},{9,8},{10,11... | collective-permute-start | bytes 3080 | tf_op jit(solution)/shard_map/ppermute | solution.py:432
  41.3 6.1 %collective-permute-start.12 = (f32[2,128]{1,0:T(2,128)S(1)}, f32[2,128]{1,0:T(2,128)S(1)}, u32[]{:S(2)}, u32[]{:S(2)}) collective-permute-start(f32[2,128]{1,0:T(2,128)S(1)} %get-tuple-element.53), channel_id=1, source_target_pairs={{0,32},{1,33},{2,34},{3,35},{4,36},{5,37},{6,38},{7,39},{8,40},{9,... | collective-permute-start | bytes 3080 | tf_op jit(solution)/shard_map/ppermute | solution.py:432
  45.2 3.3 %collective-permute-start.13 = (f32[2,128]{1,0:T(2,128)S(1)}, f32[2,128]{1,0:T(2,128)S(1)}, u32[]{:S(2)}, u32[]{:S(2)}) collective-permute-start(f32[2,128]{1,0:T(2,128)S(1)} %get-tuple-element.54), channel_id=1, source_target_pairs={{0,1},{1,0},{2,3},{3,2},{4,5},{5,4},{6,7},{7,6},{8,9},{9,8},{10,11... | collective-permute-start | bytes 3080 | tf_op jit(solution)/shard_map/ppermute | solution.py:432
  45.2 3.3 %collective-permute-start.14 = (f32[2,128]{1,0:T(2,128)S(1)}, f32[2,128]{1,0:T(2,128)S(1)}, u32[]{:S(2)}, u32[]{:S(2)}) collective-permute-start(f32[2,128]{1,0:T(2,128)S(1)} %get-tuple-element.55), channel_id=1, source_target_pairs={{0,1},{1,0},{2,3},{3,2},{4,5},{5,4},{6,7},{7,6},{8,9},{9,8},{10,11... | collective-permute-start | bytes 3080 | tf_op jit(solution)/shard_map/ppermute | solution.py:432
  45.9 2.6 %collective-permute-start.15 = (f32[2,128]{1,0:T(2,128)S(1)}, f32[2,128]{1,0:T(2,128)S(1)}, u32[]{:S(2)}, u32[]{:S(2)}) collective-permute-start(f32[2,128]{1,0:T(2,128)S(1)} %get-tuple-element.56), channel_id=1, source_target_pairs={{0,32},{1,2},{2,1},{3,4},{4,3},{5,6},{6,5},{7,8},{8,7},{9,10},{10,... | collective-permute-start | bytes 3080 | tf_op jit(solution)/shard_map/ppermute | solution.py:432
  48.8 12.1 %collective-permute-start.16 = (f32[2,128]{1,0:T(2,128)S(1)}, f32[2,128]{1,0:T(2,128)S(1)}, u32[]{:S(2)}, u32[]{:S(2)}) collective-permute-start(f32[2,128]{1,0:T(2,128)S(1)} %get-tuple-element.58), channel_id=1, source_target_pairs={{0,32},{1,33},{2,34},{3,35},{4,36},{5,37},{6,38},{7,39},{8,40},{9,... | collective-permute-start | bytes 3080 | tf_op jit(solution)/shard_map/ppermute | solution.py:432
  49.9 11.0 %collective-permute-start.17 = (f32[2,128]{1,0:T(2,128)S(1)}, f32[2,128]{1,0:T(2,128)S(1)}, u32[]{:S(2)}, u32[]{:S(2)}) collective-permute-start(f32[2,128]{1,0:T(2,128)S(1)} %get-tuple-element.59), channel_id=1, source_target_pairs={{0,1},{1,0},{2,3},{3,2},{4,5},{5,4},{6,7},{7,6},{8,9},{9,8},{10,11... | collective-permute-start | bytes 3080 | tf_op jit(solution)/shard_map/ppermute | solution.py:432
  51.2 9.7 %collective-permute-start.18 = (f32[2,128]{1,0:T(2,128)S(1)}, f32[2,128]{1,0:T(2,128)S(1)}, u32[]{:S(2)}, u32[]{:S(2)}) collective-permute-start(f32[2,128]{1,0:T(2,128)S(1)} %get-tuple-element.60), channel_id=1, source_target_pairs={{0,1},{1,0},{2,3},{3,2},{4,5},{5,4},{6,7},{7,6},{8,9},{9,8},{10,11... | collective-permute-start | bytes 3080 | tf_op jit(solution)/shard_map/ppermute | solution.py:432
  53.0 8.0 %collective-permute-start.19 = (f32[2,128]{1,0:T(2,128)S(1)}, f32[2,128]{1,0:T(2,128)S(1)}, u32[]{:S(2)}, u32[]{:S(2)}) collective-permute-start(f32[2,128]{1,0:T(2,128)S(1)} %get-tuple-element.61), channel_id=1, source_target_pairs={{0,32},{1,2},{2,1},{3,4},{4,3},{5,6},{6,5},{7,8},{8,7},{9,10},{10,... | collective-permute-start | bytes 3080 | tf_op jit(solution)/shard_map/ppermute | solution.py:432

commit v7 on v6

--- a/solution.py
+++ b/solution.py
@@ -19,11 +19,12 @@
 OWN_ROWS = NN_DEV // LANES
 EXT_ROWS = OWN_ROWS + 4 * GH // LANES
 HIGH_ROWS = 32
+ELEM_ROWS = 64
 SLOTS = 320
 PAD_SLOTS = 384
 N_DEV = 256
 TGT_ROWS = N_DEV // 4
-CHUNKS = (20, 24, 20)
+CHUNKS = (16, 16, 20, 12)
 GROUP = 4
 KDIM = 32
 SPLITS = 2
@@ -91,13 +92,14 @@
     for k in range(8):
         lanes = pl.ds(pl.multiple_of(EBLK * t + LANES * k, LANES), LANES)
         turn_ref[16 * k:16 * k + 8, :] = data_ref[0:8, lanes]
-        turn_ref[16 * k + 8:16 * k + 14, :] = data_ref[8:14, lanes]
-    rows = [turn_ref[pl.ds(q, 8, stride=16), :] for q in range(14)]
-    return rows[0:9], [r.astype(jnp.int32) for r in rows[9:13]], rows[13]
-
-
-def element_gradient(ext, data_ref, turn_ref, t):
-    grads, index, volume = turn_block(data_ref, turn_ref, t)
+        turn_ref[16 * k + 8:16 * k + 10, :] = data_ref[8:10, lanes]
+    rows = [turn_ref[pl.ds(q, 8, stride=16), :] for q in range(10)]
+    return rows[0:9], rows[9]
+
+
+def element_gradient(ext, data_ref, conn_ref, turn_ref, t):
+    grads, volume = turn_block(data_ref, turn_ref, t)
+    index = [conn_ref[pl.ds(32 * t + a, 8, stride=4), :] for a in range(4)]
     corner = [gather_rows(ext, i) for i in index]
     diff = [corner[a] - corner[3] for a in range(3)]
     field = [
@@ -163,14 +165,14 @@
     target_ref[...] = jnp.broadcast_to(own, (N_DEV, LANES))
 
 
-def apply_kernel(live_ref, v_ref, ga, gb, gc, gd, data_ref,
+def apply_kernel(live_ref, v_ref, ga, gb, gc, gd, data_ref, conn_ref,
                  own_ref, oa, ob, oc, od, ext_ref, acc_ref, turn_ref):
     ext_ref[...] = extend(v_ref[0:OWN_ROWS, :], [ga, gb, gc, gd])
     acc_ref[...] = jnp.zeros_like(acc_ref)
 
     def element_terms(t):
         grads, index, volume, field = element_gradient(
-            ext_ref[...], data_ref, turn_ref, jnp.minimum(t, BLOCKS - 1)
+            ext_ref[...], data_ref, conn_ref, turn_ref, jnp.minimum(t, BLOCKS - 1)
         )
         field = [volume * f for f in field]
         terms = [
@@ -281,13 +283,14 @@
     lax.fori_loop(0, entry_ref.shape[1] // (GROUP * LANES), target_group, 0)
 
 
-def energy_kernel(live_ref, v2_ref, ga, gb, gc, gd, data_ref, partial_ref, out_ref, ext_ref, turn_ref):
+def energy_kernel(live_ref, v2_ref, ga, gb, gc, gd, data_ref, conn_ref, partial_ref,
+                  out_ref, ext_ref, turn_ref):
     ext_ref[...] = extend(v2_ref[...], [ga, gb, gc, gd])
     live = live_ref[0]
 
     def energy_of(t, slot):
         _, _, volume, field = element_gradient(
-            ext_ref[...], data_ref, turn_ref.at[slot], jnp.minimum(t, BLOCKS - 1)
+            ext_ref[...], data_ref, conn_ref, turn_ref.at[slot], jnp.minimum(t, BLOCKS - 1)
         )
         return jnp.where(t < live, volume, 0.0) * (
             field[0] * field[0] + field[1] * field[1] + field[2] * field[2]
@@ -302,7 +305,7 @@
     out_ref[...] = partial_ref[...] + share
 
 
-def far_kernel(small_ref, v1_ref, v2_ref, node_ref, e0, e1, e2,
+def far_kernel(small_ref, v1_ref, v2_ref, node_ref, e0, e1, e2, e3,
                out_ref, trace_ref, d0, d1, d2, lhs_ref):
     b = small_ref[B_ROWS, :]
     v1 = v1_ref[...]
@@ -330,7 +333,7 @@
         lhs_ref[:, r * LANES:(r + 1) * LANES] = block.astype(BF16)
     lhs = lhs_ref[:, 0:SLOTS]
     base = 0
-    for each, entry_ref in zip(CHUNKS, (e0, e1, e2)):
+    for each, entry_ref in zip(CHUNKS, (e0, e1, e2, e3)):
         res = jnp.dot(lhs, entry_ref[...], preferred_element_type=F32)
         base += each
         for q in range(each):
@@ -441,7 +444,8 @@
     small = jnp.concatenate([
         divergence, mass_shift, normal_cos, gap, normal_angle, gap, node_areas, gap,
     ]).reshape(-1, LANES)
-    data = jnp.concatenate([gradients, connectivity.astype(F32), volumes[None]], axis=0)
+    data = jnp.concatenate([gradients, volumes[None]], axis=0)
+    conn = connectivity.reshape(4, ELEM_ROWS, LANES).transpose(1, 0, 2).reshape(4 * ELEM_ROWS, LANES)
     mine, lists, points, *pieces = call(
         pick_kernel,
         [(N_DEV, LANES), jax.ShapeDtypeStruct(lists.shape, lists.dtype), surface_points.shape] + [PIECE] * 4,
@@ -464,7 +468,6 @@
                 ],
                 (small, points, targets),
             )
-            return
         done = len(chunks)
         base = sum(CHUNKS[:done])
         chunks.append(call(
@@ -484,7 +487,7 @@
         ghosts = swap(2 * step, pieces)
         own, *back = call(
             apply_kernel, [(OWN_ROWS, LANES)] + [PIECE] * 4,
-            (live_blocks, vectors[-1], *ghosts, data), smem=1,
+            (live_blocks, vectors[-1], *ghosts, data, conn), smem=1,
             scratch=[pltpu.VMEM((EXT_ROWS, LANES), F32), pltpu.VMEM((HIGH_ROWS, LANES), F32), TURN],
         )
         returned = swap(2 * step + 1, back)
@@ -500,7 +503,7 @@
         scratch=[pltpu.VMEM((TGT_ROWS, LANES), F32)] * 3 + [pltpu.VMEM((8, PAD_SLOTS), BF16)],
     )
     partial, = call(
-        energy_kernel, [(N_DEV, LANES)], (live_blocks, vectors[-1], *ghosts, data, partial), smem=1,
+        energy_kernel, [(N_DEV, LANES)], (live_blocks, vectors[-1], *ghosts, data, conn, partial), smem=1,
         scratch=[pltpu.VMEM((EXT_ROWS, LANES), F32), pltpu.VMEM((2, 128, LANES), F32)],
     )
     got = lax.all_to_all(partial, ("row", "col"), 0, 0, tiled=True)

time: 89.8 us -> 88.7 us (0.988)
  other arithmetic: 2.09 us -> 1.12 us
    convert_element_type x1 -> x0, other arithmetic: 0.93 us -> none  [per_device(): connectivity.astype(F32)]
    pallas_call x12 -> x13, Pallas kernels: 14.1 us -> 14 us  [call(): pl.pallas_call(body, out_shape=out_shapes, in_specs=specs, out_specs=[pl....]
  transfers between devices with their start and end apart: 21 -> 21, of which waited for: 3 -> 3; matrix products, arithmetic and copies ran while one was open for 2% -> 1% of each run, Pallas kernels for 13% -> 13%
where the time goes in v7:
time: 88.7 us; the launch traced here: 88.4 us
  starting transfers between devices  39.7 us (45%)
  blocking collectives  26.2 us (30%)
  Pallas kernels  14 us (16%)
  waiting for transfers between devices  3.73 us (4%)
  local copies, waits for them, and re-layouts  2.26 us (3%)
  between operations  1.5 us (2%)
  other arithmetic  1.12 us (1%)
    all_to_all x1, blocking collectives, per_device(): got = lax.all_to_all(partial, ('row', 'col'), 0, 0, tiled=True)  26.2 us
    ppermute x20, starting transfers between devices, exchange(): lax.ppermute(pieces[k], ('row', 'col'), swap_partners(rows, cols, axis, k...  24 us
    all_to_all x1, starting transfers between devices, per_device(): targets = lax.all_to_all(mine, ('row', 'col'), 0, 0, tiled=True)  15.6 us
    pallas_call x13, Pallas kernels, call(): pl.pallas_call(body, out_shape=out_shapes, in_specs=specs, out_specs=[pl....  14 us
    ppermute x20, waiting for transfers between devices, exchange(): lax.ppermute(pieces[k], ('row', 'col'), swap_partners(rows, cols, axis, k...  3.73 us
  transfers between devices with their start and end apart: 21, of which 3 were waited for; matrix products, arithmetic and copies ran while one was open for 1% of the time, Pallas kernels for 13%

profile of v7, /device:TPU:1, one launch (start us, length us, event | category | flops | bytes accessed | tf_op | source)
XLA Modules:
  0.0 88.4 jit_solution(4770627280300491945)
XLA Ops:
  3.6 15.6 %all-to-all-start = ((f32[256,1,128]{2,1,0:T(1,128)}), f32[256,1,128]{2,1,0:T(1,128)S(1)}, u32[]{:S(2)}, u32[]{:S(2)}) async-start(f32[256,1,128]{2,1,0:T(1,128)} %bitcast.10), calls=%async_computation | async-start | bytes 262144 | tf_op jit(solution)/shard_map/all_to_all | solution.py:454
  19.3 2.2 %collective-permute-start = (f32[2,128]{1,0:T(2,128)S(1)}, f32[2,128]{1,0:T(2,128)S(1)}, u32[]{:S(2)}, u32[]{:S(2)}) collective-permute-start(f32[2,128]{1,0:T(2,128)S(1)} %get-tuple-element.37), channel_id=1, source_target_pairs={{0,32},{1,33},{2,34},{3,35},{4,36},{5,37},{6,38},{7,39},{8,40},{9,... | collective-permute-start | bytes 3080 | tf_op jit(solution)/shard_map/ppermute | solution.py:435
  22.5 1.2 %collective-permute-start.3 = (f32[2,128]{1,0:T(2,128)S(1)}, f32[2,128]{1,0:T(2,128)S(1)}, u32[]{:S(2)}, u32[]{:S(2)}) collective-permute-start(f32[2,128]{1,0:T(2,128)S(1)} %get-tuple-element.40), channel_id=1, source_target_pairs={{0,32},{1,2},{2,1},{3,4},{4,3},{5,6},{6,5},{7,8},{8,7},{9,10},{10,... | collective-permute-start | bytes 3080 | tf_op jit(solution)/shard_map/ppermute | solution.py:435
  23.7 1.1 %pad_maximum_fusion.data_ref = f32[10,8192]{1,0:T(8,128)S(1)} fusion(f32[1,8192]{1,0:T(1,128)} %bitcast.39, f32[9,8192]{1,0:T(8,128)} %param.13), kind=kLoop, calls=%fused_computation | loop fusion | flops 81920 | bytes 655360 | tf_op jit(solution)/shard_map/concatenate | solution.py:447
  25.5 1.7 %shard_map.132 = (f32[16,128]{1,0:T(8,128)S(1)}, f32[2,128]{1,0:T(2,128)S(1)}, f32[2,128]{1,0:T(2,128)S(1)}, f32[2,128]{1,0:T(2,128)S(1)}, f32[2,128]{1,0:T(2,128)S(1)}) custom-call(s32[1]{0:T(128)S(6)} %copy.20.live_ref, f32[41,128]{1,0:T(8,128)S(1)} %bitcast.25, f32[2,128]{1,0:T(2,128)S(1)} %collective-permute-done.ga, ...), custom_call_target="tpu_custom_call" | custom-call | flops 2000000 | bytes 1048576 | tf_op jit(solution)/shard_map/pallas_call | solution.py:395
  27.7 1.8 %collective-permute-start.6 = (f32[2,128]{1,0:T(2,128)S(1)}, f32[2,128]{1,0:T(2,128)S(1)}, u32[]{:S(2)}, u32[]{:S(2)}) collective-permute-start(f32[2,128]{1,0:T(2,128)S(1)} %get-tuple-element.44), channel_id=1, source_target_pairs={{0,1},{1,0},{2,3},{3,2},{4,5},{5,4},{6,7},{7,6},{8,9},{9,8},{10,11... | collective-permute-start | bytes 3080 | tf_op jit(solution)/shard_map/ppermute | solution.py:435
  29.9 1.1 %collective-permute-done.5.rb = f32[2,128]{1,0:T(2,128)S(1)} collective-permute-done((f32[2,128]{1,0:T(2,128)S(1)}, f32[2,128]{1,0:T(2,128)S(1)}, u32[]{:S(2)}, u32[]{:S(2)}) %collective-permute-start.5) | collective-permute-done | bytes 1056 | tf_op jit(solution)/shard_map/ppermute | solution.py:435
  31.3 3.3 %collective-permute-start.10 = (f32[2,128]{1,0:T(2,128)S(1)}, f32[2,128]{1,0:T(2,128)S(1)}, u32[]{:S(2)}, u32[]{:S(2)}) collective-permute-start(f32[2,128]{1,0:T(2,128)S(1)} %get-tuple-element.50), channel_id=1, source_target_pairs={{0,1},{1,0},{2,3},{3,2},{4,5},{5,4},{6,7},{7,6},{8,9},{9,8},{10,11... | collective-permute-start | bytes 3080 | tf_op jit(solution)/shard_map/ppermute | solution.py:435
  34.6 1.2 %collective-permute-start.11 = (f32[2,128]{1,0:T(2,128)S(1)}, f32[2,128]{1,0:T(2,128)S(1)}, u32[]{:S(2)}, u32[]{:S(2)}) collective-permute-start(f32[2,128]{1,0:T(2,128)S(1)} %get-tuple-element.51), channel_id=1, source_target_pairs={{0,32},{1,2},{2,1},{3,4},{4,3},{5,6},{6,5},{7,8},{8,7},{9,10},{10,... | collective-permute-start | bytes 3080 | tf_op jit(solution)/shard_map/ppermute | solution.py:435
  35.8 1.6 %collective-permute-start.9 = (f32[2,128]{1,0:T(2,128)S(1)}, f32[2,128]{1,0:T(2,128)S(1)}, u32[]{:S(2)}, u32[]{:S(2)}) collective-permute-start(f32[2,128]{1,0:T(2,128)S(1)} %get-tuple-element.49), channel_id=1, source_target_pairs={{0,1},{1,0},{2,3},{3,2},{4,5},{5,4},{6,7},{7,6},{8,9},{9,8},{10,11... | collective-permute-start | bytes 3080 | tf_op jit(solution)/shard_map/ppermute | solution.py:435
  37.4 1.4 %collective-permute-done.9.gb = f32[2,128]{1,0:T(2,128)S(1)} collective-permute-done((f32[2,128]{1,0:T(2,128)S(1)}, f32[2,128]{1,0:T(2,128)S(1)}, u32[]{:S(2)}, u32[]{:S(2)}) %collective-permute-start.9) | collective-permute-done | bytes 1056 | tf_op jit(solution)/shard_map/ppermute | solution.py:435
  38.8 1.7 %shard_map.134 = (f32[16,128]{1,0:T(8,128)S(1)}, f32[2,128]{1,0:T(2,128)S(1)}, f32[2,128]{1,0:T(2,128)S(1)}, f32[2,128]{1,0:T(2,128)S(1)}, f32[2,128]{1,0:T(2,128)S(1)}) custom-call(s32[1]{0:T(128)S(6)} %copy.20.live_ref, f32[16,128]{1,0:T(8,128)S(1)} %get-tuple-element.47.v_ref.v1_ref, f32[2,128]{1,0:T(2,128)S(1)} %collective-permute-done.8.ga, ...), custom_call_target="tpu_custom_call" | custom-call | flops 2000000 | bytes 1048576 | tf_op jit(solution)/shard_map/pallas_call | solution.py:395
  40.5 3.9 %collective-permute-start.12 = (f32[2,128]{1,0:T(2,128)S(1)}, f32[2,128]{1,0:T(2,128)S(1)}, u32[]{:S(2)}, u32[]{:S(2)}) collective-permute-start(f32[2,128]{1,0:T(2,128)S(1)} %get-tuple-element.53), channel_id=1, source_target_pairs={{0,32},{1,33},{2,34},{3,35},{4,36},{5,37},{6,38},{7,39},{8,40},{9,... | collective-permute-start | bytes 3080 | tf_op jit(solution)/shard_map/ppermute | solution.py:435
  44.3 1.6 %collective-permute-start.14 = (f32[2,128]{1,0:T(2,128)S(1)}, f32[2,128]{1,0:T(2,128)S(1)}, u32[]{:S(2)}, u32[]{:S(2)}) collective-permute-start(f32[2,128]{1,0:T(2,128)S(1)} %get-tuple-element.55), channel_id=1, source_target_pairs={{0,1},{1,0},{2,3},{3,2},{4,5},{5,4},{6,7},{7,6},{8,9},{9,8},{10,11... | collective-permute-start | bytes 3080 | tf_op jit(solution)/shard_map/ppermute | solution.py:435
  46.5 1.1 %collective-permute-done.13.rb = f32[2,128]{1,0:T(2,128)S(1)} collective-permute-done((f32[2,128]{1,0:T(2,128)S(1)}, f32[2,128]{1,0:T(2,128)S(1)}, u32[]{:S(2)}, u32[]{:S(2)}) %collective-permute-start.13) | collective-permute-done | bytes 1056 | tf_op jit(solution)/shard_map/ppermute | solution.py:435
  47.9 1.1 %collective-permute-start.16 = (f32[2,128]{1,0:T(2,128)S(1)}, f32[2,128]{1,0:T(2,128)S(1)}, u32[]{:S(2)}, u32[]{:S(2)}) collective-permute-start(f32[2,128]{1,0:T(2,128)S(1)} %get-tuple-element.58), channel_id=1, source_target_pairs={{0,32},{1,33},{2,34},{3,35},{4,36},{5,37},{6,38},{7,39},{8,40},{9,... | collective-permute-start | bytes 3080 | tf_op jit(solution)/shard_map/ppermute | solution.py:435
  49.0 1.3 %collective-permute-start.17 = (f32[2,128]{1,0:T(2,128)S(1)}, f32[2,128]{1,0:T(2,128)S(1)}, u32[]{:S(2)}, u32[]{:S(2)}) collective-permute-start(f32[2,128]{1,0:T(2,128)S(1)} %get-tuple-element.59), channel_id=1, source_target_pairs={{0,1},{1,0},{2,3},{3,2},{4,5},{5,4},{6,7},{7,6},{8,9},{9,8},{10,11... | collective-permute-start | bytes 3080 | tf_op jit(solution)/shard_map/ppermute | solution.py:435
  50.3 2.5 %collective-permute-start.18 = (f32[2,128]{1,0:T(2,128)S(1)}, f32[2,128]{1,0:T(2,128)S(1)}, u32[]{:S(2)}, u32[]{:S(2)}) collective-permute-start(f32[2,128]{1,0:T(2,128)S(1)} %get-tuple-element.60), channel_id=1, source_target_pairs={{0,1},{1,0},{2,3},{3,2},{4,5},{5,4},{6,7},{7,6},{8,9},{9,8},{10,11... | collective-permute-start | bytes 3080 | tf_op jit(solution)/shard_map/ppermute | solution.py:435
  53.8 1.1 %shard_map.140.e3 = bf16[320,1536]{1,0:T(8,128)(2,1)S(1)} custom-call(f32[6,320,128]{2,1,0:T(8,128)S(1)} %get-tuple-element.64.refs_0_, bf16[320,32]{1,0:T(8,128)(2,1)S(1)} %get-tuple-element.65.refs_1_, bf16[32,8192]{1,0:T(8,128)(2,1)S(1)} %get-tuple-element.66.refs_2_, f32[3,64,128]{2,1,0:T(8,128)S(1)} %get-tuple-element.67.refs_3_), custom_call_target="tpu_custom_call" | custom-call | flops 2000000 | bytes 1048576 | tf_op jit(solution)/shard_map/pallas_call | solution.py:395
  54.9 1.8 %shard_map.139.e2 = bf16[320,2560]{1,0:T(8,128)(2,1)S(1)} custom-call(f32[6,320,128]{2,1,0:T(8,128)S(1)} %get-tuple-element.64.refs_0_, bf16[320,32]{1,0:T(8,128)(2,1)S(1)} %get-tuple-element.65.refs_1_, bf16[32,8192]{1,0:T(8,128)(2,1)S(1)} %get-tuple-element.66.refs_2_, f32[3,64,128]{2,1,0:T(8,128)S(1)} %get-tuple-element.67.refs_3_), custom_call_target="tpu_custom_call" | custom-call | flops 2000000 | bytes 1048576 | tf_op jit(solution)/shard_map/pallas_call | solution.py:395
  56.7 1.5 %shard_map.138.e1 = bf16[320,2048]{1,0:T(8,128)(2,1)S(1)} custom-call(f32[6,320,128]{2,1,0:T(8,128)S(1)} %get-tuple-element.64.refs_0_, bf16[320,32]{1,0:T(8,128)(2,1)S(1)} %get-tuple-element.65.refs_1_, bf16[32,8192]{1,0:T(8,128)(2,1)S(1)} %get-tuple-element.66.refs_2_, f32[3,64,128]{2,1,0:T(8,128)S(1)} %get-tuple-element.67.refs_3_), custom_call_target="tpu_custom_call" | custom-call | flops 2000000 | bytes 1048576 | tf_op jit(solution)/shard_map/pallas_call | solution.py:395
  58.1 1.4 %shard_map.137.e0 = bf16[320,2048]{1,0:T(8,128)(2,1)S(1)} custom-call(f32[6,320,128]{2,1,0:T(8,128)S(1)} %get-tuple-element.64.refs_0_, bf16[320,32]{1,0:T(8,128)(2,1)S(1)} %get-tuple-element.65.refs_1_, bf16[32,8192]{1,0:T(8,128)(2,1)S(1)} %get-tuple-element.66.refs_2_, f32[3,64,128]{2,1,0:T(8,128)S(1)} %get-tuple-element.67.refs_3_), custom_call_target="tpu_custom_call" | custom-call | flops 2000000 | bytes 1048576 | tf_op jit(solution)/shard_map/pallas_call | solution.py:395
  59.6 1.1 %shard_map.141 = (f32[256,128]{1,0:T(8,128)S(1)}, f32[3,8,128]{2,1,0:T(8,128)S(1)}) custom-call(f32[41,128]{1,0:T(8,128)S(1)} %bitcast.30, f32[16,128]{1,0:T(8,128)S(1)} %get-tuple-element.47.v_ref.v1_ref, f32[16,128]{1,0:T(8,128)S(1)} %get-tuple-element.57.v2_ref, s32[8,128]{1,0:T(8,128)S(1)} %pad_bitcast_fusion.node_ref, ...), custom_call_target="tpu_custom_call" | custom-call | flops 2000000 | bytes 1048576 | tf_op jit(solution)/shard_map/pallas_call | solution.py:395
  61.5 26.2 %all_to_all.22 = f32[256,1,128]{2,1,0:T(1,128)S(1)} all-to-all(f32[256,1,128]{2,1,0:T(1,128)S(1)} %bitcast.35), channel_id=1, replica_groups=mesh['row'=8,'col'=32] {'row','col'}, dimensions={0} | all-to-all | bytes 262144 | tf_op jit(solution)/shard_map/all_to_all | solution.py:509
  (44 shorter events, 8.5 us)
Async XLA Ops:
  0.6 24.9 %copy-start = (s32[4,8192]{1,0:T(4,128)S(1)}, s32[4,8192]{1,0:T(4,128)}, u32[]{:S(2)}) copy-start(s32[4,8192]{1,0:T(4,128)} %param.12) | copy-start | bytes 393220
  1.5 0.7 copy-start.1
  3.6 49.2 %all-to-all-start = ((f32[256,1,128]{2,1,0:T(1,128)}), f32[256,1,128]{2,1,0:T(1,128)S(1)}, u32[]{:S(2)}, u32[]{:S(2)}) async-start(f32[256,1,128]{2,1,0:T(1,128)} %bitcast.10), calls=%async_computation | async-start | bytes 262144 | tf_op jit(solution)/shard_map/all_to_all | solution.py:454
  19.3 27.2 %copy-start.3 = (s32[320]{0:T(512)S(1)}, s32[320]{0:T(512)}, u32[]{:S(2)}) copy-start(s32[320]{0:T(512)} %param.19) | copy-start | bytes 3844
  19.3 6.1 %collective-permute-start = (f32[2,128]{1,0:T(2,128)S(1)}, f32[2,128]{1,0:T(2,128)S(1)}, u32[]{:S(2)}, u32[]{:S(2)}) collective-permute-start(f32[2,128]{1,0:T(2,128)S(1)} %get-tuple-element.37), channel_id=1, source_target_pairs={{0,32},{1,33},{2,34},{3,35},{4,36},{5,37},{6,38},{7,39},{8,40},{9,... | collective-permute-start | bytes 3080 | tf_op jit(solution)/shard_map/ppermute | solution.py:435
  21.5 3.9 %collective-permute-start.1 = (f32[2,128]{1,0:T(2,128)S(1)}, f32[2,128]{1,0:T(2,128)S(1)}, u32[]{:S(2)}, u32[]{:S(2)}) collective-permute-start(f32[2,128]{1,0:T(2,128)S(1)} %get-tuple-element.38), channel_id=1, source_target_pairs={{0,1},{1,0},{2,3},{3,2},{4,5},{5,4},{6,7},{7,6},{8,9},{9,8},{10,11... | collective-permute-start | bytes 3080 | tf_op jit(solution)/shard_map/ppermute | solution.py:435
  21.5 3.9 %collective-permute-start.2 = (f32[2,128]{1,0:T(2,128)S(1)}, f32[2,128]{1,0:T(2,128)S(1)}, u32[]{:S(2)}, u32[]{:S(2)}) collective-permute-start(f32[2,128]{1,0:T(2,128)S(1)} %get-tuple-element.39), channel_id=1, source_target_pairs={{0,1},{1,0},{2,3},{3,2},{4,5},{5,4},{6,7},{7,6},{8,9},{9,8},{10,11... | collective-permute-start | bytes 3080 | tf_op jit(solution)/shard_map/ppermute | solution.py:435
  22.5 3.0 %collective-permute-start.3 = (f32[2,128]{1,0:T(2,128)S(1)}, f32[2,128]{1,0:T(2,128)S(1)}, u32[]{:S(2)}, u32[]{:S(2)}) collective-permute-start(f32[2,128]{1,0:T(2,128)S(1)} %get-tuple-element.40), channel_id=1, source_target_pairs={{0,32},{1,2},{2,1},{3,4},{4,3},{5,6},{6,5},{7,8},{8,7},{9,10},{10,... | collective-permute-start | bytes 3080 | tf_op jit(solution)/shard_map/ppermute | solution.py:435
  27.2 2.7 %collective-permute-start.4 = (f32[2,128]{1,0:T(2,128)S(1)}, f32[2,128]{1,0:T(2,128)S(1)}, u32[]{:S(2)}, u32[]{:S(2)}) collective-permute-start(f32[2,128]{1,0:T(2,128)S(1)} %get-tuple-element.42), channel_id=1, source_target_pairs={{0,32},{1,33},{2,34},{3,35},{4,36},{5,37},{6,38},{7,39},{8,40},{9,... | collective-permute-start | bytes 3080 | tf_op jit(solution)/shard_map/ppermute | solution.py:435
  27.7 3.3 %collective-permute-start.5 = (f32[2,128]{1,0:T(2,128)S(1)}, f32[2,128]{1,0:T(2,128)S(1)}, u32[]{:S(2)}, u32[]{:S(2)}) collective-permute-start(f32[2,128]{1,0:T(2,128)S(1)} %get-tuple-element.43), channel_id=1, source_target_pairs={{0,1},{1,0},{2,3},{3,2},{4,5},{5,4},{6,7},{7,6},{8,9},{9,8},{10,11... | collective-permute-start | bytes 3080 | tf_op jit(solution)/shard_map/ppermute | solution.py:435
  27.7 3.3 %collective-permute-start.6 = (f32[2,128]{1,0:T(2,128)S(1)}, f32[2,128]{1,0:T(2,128)S(1)}, u32[]{:S(2)}, u32[]{:S(2)}) collective-permute-start(f32[2,128]{1,0:T(2,128)S(1)} %get-tuple-element.44), channel_id=1, source_target_pairs={{0,1},{1,0},{2,3},{3,2},{4,5},{5,4},{6,7},{7,6},{8,9},{9,8},{10,11... | collective-permute-start | bytes 3080 | tf_op jit(solution)/shard_map/ppermute | solution.py:435
  29.6 1.4 %collective-permute-start.7 = (f32[2,128]{1,0:T(2,128)S(1)}, f32[2,128]{1,0:T(2,128)S(1)}, u32[]{:S(2)}, u32[]{:S(2)}) collective-permute-start(f32[2,128]{1,0:T(2,128)S(1)} %get-tuple-element.45), channel_id=1, source_target_pairs={{0,32},{1,2},{2,1},{3,4},{4,3},{5,6},{6,5},{7,8},{8,7},{9,10},{10,... | collective-permute-start | bytes 3080 | tf_op jit(solution)/shard_map/ppermute | solution.py:435
  31.3 6.1 %collective-permute-start.10 = (f32[2,128]{1,0:T(2,128)S(1)}, f32[2,128]{1,0:T(2,128)S(1)}, u32[]{:S(2)}, u32[]{:S(2)}) collective-permute-start(f32[2,128]{1,0:T(2,128)S(1)} %get-tuple-element.50), channel_id=1, source_target_pairs={{0,1},{1,0},{2,3},{3,2},{4,5},{5,4},{6,7},{7,6},{8,9},{9,8},{10,11... | collective-permute-start | bytes 3080 | tf_op jit(solution)/shard_map/ppermute | solution.py:435
  34.6 2.8 %collective-permute-start.11 = (f32[2,128]{1,0:T(2,128)S(1)}, f32[2,128]{1,0:T(2,128)S(1)}, u32[]{:S(2)}, u32[]{:S(2)}) collective-permute-start(f32[2,128]{1,0:T(2,128)S(1)} %get-tuple-element.51), channel_id=1, source_target_pairs={{0,32},{1,2},{2,1},{3,4},{4,3},{5,6},{6,5},{7,8},{8,7},{9,10},{10,... | collective-permute-start | bytes 3080 | tf_op jit(solution)/shard_map/ppermute | solution.py:435
  35.8 1.6 %collective-permute-start.8 = (f32[2,128]{1,0:T(2,128)S(1)}, f32[2,128]{1,0:T(2,128)S(1)}, u32[]{:S(2)}, u32[]{:S(2)}) collective-permute-start(f32[2,128]{1,0:T(2,128)S(1)} %get-tuple-element.48), channel_id=1, source_target_pairs={{0,32},{1,33},{2,34},{3,35},{4,36},{5,37},{6,38},{7,39},{8,40},{9,... | collective-permute-start | bytes 3080 | tf_op jit(solution)/shard_map/ppermute | solution.py:435
  35.8 3.0 %collective-permute-start.9 = (f32[2,128]{1,0:T(2,128)S(1)}, f32[2,128]{1,0:T(2,128)S(1)}, u32[]{:S(2)}, u32[]{:S(2)}) collective-permute-start(f32[2,128]{1,0:T(2,128)S(1)} %get-tuple-element.49), channel_id=1, source_target_pairs={{0,1},{1,0},{2,3},{3,2},{4,5},{5,4},{6,7},{7,6},{8,9},{9,8},{10,11... | collective-permute-start | bytes 3080 | tf_op jit(solution)/shard_map/ppermute | solution.py:435
  40.5 6.0 %collective-permute-start.12 = (f32[2,128]{1,0:T(2,128)S(1)}, f32[2,128]{1,0:T(2,128)S(1)}, u32[]{:S(2)}, u32[]{:S(2)}) collective-permute-start(f32[2,128]{1,0:T(2,128)S(1)} %get-tuple-element.53), channel_id=1, source_target_pairs={{0,32},{1,33},{2,34},{3,35},{4,36},{5,37},{6,38},{7,39},{8,40},{9,... | collective-permute-start | bytes 3080 | tf_op jit(solution)/shard_map/ppermute | solution.py:435
  44.3 3.3 %collective-permute-start.13 = (f32[2,128]{1,0:T(2,128)S(1)}, f32[2,128]{1,0:T(2,128)S(1)}, u32[]{:S(2)}, u32[]{:S(2)}) collective-permute-start(f32[2,128]{1,0:T(2,128)S(1)} %get-tuple-element.54), channel_id=1, source_target_pairs={{0,1},{1,0},{2,3},{3,2},{4,5},{5,4},{6,7},{7,6},{8,9},{9,8},{10,11... | collective-permute-start | bytes 3080 | tf_op jit(solution)/shard_map/ppermute | solution.py:435
  44.3 3.3 %collective-permute-start.14 = (f32[2,128]{1,0:T(2,128)S(1)}, f32[2,128]{1,0:T(2,128)S(1)}, u32[]{:S(2)}, u32[]{:S(2)}) collective-permute-start(f32[2,128]{1,0:T(2,128)S(1)} %get-tuple-element.55), channel_id=1, source_target_pairs={{0,1},{1,0},{2,3},{3,2},{4,5},{5,4},{6,7},{7,6},{8,9},{9,8},{10,11... | collective-permute-start | bytes 3080 | tf_op jit(solution)/shard_map/ppermute | solution.py:435
  45.9 1.7 %collective-permute-start.15 = (f32[2,128]{1,0:T(2,128)S(1)}, f32[2,128]{1,0:T(2,128)S(1)}, u32[]{:S(2)}, u32[]{:S(2)}) collective-permute-start(f32[2,128]{1,0:T(2,128)S(1)} %get-tuple-element.56), channel_id=1, source_target_pairs={{0,32},{1,2},{2,1},{3,4},{4,3},{5,6},{6,5},{7,8},{8,7},{9,10},{10,... | collective-permute-start | bytes 3080 | tf_op jit(solution)/shard_map/ppermute | solution.py:435
  47.9 12.8 %collective-permute-start.16 = (f32[2,128]{1,0:T(2,128)S(1)}, f32[2,128]{1,0:T(2,128)S(1)}, u32[]{:S(2)}, u32[]{:S(2)}) collective-permute-start(f32[2,128]{1,0:T(2,128)S(1)} %get-tuple-element.58), channel_id=1, source_target_pairs={{0,32},{1,33},{2,34},{3,35},{4,36},{5,37},{6,38},{7,39},{8,40},{9,... | collective-permute-start | bytes 3080 | tf_op jit(solution)/shard_map/ppermute | solution.py:435
  49.0 11.7 %collective-permute-start.17 = (f32[2,128]{1,0:T(2,128)S(1)}, f32[2,128]{1,0:T(2,128)S(1)}, u32[]{:S(2)}, u32[]{:S(2)}) collective-permute-start(f32[2,128]{1,0:T(2,128)S(1)} %get-tuple-element.59), channel_id=1, source_target_pairs={{0,1},{1,0},{2,3},{3,2},{4,5},{5,4},{6,7},{7,6},{8,9},{9,8},{10,11... | collective-permute-start | bytes 3080 | tf_op jit(solution)/shard_map/ppermute | solution.py:435
  50.3 10.4 %collective-permute-start.18 = (f32[2,128]{1,0:T(2,128)S(1)}, f32[2,128]{1,0:T(2,128)S(1)}, u32[]{:S(2)}, u32[]{:S(2)}) collective-permute-start(f32[2,128]{1,0:T(2,128)S(1)} %get-tuple-element.60), channel_id=1, source_target_pairs={{0,1},{1,0},{2,3},{3,2},{4,5},{5,4},{6,7},{7,6},{8,9},{9,8},{10,11... | collective-permute-start | bytes 3080 | tf_op jit(solution)/shard_map/ppermute | solution.py:435
  52.8 7.9 %collective-permute-start.19 = (f32[2,128]{1,0:T(2,128)S(1)}, f32[2,128]{1,0:T(2,128)S(1)}, u32[]{:S(2)}, u32[]{:S(2)}) collective-permute-start(f32[2,128]{1,0:T(2,128)S(1)} %get-tuple-element.61), channel_id=1, source_target_pairs={{0,32},{1,2},{2,1},{3,4},{4,3},{5,6},{6,5},{7,8},{8,7},{9,10},{10,... | collective-permute-start | bytes 3080 | tf_op jit(solution)/shard_map/ppermute | solution.py:435
  (1 other events, 0.7 us)
